TPU v7x, 512 devices: a whole 4x4x16 slice. The times are simulated.
512 devices in a mesh: gx: 16 (over z), gy: 8 (over x, core), gz: 4 (over y).
Axes of the slice: x: 4, y: 4, z: 16, core: 2. Of those that a mesh axis runs over, the one named last changes fastest.
Arguments:
- populations: float32 [19, 32, 64, 512], P(None, ('gy', 'gz'), 'gx'), may hold values from 0.5 to 1.5
- viscosity: float32 [32, 64, 512], P(('gy', 'gz'), 'gx'), may hold values from 0.01 to 0.3
- links: int32 [32, 64, 512], P(('gy', 'gz'), 'gx'), may hold values from 0 to 262143, as said below
- flags: int32 [32, 64, 512], P(('gy', 'gz'), 'gx'), may hold values from 0 to 2, as said below
- neighbours: int32 [32, 64, 18], P(('gy', 'gz'), 'gx'), may hold values from -1 to 63, as said below
- owners: int32 [32, 64], P(('gy', 'gz')), may hold values from 0 to 15, as said below
- slots: int32 [32, 64], P(('gy', 'gz')), may hold values from 0 to 15, as said below
- concentrations: float32 [4, 128, 64, 512], P(None, 'gx', 'gy', 'gz'), may hold values from 0.2 to 2
- diffusivity: float32 [128, 64, 512], P('gx', 'gy', 'gz'), may hold values from 0.04 to 0.12
- uptake_rate: float32 [128, 64, 512], P('gx', 'gy', 'gz'), may hold values from 0.02 to 0.2
Outputs:
- weighted_populations: float32 [19, 32, 64, 512], P(None, ('gy', 'gz'), 'gx')
- tissue_conc: float32 [4, 128, 64, 512], P(None, 'gx', 'gy', 'gz')
Inputs may be any that keep to these rules, and one draw needn't show every extreme that they name: `links`: bit i - 1 is set when the link of population i into the site is open. `flags`: 0 interior site, 1 inlet site, 2 outlet site. `neighbours`: -1 where no block lies beside; the relation is mutual: if block b has N in direction k, N has b in the opposite direction; a block beside lies in the list of the same index of gx or of the one next to it. `owners`: no two of the 4 blocks on one index of gx have the same owner, and in every segment some owner receives exactly 1 from every index of gx. `slots`: distinct among the blocks of one segment with one owner.
All inputs are finite; a program needn't handle non-finite values.
Results may differ from a plain program's by a relative error of at most 0.0003.
Values sent between devices are 32-bit elements; how exact they have to be, the bound alone decides.
No kernel may reach another device: no remote copies, remote signals or barrier semaphores. Data moves between devices by JAX's collectives and lax.ppermute only.
A program may use at most 128 MiB of HBM per device.

v0:
```python
import jax
import jax.numpy as jnp
import numpy as np
from jax import lax
from jax.sharding import PartitionSpec as P

FLOW_STEPS = 4
TISSUE_STEPS = 3


LATTICE_DIRS = (
    (0, 0, 0),
    (1, 0, 0),
    (-1, 0, 0),
    (0, 1, 0),
    (0, -1, 0),
    (0, 0, 1),
    (0, 0, -1),
    (1, 1, 0),
    (-1, -1, 0),
    (1, -1, 0),
    (-1, 1, 0),
    (1, 0, 1),
    (-1, 0, -1),
    (1, 0, -1),
    (-1, 0, 1),
    (0, 1, 1),
    (0, -1, -1),
    (0, 1, -1),
    (0, -1, 1),
)
DIFFUSION_GAIN = (1.0, 0.6, 0.7, 0.35)
HALF_SATURATION = (0.3, 0.5, 0.8, 0.2)
ADVECT_GAIN = 3.0
INLET_DENSITY = 1.03
OUTLET_DENSITY = 0.97


def padded(cells, sides, width):
    for axis, dim in sides:
        count = lax.axis_size(axis)
        ends = count - 1
        head = lax.slice_in_dim(cells, 0, width, axis=dim)
        tail = lax.slice_in_dim(cells, cells.shape[dim] - width, cells.shape[dim], axis=dim)
        cells = jnp.concatenate(
            [
                lax.ppermute(tail, axis, [(i, (i + 1) % count) for i in range(ends)]),
                cells,
                lax.ppermute(head, axis, [((i + 1) % count, i) for i in range(ends)]),
            ],
            axis=dim,
        )
    return cells


def lattice_tables():
    vectors = np.array(LATTICE_DIRS, dtype=np.int64)
    weights = np.array([1.0 / 3.0] + [1.0 / 18.0] * 6 + [1.0 / 36.0] * 12)
    opposite = [
        LATTICE_DIRS.index(tuple((-part_val for part_val in LATTICE_DIRS[member])))
        for member in range(19)
    ]
    sites = np.arange(512)
    coords = np.stack([sites // 64, sites // 8 % 8, sites % 8], axis=1)
    stride = np.array([64, 8, 1])
    shell_sites = sites[((coords == 0) | (coords == 7)).any(axis=1)]
    position = {}
    rim_source = []
    for member in range(1, 19):
        for site_id in shell_sites:
            position[member, int(site_id)] = len(rim_source)
            rim_source.append(member * 512 + int(site_id))
    rim_width = -(-len(rim_source) // 128) * 128
    request_dir = []
    request_pos = []
    offsets = [0]
    counts = [0]
    selects = [sites.copy()]
    dir_maps = [np.zeros(512, np.int64)]
    arriving_masks = [np.zeros(512, bool)]
    shifts = [0]
    for member in range(1, 19):
        source = coords - vectors[member]
        arriving = ((source < 0) | (source > 7)).any(axis=1)
        select = sites.copy()
        dir_map = np.zeros(512, np.int64)
        offsets.append(len(request_dir))
        counts.append(int(arriving.sum()))
        for rank_pos, site_id in enumerate(sites[arriving]):
            block_dir = tuple((int(part_val) for part_val in source[site_id] // 8))
            dir_index = LATTICE_DIRS.index(block_dir) - 1
            local_site = int((source[site_id] % 8 * stride).sum())
            request_dir.append(dir_index)
            request_pos.append(position[member, local_site])
            select[site_id] = 512 + rank_pos
            dir_map[site_id] = dir_index
        selects.append(select)
        dir_maps.append(dir_map)
        arriving_masks.append(arriving)
        shifts.append(int((vectors[member] * stride).sum()))
    request_width = -(-len(request_dir) // 128) * 128
    request_dir = request_dir + [0] * (request_width - len(request_dir))
    request_pos = request_pos + [0] * (request_width - len(request_pos))
    return {
        "vectors": vectors,
        "weights": weights,
        "opposite": opposite,
        "rim_source": np.array(rim_source),
        "rim_width": rim_width,
        "request_dir": np.array(request_dir),
        "request_pos": np.array(request_pos),
        "offsets": offsets,
        "counts": counts,
        "selects": selects,
        "dir_maps": dir_maps,
        "arriving": arriving_masks,
        "shifts": shifts,
    }


def equilibrium(density, momentum, vectors, weights):
    project = jnp.tensordot(vectors, momentum, axes=1, precision=lax.Precision.HIGHEST)
    square = jnp.sum(momentum * momentum, axis=0)
    return weights[:, None, None] * (
        density + 3.0 * project + 4.5 * project * project - 1.5 * square
    )


def collide(popul, relax, vectors, weights):
    density = jnp.sum(popul, axis=0)
    momentum = jnp.tensordot(vectors.T, popul, axes=1, precision=lax.Precision.HIGHEST)
    return popul - relax * (popul - equilibrium(density, momentum, vectors, weights))


def rim_rows(post, tables):
    block_count = post.shape[1]
    flat = jnp.transpose(post, (1, 0, 2)).reshape(block_count, 19 * 512)
    rim = jnp.take(flat, jnp.asarray(tables["rim_source"], jnp.int32), axis=1)
    return jnp.pad(rim, ((0, 0), (0, tables["rim_width"] - rim.shape[1])))


def stream(post, arrived, link_bits, beside_ids, tables):
    result = [post[0]]
    for member in range(1, 19):
        rolled = jnp.roll(post[member], tables["shifts"][member], axis=-1)
        start_col = tables["offsets"][member]
        pool = jnp.concatenate(
            [rolled, arrived[:, start_col : start_col + tables["counts"][member]]], axis=1
        )
        pulled = jnp.take(pool, jnp.asarray(tables["selects"][member], jnp.int32), axis=1)
        beside = (
            jnp.take(beside_ids, jnp.asarray(tables["dir_maps"][member], jnp.int32), axis=1) >= 0
        )
        link_open = jnp.right_shift(link_bits, member - 1) % 2 == 1
        arriving = jnp.asarray(tables["arriving"][member])[None, :]
        opened = link_open & (beside | jnp.logical_not(arriving))
        result.append(jnp.where(opened, pulled, post[tables["opposite"][member]]))
    return jnp.stack(result)


def boundary(popul, site_flags, vectors, weights):
    momentum = jnp.tensordot(vectors.T, popul, axes=1, precision=lax.Precision.HIGHEST)
    density = jnp.where(site_flags == 1, INLET_DENSITY, OUTLET_DENSITY)
    settled = equilibrium(density, momentum, vectors, weights)
    return jnp.where(site_flags[None] > 0, settled, popul)


def shifted(field, offset):
    extent_x, extent_y, extent_z = field.shape[-3:]
    step_x, step_y, step_z = offset
    return field[
        ...,
        1 + step_x : extent_x - 1 + step_x,
        1 + step_y : extent_y - 1 + step_y,
        1 + step_z : extent_z - 1 + step_z,
    ]


def tissue_step(conc_ext, diff_ext, uptake_here, velocity):
    center = conc_ext[:, 1:-1, 1:-1, 1:-1]
    diff_mid = diff_ext[1:-1, 1:-1, 1:-1]
    spread = jnp.zeros_like(center)
    for offset in ((1, 0, 0), (-1, 0, 0), (0, 1, 0), (0, -1, 0), (0, 0, 1), (0, 0, -1)):
        beside_conc = shifted(conc_ext, offset)
        beside_diff = shifted(diff_ext, offset)
        spread = spread + 0.5 * (diff_mid + beside_diff) * (beside_conc - center)
    drifted = jnp.zeros_like(center)
    for axis_pos in range(3):
        unit_vec = [0, 0, 0]
        unit_vec[axis_pos] = 1
        ahead = shifted(conc_ext, tuple(unit_vec))
        behind = shifted(conc_ext, tuple((-part_val for part_val in unit_vec)))
        speed_axis = ADVECT_GAIN * velocity[axis_pos]
        drifted = (
            drifted
            - jnp.maximum(speed_axis, 0.0) * (center - behind)
            - jnp.minimum(speed_axis, 0.0) * (ahead - center)
        )
    species_gain = jnp.array(DIFFUSION_GAIN, jnp.float32)[:, None, None, None]
    halfsat = jnp.array(HALF_SATURATION, jnp.float32)[:, None, None, None]
    uptake = uptake_here * center / (halfsat + jnp.abs(center))
    reaction = jnp.stack([-uptake[0], -uptake[1], 2.0 * uptake[1], -uptake[3]])
    return center + species_gain * spread + drifted + reaction


def shards(
    populations,
    viscosity,
    links,
    flags,
    neighbours,
    owners,
    slots,
    concentrations,
    diffusivity,
    uptake_rate,
):
    tables = lattice_tables()
    weights = jnp.asarray(tables["weights"], jnp.float32)
    vectors = jnp.asarray(tables["vectors"], jnp.float32)
    popul = populations[:, 0] * weights[:, None, None]
    relax = 1.0 / (3.0 * viscosity[0] + 0.5)
    link_bits = links[0]
    site_flags = flags[0]
    beside_ids = neighbours[0]
    block_count = popul.shape[1]
    request_block = jnp.take(beside_ids, jnp.asarray(tables["request_dir"], jnp.int32), axis=1)
    request_pos = jnp.asarray(tables["request_pos"], jnp.int32)
    first_block = (lax.axis_index("gx") - 1) * block_count
    local_block = request_block - first_block
    valid = (local_block >= 0) & (local_block < 3 * block_count)
    for turn_index in range(FLOW_STEPS):
        post = collide(popul, relax, vectors, weights)
        rim = rim_rows(post, tables)
        extended = padded(rim, (("gx", 0),), block_count)
        flat_index = (
            jnp.clip(local_block, 0, 3 * block_count - 1) * extended.shape[1] + request_pos[None, :]
        )
        arrived = jnp.where(valid, jnp.take(extended.reshape(-1), flat_index), 0.0)
        popul = stream(post, arrived, link_bits, beside_ids, tables)
        popul = boundary(popul, site_flags, vectors, weights)
    weighted = (popul / weights[:, None, None])[:, None]
    momentum = jnp.tensordot(vectors.T, popul, axes=1, precision=lax.Precision.HIGHEST)
    block_rows = jnp.transpose(momentum, (1, 0, 2)).reshape(block_count, 3 * 512)
    extent_x, extent_y, extent_z = concentrations.shape[1:]
    slot_x = extent_x // 8
    slot_y = extent_y // 8
    slot_z = extent_z // 8
    slot_total = slot_x * slot_y * slot_z
    owner_all = owners[0]
    slot_all = slots[0]
    my_index = lax.axis_index("gx")
    slot_ids = jnp.arange(slot_total, dtype=jnp.int32)
    start_blocks = jnp.zeros((slot_total, 3 * 512), jnp.float32)
    piece = jax.tree.map(lambda part: lax.all_gather(part, "gx", axis=0, tiled=True), block_rows)
    row_count = piece.shape[0]
    piece_owner = lax.slice_in_dim(owner_all, 0, row_count, axis=0)
    piece_slot = lax.slice_in_dim(slot_all, 0, row_count, axis=0)
    hit = (piece_owner[None, :] == my_index) & (piece_slot[None, :] == slot_ids[:, None])
    brick_blocks = start_blocks + jnp.dot(
        hit.astype(jnp.float32), piece, precision=lax.Precision.HIGHEST
    )
    velocity = (
        brick_blocks.reshape(slot_x, slot_y, slot_z, 3, 8, 8, 8)
        .transpose(3, 0, 4, 1, 5, 2, 6)
        .reshape(3, extent_x, extent_y, extent_z)
    )
    conc_ext, diff_ext = (
        padded(concentrations, (("gx", 1), ("gy", 2), ("gz", 3)), 1),
        padded(diffusivity[None], (("gx", 1), ("gy", 2), ("gz", 3)), 1),
    )
    diff_ext = diff_ext[0]
    conc = tissue_step(conc_ext, diff_ext, uptake_rate, velocity)
    for turn_index in range(TISSUE_STEPS - 1):
        conc_ext = padded(conc, (("gx", 1), ("gy", 2), ("gz", 3)), 1)
        conc = tissue_step(conc_ext, diff_ext, uptake_rate, velocity)
    return (weighted, conc)


def solution(mesh):
    return jax.shard_map(
        shards,
        mesh=mesh,
        in_specs=(
            P(None, ("gy", "gz"), "gx", None),
            P(("gy", "gz"), "gx", None),
            P(("gy", "gz"), "gx", None),
            P(("gy", "gz"), "gx", None),
            P(("gy", "gz"), "gx", None),
            P(("gy", "gz"), None),
            P(("gy", "gz"), None),
            P(None, "gx", "gy", "gz"),
            P("gx", "gy", "gz"),
            P("gx", "gy", "gz"),
        ),
        out_specs=(P(None, ("gy", "gz"), "gx", None), P(None, "gx", "gy", "gz")),
        check_vma=False,
    )
```

profile of v0, /device:TPU:90, one launch (start us, length us, event | category | flops | bytes accessed | tf_op | source)
XLA Modules:
  0.0 563.2 jit_solution(15572680658996601639)
XLA Ops:
  8.6 11.3 %gather_fusion.2 = f32[5328,4]{1,0:T(8,128)S(1)} fusion(f32[4,9728]{0,1:T(8,128)} %bitcast.1073, s32[6144]{0:T(1024)S(1)} %pad_clamp_fusion.1), kind=kCustom, calls=%fused_computation.1.clone | custom fusion | bytes 191808 | tf_op jit(solution)/shard_map/jit(_take)/gather | solution.py:138
  21.0 3.8 collective-permute-start
  26.9 4.9 collective-permute-start.8
  33.8 5.1 collective-permute-start.15
  39.3 3.5 gather_fusion
  47.8 3.6 collective-permute-start.11
  72.1 4.6 collective-permute-start.13
  81.4 4.4 collective-permute-done.14
  94.5 3.4 collective-permute-start.18
  99.6 39.8 %gather_fusion.3 = f32[7680]{0:T(1024)S(1)} fusion(f32[64512]{0:T(1024)S(1)} %reshape.235, s32[8192]{0:T(1024)S(1)} %pad_clamp_fusion), kind=kCustom, calls=%fused_computation.2.clone | custom fusion | bytes 92160 | tf_op jit(solution)/shard_map/jit(_take)/gather | solution.py:239
  178.9 3.0 copy.795
  181.9 11.2 %gather_fusion.39 = f32[5328,4]{1,0:T(8,128)S(1)} fusion(f32[4,9728]{0,1:T(8,128)} %copy.795, s32[6144]{0:T(1024)S(1)} %pad_clamp_fusion.1), kind=kCustom, calls=%fused_computation.22.clone | custom fusion | bytes 191808 | tf_op jit(solution)/shard_map/jit(_take)/gather | solution.py:138
  194.0 5.1 collective-permute-start.2
  201.5 4.0 collective-permute-done.3
  205.7 39.8 %gather_fusion.40 = f32[7680]{0:T(1024)S(1)} fusion(f32[64512]{0:T(1024)S(1)} %reshape.237, s32[8192]{0:T(1024)S(1)} %pad_clamp_fusion), kind=kCustom, calls=%fused_computation.25.clone | custom fusion | bytes 92160 | tf_op jit(solution)/shard_map/jit(_take)/gather | solution.py:239
  278.1 11.2 %gather_fusion.59 = f32[5328,4]{1,0:T(8,128)S(1)} fusion(f32[4,9728]{0,1:T(8,128)} %copy.843, s32[6144]{0:T(1024)S(1)} %pad_clamp_fusion.1), kind=kCustom, calls=%fused_computation.23.clone | custom fusion | bytes 191808 | tf_op jit(solution)/shard_map/jit(_take)/gather | solution.py:138
  290.1 3.1 collective-permute-start.4
  296.5 3.5 collective-permute-done.5
  300.2 39.8 %gather_fusion.60 = f32[7680]{0:T(1024)S(1)} fusion(f32[64512]{0:T(1024)S(1)} %reshape.239, s32[8192]{0:T(1024)S(1)} %pad_clamp_fusion), kind=kCustom, calls=%fused_computation.26.clone | custom fusion | bytes 92160 | tf_op jit(solution)/shard_map/jit(_take)/gather | solution.py:239
  372.7 11.2 %gather_fusion.79 = f32[5328,4]{1,0:T(8,128)S(1)} fusion(f32[4,9728]{0,1:T(8,128)} %copy.891, s32[6144]{0:T(1024)S(1)} %pad_clamp_fusion.1), kind=kCustom, calls=%fused_computation.24.clone | custom fusion | bytes 191808 | tf_op jit(solution)/shard_map/jit(_take)/gather | solution.py:138
  384.7 5.1 collective-permute-start.6
  392.1 4.2 collective-permute-done.7
  396.4 39.8 %gather_fusion.80 = f32[7680]{0:T(1024)S(1)} fusion(f32[64512]{0:T(1024)S(1)} %reshape.241, s32[8192]{0:T(1024)S(1)} %pad_clamp_fusion), kind=kCustom, calls=%fused_computation.27.clone | custom fusion | bytes 92160 | tf_op jit(solution)/shard_map/jit(_take)/gather | solution.py:239
  466.0 30.3 %all-gather = f32[16,4,1536]{2,1,0:T(4,128)S(1)} all-gather(f32[1,4,1536]{2,1,0:T(4,128)S(1)} %reshape.1045), channel_id=1, replica_groups=mesh['gx'=16,'gy'=8,'gz'=4] {'gx'}, dimensions={0}, use_global_device_ids=true | all-gather | bytes 417792 | tf_op jit(solution)/shard_map/all_gather | solution.py:255
  503.9 3.9 collective-permute-start.21
  517.0 4.6 collective-permute-start.24
  522.9 4.9 collective-permute-done.24
  527.8 4.1 collective-permute-done.25
  532.3 3.9 collective-permute-start.26
  538.3 3.6 collective-permute-done.27
  552.6 5.0 collective-permute-done.30
  557.6 4.1 collective-permute-done.31
  (1156 shorter events, 226.5 us)
Async XLA Ops:
  21.0 78.3 %collective-permute-start = (f32[4,5376]{1,0:T(4,128)S(1)}, f32[4,5376]{1,0:T(4,128)S(1)}, u32[]{:S(2)}, u32[]{:S(2)}) collective-permute-start(f32[4,5376]{1,0:T(4,128)S(1)} %pad.13.clone), channel_id=1, source_target_pairs={{0,32},{32,64},{64,96},{96,128},{128,160},{160,192},{192,224},{224... | collective-permute-start | bytes 258056 | tf_op jit(solution)/shard_map/ppermute | solution.py:47
  24.9 74.5 %collective-permute-start.1 = (f32[4,5376]{1,0:T(4,128)S(1)}, f32[4,5376]{1,0:T(4,128)S(1)}, u32[]{:S(2)}, u32[]{:S(2)}) collective-permute-start(f32[4,5376]{1,0:T(4,128)S(1)} %pad.13.clone), channel_id=1, source_target_pairs={{32,0},{64,32},{96,64},{128,96},{160,128},{192,160},{224,192},{256... | collective-permute-start | bytes 258056 | tf_op jit(solution)/shard_map/ppermute | solution.py:49
  26.9 18.9 %collective-permute-start.8 = (f32[1,1,8,128]{3,2,1,0:T(8,128)S(1)}, f32[1,1,8,128]{3,2,1,0:T(8,128)S(1)}, u32[]{:S(2)}, u32[]{:S(2)}) collective-permute-start(f32[1,1,8,128]{3,2,1,0:T(8,128)S(1)} %get-tuple-element.219), channel_id=1, source_target_pairs={{0,32},{32,64},{64,96},{96,128},{128,160},{160,192},{192,224},{224... | collective-permute-start | bytes 12296 | tf_op jit(solution)/shard_map/ppermute | solution.py:47
  31.9 14.0 %collective-permute-start.9 = (f32[1,1,8,128]{3,2,1,0:T(8,128)S(1)}, f32[1,1,8,128]{3,2,1,0:T(8,128)S(1)}, u32[]{:S(2)}, u32[]{:S(2)}) collective-permute-start(f32[1,1,8,128]{3,2,1,0:T(8,128)S(1)} %get-tuple-element.220), channel_id=1, source_target_pairs={{32,0},{64,32},{96,64},{128,96},{160,128},{192,160},{224,192},{256... | collective-permute-start | bytes 12296 | tf_op jit(solution)/shard_map/ppermute | solution.py:49
  33.8 47.4 %collective-permute-start.15 = (f32[4,1,8,128]{3,2,1,0:T(8,128)S(1)}, f32[4,1,8,128]{3,2,1,0:T(8,128)S(1)}, u32[]{:S(2)}, u32[]{:S(2)}) collective-permute-start(f32[4,1,8,128]{3,2,1,0:T(8,128)S(1)} %get-tuple-element.208), channel_id=1, source_target_pairs={{0,32},{32,64},{64,96},{96,128},{128,160},{160,192},{192,224},{224... | collective-permute-start | bytes 49160 | tf_op jit(solution)/shard_map/ppermute | solution.py:47
  45.9 24.8 %collective-permute-start.10 = (f32[1,10,1,128]{3,2,1,0:T(1,128)S(1)}, f32[1,10,1,128]{3,2,1,0:T(1,128)S(1)}, u32[]{:S(2)}, u32[]{:S(2)}) collective-permute-start(f32[1,10,1,128]{3,2,1,0:T(1,128)S(1)} %get-tuple-element.217), channel_id=1, source_target_pairs={{0,4},{4,8},{8,12},{12,16},{16,20},{20,24},{24,28},{1,5},{5,9},{9,... | collective-permute-start | bytes 15368 | tf_op jit(solution)/shard_map/ppermute | solution.py:47
  47.8 22.9 %collective-permute-start.11 = (f32[1,10,1,128]{3,2,1,0:T(1,128)S(1)}, f32[1,10,1,128]{3,2,1,0:T(1,128)S(1)}, u32[]{:S(2)}, u32[]{:S(2)}) collective-permute-start(f32[1,10,1,128]{3,2,1,0:T(1,128)S(1)} %get-tuple-element.218), channel_id=1, source_target_pairs={{4,0},{8,4},{12,8},{16,12},{20,16},{24,20},{28,24},{5,1},{9,5},{13... | collective-permute-start | bytes 15368 | tf_op jit(solution)/shard_map/ppermute | solution.py:49
  70.8 8.2 %collective-permute-start.12 = (f32[1,10,10,1]{3,2,1,0:T(8,128)S(1)}, f32[1,10,10,1]{3,2,1,0:T(8,128)S(1)}, u32[]{:S(2)}, u32[]{:S(2)}) collective-permute-start(f32[1,10,10,1]{3,2,1,0:T(8,128)S(1)} %get-tuple-element.215), channel_id=1, source_target_pairs={{0,1},{1,2},{2,3},{4,5},{5,6},{6,7},{8,9},{9,10},{10,11},{12,13},{... | collective-permute-start | bytes 1208 | tf_op jit(solution)/shard_map/ppermute | solution.py:47
  72.1 8.8 %collective-permute-start.13 = (f32[1,10,10,1]{3,2,1,0:T(8,128)S(1)}, f32[1,10,10,1]{3,2,1,0:T(8,128)S(1)}, u32[]{:S(2)}, u32[]{:S(2)}) collective-permute-start(f32[1,10,10,1]{3,2,1,0:T(8,128)S(1)} %get-tuple-element.216), channel_id=1, source_target_pairs={{1,0},{2,1},{3,2},{5,4},{6,5},{7,6},{9,8},{10,9},{11,10},{13,12},{... | collective-permute-start | bytes 1208 | tf_op jit(solution)/shard_map/ppermute | solution.py:49
  79.0 6.8 %collective-permute-start.14 = (f32[4,1,8,128]{3,2,1,0:T(8,128)S(1)}, f32[4,1,8,128]{3,2,1,0:T(8,128)S(1)}, u32[]{:S(2)}, u32[]{:S(2)}) collective-permute-start(f32[4,1,8,128]{3,2,1,0:T(8,128)S(1)} %get-tuple-element.207), channel_id=1, source_target_pairs={{32,0},{64,32},{96,64},{128,96},{160,128},{192,160},{224,192},{256... | collective-permute-start | bytes 49160 | tf_op jit(solution)/shard_map/ppermute | solution.py:49
  86.5 5.0 collective-permute-start.16
  88.4 5.1 collective-permute-start.17
  94.5 406.0 %collective-permute-start.18 = (f32[4,10,10,1]{3,2,1,0:T(8,128)}, f32[4,10,10,1]{3,2,1,0:T(8,128)}, u32[]{:S(2)}, u32[]{:S(2)}) collective-permute-start(f32[4,10,10,1]{3,2,1,0:T(8,128)} %get-tuple-element.76), channel_id=1, source_target_pairs={{1,0},{2,1},{3,2},{5,4},{6,5},{7,6},{9,8},{10,9},{11,10},{13,12},{... | collective-permute-start | bytes 4808 | tf_op jit(solution)/shard_map/ppermute | solution.py:49
  97.8 402.6 %collective-permute-start.19 = (f32[4,10,10,1]{3,2,1,0:T(8,128)}, f32[4,10,10,1]{3,2,1,0:T(8,128)}, u32[]{:S(2)}, u32[]{:S(2)}) collective-permute-start(f32[4,10,10,1]{3,2,1,0:T(8,128)} %get-tuple-element.77), channel_id=1, source_target_pairs={{0,1},{1,2},{2,3},{4,5},{5,6},{6,7},{8,9},{9,10},{10,11},{12,13},{... | collective-permute-start | bytes 4808 | tf_op jit(solution)/shard_map/ppermute | solution.py:47
  194.0 7.6 %collective-permute-start.2 = (f32[4,5376]{1,0:T(4,128)S(1)}, f32[4,5376]{1,0:T(4,128)S(1)}, u32[]{:S(2)}, u32[]{:S(2)}) collective-permute-start(f32[4,5376]{1,0:T(4,128)S(1)} %pad.14.clone), channel_id=1, source_target_pairs={{0,32},{32,64},{64,96},{96,128},{128,160},{160,192},{192,224},{224... | collective-permute-start | bytes 258056 | tf_op jit(solution)/shard_map/ppermute | solution.py:47
  199.1 6.4 %collective-permute-start.3 = (f32[4,5376]{1,0:T(4,128)S(1)}, f32[4,5376]{1,0:T(4,128)S(1)}, u32[]{:S(2)}, u32[]{:S(2)}) collective-permute-start(f32[4,5376]{1,0:T(4,128)S(1)} %pad.14.clone), channel_id=1, source_target_pairs={{32,0},{64,32},{96,64},{128,96},{160,128},{192,160},{224,192},{256... | collective-permute-start | bytes 258056 | tf_op jit(solution)/shard_map/ppermute | solution.py:49
  290.1 6.4 %collective-permute-start.4 = (f32[4,5376]{1,0:T(4,128)S(1)}, f32[4,5376]{1,0:T(4,128)S(1)}, u32[]{:S(2)}, u32[]{:S(2)}) collective-permute-start(f32[4,5376]{1,0:T(4,128)S(1)} %pad.15.clone), channel_id=1, source_target_pairs={{0,32},{32,64},{64,96},{96,128},{128,160},{160,192},{192,224},{224... | collective-permute-start | bytes 258056 | tf_op jit(solution)/shard_map/ppermute | solution.py:47
  293.3 6.8 %collective-permute-start.5 = (f32[4,5376]{1,0:T(4,128)S(1)}, f32[4,5376]{1,0:T(4,128)S(1)}, u32[]{:S(2)}, u32[]{:S(2)}) collective-permute-start(f32[4,5376]{1,0:T(4,128)S(1)} %pad.15.clone), channel_id=1, source_target_pairs={{32,0},{64,32},{96,64},{128,96},{160,128},{192,160},{224,192},{256... | collective-permute-start | bytes 258056 | tf_op jit(solution)/shard_map/ppermute | solution.py:49
  384.7 7.4 %collective-permute-start.6 = (f32[4,5376]{1,0:T(4,128)S(1)}, f32[4,5376]{1,0:T(4,128)S(1)}, u32[]{:S(2)}, u32[]{:S(2)}) collective-permute-start(f32[4,5376]{1,0:T(4,128)S(1)} %pad.16.clone), channel_id=1, source_target_pairs={{0,32},{32,64},{64,96},{96,128},{128,160},{160,192},{192,224},{224... | collective-permute-start | bytes 258056 | tf_op jit(solution)/shard_map/ppermute | solution.py:47
  389.8 6.4 %collective-permute-start.7 = (f32[4,5376]{1,0:T(4,128)S(1)}, f32[4,5376]{1,0:T(4,128)S(1)}, u32[]{:S(2)}, u32[]{:S(2)}) collective-permute-start(f32[4,5376]{1,0:T(4,128)S(1)} %pad.16.clone), channel_id=1, source_target_pairs={{32,0},{64,32},{96,64},{128,96},{160,128},{192,160},{224,192},{256... | collective-permute-start | bytes 258056 | tf_op jit(solution)/shard_map/ppermute | solution.py:49
  502.0 5.9 %collective-permute-start.20 = (f32[4,1,8,128]{3,2,1,0:T(8,128)S(1)}, f32[4,1,8,128]{3,2,1,0:T(8,128)S(1)}, u32[]{:S(2)}, u32[]{:S(2)}) collective-permute-start(f32[4,1,8,128]{3,2,1,0:T(8,128)S(1)} %get-tuple-element.202), channel_id=1, source_target_pairs={{32,0},{64,32},{96,64},{128,96},{160,128},{192,160},{224,192},{256... | collective-permute-start | bytes 49160 | tf_op jit(solution)/shard_map/ppermute | solution.py:49
  503.9 5.8 %collective-permute-start.21 = (f32[4,1,8,128]{3,2,1,0:T(8,128)S(1)}, f32[4,1,8,128]{3,2,1,0:T(8,128)S(1)}, u32[]{:S(2)}, u32[]{:S(2)}) collective-permute-start(f32[4,1,8,128]{3,2,1,0:T(8,128)S(1)} %get-tuple-element.201), channel_id=1, source_target_pairs={{0,32},{32,64},{64,96},{96,128},{128,160},{160,192},{192,224},{224... | collective-permute-start | bytes 49160 | tf_op jit(solution)/shard_map/ppermute | solution.py:47
  509.7 4.3 collective-permute-start.22
  511.7 5.1 collective-permute-start.23
  517.0 10.8 %collective-permute-start.24 = (f32[4,10,10,1]{3,2,1,0:T(8,128)S(1)}, f32[4,10,10,1]{3,2,1,0:T(8,128)S(1)}, u32[]{:S(2)}, u32[]{:S(2)}) collective-permute-start(f32[4,10,10,1]{3,2,1,0:T(8,128)S(1)} %get-tuple-element.74), channel_id=1, source_target_pairs={{1,0},{2,1},{3,2},{5,4},{6,5},{7,6},{9,8},{10,9},{11,10},{13,12},{... | collective-permute-start | bytes 4808 | tf_op jit(solution)/shard_map/ppermute | solution.py:49
  521.6 10.4 %collective-permute-start.25 = (f32[4,10,10,1]{3,2,1,0:T(8,128)S(1)}, f32[4,10,10,1]{3,2,1,0:T(8,128)S(1)}, u32[]{:S(2)}, u32[]{:S(2)}) collective-permute-start(f32[4,10,10,1]{3,2,1,0:T(8,128)S(1)} %get-tuple-element.75), channel_id=1, source_target_pairs={{0,1},{1,2},{2,3},{4,5},{5,6},{6,7},{8,9},{9,10},{10,11},{12,13},{... | collective-permute-start | bytes 4808 | tf_op jit(solution)/shard_map/ppermute | solution.py:47
  532.3 5.9 %collective-permute-start.26 = (f32[4,1,8,128]{3,2,1,0:T(8,128)S(1)}, f32[4,1,8,128]{3,2,1,0:T(8,128)S(1)}, u32[]{:S(2)}, u32[]{:S(2)}) collective-permute-start(f32[4,1,8,128]{3,2,1,0:T(8,128)S(1)} %get-tuple-element.200), channel_id=1, source_target_pairs={{32,0},{64,32},{96,64},{128,96},{160,128},{192,160},{224,192},{256... | collective-permute-start | bytes 49160 | tf_op jit(solution)/shard_map/ppermute | solution.py:49
  536.2 5.6 %collective-permute-start.27 = (f32[4,1,8,128]{3,2,1,0:T(8,128)S(1)}, f32[4,1,8,128]{3,2,1,0:T(8,128)S(1)}, u32[]{:S(2)}, u32[]{:S(2)}) collective-permute-start(f32[4,1,8,128]{3,2,1,0:T(8,128)S(1)} %get-tuple-element.199), channel_id=1, source_target_pairs={{0,32},{32,64},{64,96},{96,128},{128,160},{160,192},{192,224},{224... | collective-permute-start | bytes 49160 | tf_op jit(solution)/shard_map/ppermute | solution.py:47
  541.8 4.3 collective-permute-start.28
  543.8 5.1 collective-permute-start.29
  549.1 8.5 %collective-permute-start.30 = (f32[4,10,10,1]{3,2,1,0:T(8,128)S(1)}, f32[4,10,10,1]{3,2,1,0:T(8,128)S(1)}, u32[]{:S(2)}, u32[]{:S(2)}) collective-permute-start(f32[4,10,10,1]{3,2,1,0:T(8,128)S(1)} %get-tuple-element.72), channel_id=1, source_target_pairs={{1,0},{2,1},{3,2},{5,4},{6,5},{7,6},{9,8},{10,9},{11,10},{13,12},{... | collective-permute-start | bytes 4808 | tf_op jit(solution)/shard_map/ppermute | solution.py:49
  551.3 10.5 %collective-permute-start.31 = (f32[4,10,10,1]{3,2,1,0:T(8,128)S(1)}, f32[4,10,10,1]{3,2,1,0:T(8,128)S(1)}, u32[]{:S(2)}, u32[]{:S(2)}) collective-permute-start(f32[4,10,10,1]{3,2,1,0:T(8,128)S(1)} %get-tuple-element.73), channel_id=1, source_target_pairs={{0,1},{1,2},{2,3},{4,5},{5,6},{6,7},{8,9},{9,10},{10,11},{12,13},{... | collective-permute-start | bytes 4808 | tf_op jit(solution)/shard_map/ppermute | solution.py:47
  (228 other events, 6300.8 us)
where the time goes:
time: 572 us; the launch traced here: 563 us
  local copies, waits for them, and re-layouts  351 us (61%)
  starting transfers between devices  90.9 us (16%)
  waiting for transfers between devices  47.4 us (8%)
  blocking collectives  30.3 us (5%)
  other arithmetic  28.9 us (5%)
  matrix products  7.81 us (1%)
  between operations  6.93 us (1%)
    gather x8, local copies, waits for them, and re-layouts, shards(): arrived = jnp.where(valid, jnp.take(extended.reshape(-1), flat_index), 0.0)  159 us
    gather x144, local copies, waits for them, and re-layouts, stream(): jnp.take(pool, jnp.asarray(tables['selects'][member], jnp.int32), axis=1)  82.4 us
    ppermute x16, starting transfers between devices, padded(): lax.ppermute(tail, axis, [(i, (i + 1) % count) for i in range(ends)])  47.8 us
    gather x4, local copies, waits for them, and re-layouts, rim_rows(): rim = jnp.take(flat, jnp.asarray(tables['rim_source'], jnp.int32), axis=1)  44.8 us
    ppermute x16, starting transfers between devices, padded(): lax.ppermute(head, axis, [((i + 1) % count, i) for i in range(ends)])  43.1 us
    all_gather x1, blocking collectives, shards(): lax.all_gather(part, 'gx', axis=0, tiled=True)  30.3 us
    ppermute x16, waiting for transfers between devices, padded(): lax.ppermute(head, axis, [((i + 1) % count, i) for i in range(ends)])  26 us
    ppermute x16, waiting for transfers between devices, padded(): lax.ppermute(tail, axis, [(i, (i + 1) % count) for i in range(ends)])  21.3 us
  transfers between devices with their start and end apart: 32, of which 14 were waited for; matrix products, arithmetic and copies ran while one was open for 64% of the time, Pallas kernels for 0%

commit v1 on v0

v1 whole, which is shorter than its diff:
```python
import jax
import jax.numpy as jnp
import numpy as np
from jax import lax
from jax.experimental import pallas as pl
from jax.experimental.pallas import tpu as pltpu
from jax.sharding import PartitionSpec as P

FLOW_STEPS = 4
DIRS = (
    (0, 0, 0),
    (1, 0, 0), (-1, 0, 0), (0, 1, 0), (0, -1, 0), (0, 0, 1), (0, 0, -1),
    (1, 1, 0), (-1, -1, 0), (1, -1, 0), (-1, 1, 0),
    (1, 0, 1), (-1, 0, -1), (1, 0, -1), (-1, 0, 1),
    (0, 1, 1), (0, -1, -1), (0, 1, -1), (0, -1, 1),
)
WEIGHT = (1.0 / 3.0,) + (1.0 / 18.0,) * 6 + (1.0 / 36.0,) * 12
OPP = tuple(DIRS.index(tuple(-v for v in c)) for c in DIRS)
GAIN = (1.0, 0.6, 0.7, 0.35)
HALF = (0.3, 0.5, 0.8, 0.2)
STRIDE = (64, 8, 1)
SITE = np.arange(512)
COORD = np.stack([SITE // 64, SITE // 8 % 8, SITE % 8], axis=1)
UNITS = tuple((a, s) for a in range(3) for s in (1, -1))
UNIT_POPS = tuple(tuple(i for i in range(1, 19) if DIRS[i][a] == s) for a, s in UNITS)
UNIT_SLOT = tuple(
    ((7, 5, 3, 1, 6) if a == 0 else (7, 6, 5, 4, 3))
    if s == 1
    else ((0, 2, 4, 6, 1) if a == 0 else (0, 1, 2, 3, 4))
    for a, s in UNITS
)
F32 = jnp.float32
GRID = (2, 8, 128)


def unit_of(a, s):
    return 2 * a + (0 if s == 1 else 1)


def dir_index(vec):
    return DIRS.index(tuple(vec)) - 1


def edge_unit(i):
    axes = [a for a in range(3) if DIRS[i][a]]
    return axes[1], axes[0]


class Sites:
    def __init__(self):
        sub = lax.broadcasted_iota(jnp.int32, GRID, 1)
        self.lane = lax.broadcasted_iota(jnp.int32, GRID, 2)
        self.sub = sub
        self.coord = (
            (sub & 3) * 2 + (self.lane >> 6),
            (self.lane >> 3) & 7,
            self.lane & 7,
        )
        self.cache = {}

    def plane(self, a, value):
        key = (a, value)
        if key not in self.cache:
            self.cache[key] = self.coord[a] == value
        return self.cache[key]

    def roll(self, v, n, dest):
        low = n % 128
        rows = (n - low) // 128
        lanes = SITE[dest] % 128

        def shift(x, k):
            return pltpu.roll(x, k % 8, 1) if k % 8 else x

        r = pltpu.roll(v, low, 2) if low else v
        same, carried = (lanes >= low).any(), (lanes < low).any()
        if same and carried:
            return jnp.where(self.lane >= low, shift(r, rows), shift(r, rows + 1))
        return shift(r, rows if same else rows + 1)


def moments(f):
    j = []
    for a in range(3):
        t = None
        for i in range(1, 19):
            if DIRS[i][a] == 0:
                continue
            if t is None:
                t = f[i] if DIRS[i][a] == 1 else -f[i]
            else:
                t = t + f[i] if DIRS[i][a] == 1 else t - f[i]
        j.append(t)
    return j


def equilibrium(r, j):
    base = r - 1.5 * (j[0] * j[0] + j[1] * j[1] + j[2] * j[2])
    out = [base * WEIGHT[0]] + [None] * 18
    for i in range(1, 19, 2):
        c = DIRS[i]
        p = None
        for a in range(3):
            if c[a]:
                t = j[a] if c[a] == 1 else -j[a]
                p = t if p is None else p + t
        even = base + 4.5 * (p * p)
        odd = 3.0 * p
        out[i] = WEIGHT[i] * (even + odd)
        out[i + 1] = WEIGHT[i] * (even - odd)
    return out


CODE = 38


def collide_pack(sites, f, relax, post_ref, unit_ref, base=0):
    r = f[0]
    for i in range(1, 19):
        r = r + f[i]
    feq = equilibrium(r, moments(f))
    post = [f[i] - relax * (f[i] - feq[i]) for i in range(19)]
    for i in range(19):
        post_ref[2 * i : 2 * i + 2] = post[i]
    for u, (a, s) in enumerate(UNITS):
        src = 7 if s == 1 else 0
        acc = post[UNIT_POPS[u][0]]
        for i, slot in list(zip(UNIT_POPS[u], UNIT_SLOT[u]))[1:]:
            moved = sites.roll(post[i], (slot - src) * STRIDE[a], COORD[:, a] == slot)
            acc = jnp.where(sites.plane(a, slot), moved, acc)
        unit_ref[base + 2 * u : base + 2 * u + 2] = acc


def stream(sites, me, nbr_ref, post_ref, unit_ref, left_ref, right_ref, code_ref, pool, got, base=0):
    for u in range(6):
        pool[u, 0:16] = left_ref[2 * u : 2 * u + 2].reshape(16, 128)
        pool[u, 16:32] = unit_ref[base + 2 * u : base + 2 * u + 2].reshape(16, 128)
        pool[u, 32:48] = right_ref[2 * u : 2 * u + 2].reshape(16, 128)
    first = (me - 1) * 4
    for k in range(18):
        d = DIRS[k + 1]
        i = OPP[k + 1]
        axes = [a for a in range(3) if d[a]]
        a = axes[0] if len(axes) == 1 else edge_unit(i)[0]
        u = unit_of(a, -d[a])
        for b in range(4):
            n = jnp.clip(nbr_ref[0, b, k] - first, 0, 11)
            got[k, 4 * b : 4 * b + 4] = pool[u, pl.ds(pl.multiple_of(4 * n, 4), 4), :]
    eff = code_ref[CODE + 2 : CODE + 4].astype(jnp.int32)
    f = [post_ref[0:2]]
    for i in range(1, 19):
        c = DIRS[i]
        axes = [a for a in range(3) if c[a]]
        dest = {a: (0 if c[a] == 1 else 7) for a in axes}
        at = {a: COORD[:, a] == dest[a] for a in axes}
        shift = sum(c[a] * STRIDE[a] for a in range(3))
        pulled = sites.roll(post_ref[2 * i : 2 * i + 2], shift, ~np.any([at[a] for a in axes], axis=0))
        for a in axes:
            u = unit_of(a, c[a])
            slot = UNIT_SLOT[u][UNIT_POPS[u].index(i)]
            face = [0, 0, 0]
            face[a] = -c[a]
            n = (dest[a] - slot) * STRIDE[a] + shift - c[a] * STRIDE[a]
            where = at[a].copy()
            for o in axes:
                if o != a:
                    where &= ~at[o]
            v = sites.roll(got[dir_index(face)].reshape(GRID), n, where)
            pulled = jnp.where(sites.plane(a, dest[a]), v, pulled)
        if len(axes) == 2:
            a, o = edge_unit(i)
            u = unit_of(a, c[a])
            slot = UNIT_SLOT[u][UNIT_POPS[u].index(i)]
            n = (dest[a] - slot) * STRIDE[a] + (dest[o] - (7 - dest[o])) * STRIDE[o]
            v = sites.roll(got[dir_index([-t for t in c])].reshape(GRID), n, at[a] & at[o])
            both = sites.plane(a, dest[a]) & sites.plane(o, dest[o])
            pulled = jnp.where(both, v, pulled)
        o = OPP[i]
        f.append(jnp.where((eff & (1 << (i - 1))) != 0, pulled, post_ref[2 * o : 2 * o + 2]))
    flag = eff >> 18
    feq = equilibrium(jnp.where(flag == 1, 1.03, 0.97).astype(F32), moments(f))
    edge = flag > 0
    return [jnp.where(edge, feq[i], f[i]) for i in range(19)]


def to_rows(dst, value, b_rows=4):
    for r in range(4):
        dst[pl.ds(r, 4, stride=4), :] = value[:, 128 * r : 128 * r + 128]


def slab(field, plane):
    return 12 + 3 * field + plane


def first_kernel(nbr_ref, pop_hbm, visc_hbm, link_hbm, flag_hbm, conc_hbm, diff_hbm, upt_hbm,
                 state, lo, hi,
                 rows, irows, pop_ref, visc_ref, link_ref, flag_in, sem):
    pairs = [(pop_hbm, pop_ref), (visc_hbm, visc_ref), (link_hbm, link_ref), (flag_hbm, flag_in)]
    for out, base in ((lo, 0), (hi, 5)):
        fields = [conc_hbm.at[s] for s in range(4)] + [diff_hbm, upt_hbm]
        for n, field in enumerate(fields):
            pairs.append((field.at[base : base + 3], out.at[slab(n, 0) : slab(n, 3)]))
    copies = [pltpu.make_async_copy(src, dst, sem.at[n]) for n, (src, dst) in enumerate(pairs)]
    for copy in copies:
        copy.start()
    for copy in copies:
        copy.wait()
    sites = Sites()
    f = []
    for i in range(19):
        to_rows(rows.at[i], pop_ref[i, 0])
    to_rows(rows.at[19], visc_ref[0])
    to_rows(irows.at[0], link_ref[0])
    to_rows(irows.at[1], flag_in[0])
    f = [rows[i].reshape(GRID) * np.float32(WEIGHT[i]) for i in range(19)]
    relax = 1.0 / (3.0 * rows[19].reshape(GRID) + 0.5)
    state[38:40] = relax
    group = lax.broadcasted_iota(jnp.int32, GRID, 0) * 2 + (sites.sub >> 2)
    closed = jnp.zeros(GRID, jnp.int32)
    zero = jnp.zeros(GRID, jnp.int32)
    for k in range(18):
        d = DIRS[k + 1]
        axes = [a for a in range(3) if d[a]]
        if len(axes) == 1:
            a = axes[0]
            s = -d[a]
            bits = jnp.full(GRID, 1 << (OPP[k + 1] - 1), jnp.int32)
            for i in UNIT_POPS[unit_of(a, s)]:
                others = [o for o in range(3) if o != a and DIRS[i][o]]
                if others:
                    o = others[0]
                    off = sites.plane(o, 0 if DIRS[i][o] == 1 else 7)
                    bits = bits | jnp.where(off, 0, 1 << (i - 1))
            bits = jnp.where(sites.plane(a, 0 if s == 1 else 7), bits, 0)
        else:
            i = OPP[k + 1]
            c = DIRS[i]
            a, o = axes
            at = sites.plane(a, 0 if c[a] == 1 else 7) & sites.plane(o, 0 if c[o] == 1 else 7)
            bits = jnp.where(at, 1 << (i - 1), 0)
        gone = [(nbr_ref[0, b, k] < 0).astype(jnp.int32) for b in range(4)]
        miss = jnp.where(
            group < 2,
            jnp.where(group == 0, gone[0], gone[1]),
            jnp.where(group == 2, gone[2], gone[3]),
        )
        closed = closed | jnp.where(miss != 0, bits, zero)
    code = (irows[0].reshape(GRID) & ~closed & ((1 << 18) - 1)) + (irows[1].reshape(GRID) << 18)
    state[40:42] = code.astype(F32)
    collide_pack(sites, f, relax, state, state, CODE + 4)
    lo[0:12] = state[42:54]
    hi[0:12] = state[42:54]


def step_kernel(nbr_ref, state, post_in, unit_in, left_ref, right_ref, post_ref, unit_ref, pool, got):
    sites = Sites()
    me = lax.axis_index("gx")
    f = stream(sites, me, nbr_ref, post_in, unit_in, left_ref, right_ref, state, pool, got)
    collide_pack(sites, f, state[CODE : CODE + 2], post_ref, unit_ref)


def second_kernel(nbr_ref, state, left_ref, right_ref, conc, diff,
                  post_ref, unit_ref, ya, yb, za, zb, pool, got):
    sites = Sites()
    me = lax.axis_index("gx")
    f = stream(sites, me, nbr_ref, state, state, left_ref, right_ref, state, pool, got, CODE + 4)
    collide_pack(sites, f, state[CODE : CODE + 2], post_ref, unit_ref)
    first_rims(conc, diff, left_ref, right_ref, ya, yb, za, zb)


def last_kernel(nbr_ref, own_ref, state, post_in, unit_in, left_ref, right_ref, out_ref, send_ref, pool, got, rows, jrows):
    sites = Sites()
    me = lax.axis_index("gx")
    f = stream(sites, me, nbr_ref, post_in, unit_in, left_ref, right_ref, state, pool, got)
    for i in range(19):
        rows[i] = (f[i] * np.float32(1.0 / WEIGHT[i])).reshape(16, 128)
    j = moments(f)
    for a in range(3):
        v = j[a]
        for bit in (8, 16, 32, 64):
            up = pltpu.roll(v, bit, 2)
            down = up if bit == 64 else pltpu.roll(v, 128 - bit, 2)
            v = jnp.where((sites.lane & bit) != 0, up, down)
        jrows[a] = v.reshape(16, 128)
    send_ref[...] = jnp.zeros(send_ref.shape, F32)
    for b in range(4):
        o = own_ref[0, 4 * me + b]
        for a in range(3):
            send_ref[o, 4 * a : 4 * a + 4] = jrows[a, 4 * b : 4 * b + 4]

        @pl.when(o < 15)
        def _():
            for a in range(3):
                send_ref[o + 1, 12 + a : 13 + a] = jrows[a, 4 * b + 3 : 4 * b + 4]

        @pl.when(o > 0)
        def _():
            for a in range(3):
                send_ref[o - 1, 15 + a : 16 + a] = jrows[a, 4 * b : 4 * b + 1]

    for i in range(19):
        for r in range(4):
            out_ref[i, 0, :, 128 * r : 128 * r + 128] = rows[i, pl.ds(r, 4, stride=4), :]


def even(axis):
    return lax.rem(lax.axis_index(axis), 2) == 0


class Rims:
    def __init__(self, lane, ya, yb):
        self.lane, self.ya, self.yb = lane, ya, yb
        self.lo = jnp.zeros((8, 128), F32)
        self.hi = jnp.zeros((8, 128), F32)
        self.y_even = even("gy")

    def put(self, value, j, s, row):
        self.ya[s, row : row + 1] = jnp.where(self.y_even, value[7:8], value[0:1])
        self.yb[s, row : row + 1] = jnp.where(self.y_even, value[0:1], value[7:8])
        at = self.lane == j
        self.lo = jnp.where(at, pltpu.roll(value, j, 1) if j else value, self.lo)
        self.hi = jnp.where(at, pltpu.roll(value, (j + 1) % 128, 1), self.hi)

    def finish(self, za, zb):
        z_even = even("gz")
        za[...] = jnp.where(z_even, self.hi, self.lo)
        zb[...] = jnp.where(z_even, self.lo, self.hi)


def first_rims(conc, diff, xl, xr, ya, yb, za, zb):
    lane = lax.broadcasted_iota(jnp.int32, (8, 128), 1)
    rims = Rims(lane, ya, yb)
    for fld in range(5):
        for p in range(12):
            q = p - 2
            if q < 0:
                v = xl[slab(fld, 3 + q)]
            elif q > 7:
                v = xr[slab(fld, q - 8)]
            else:
                v = conc[fld, q] if fld < 4 else diff[q]
            rims.put(v, fld * 12 + p, fld, p)
    rims.finish(za, zb)


class Planes:
    def __init__(self, ya, yb, za, zb):
        self.sub = lax.broadcasted_iota(jnp.int32, (8, 128), 0)
        self.lane = lax.broadcasted_iota(jnp.int32, (8, 128), 1)
        self.ya, self.yb, self.y_even = ya, yb, even("gy")
        z_even = even("gz")
        self.z_lo = jnp.where(z_even, zb[...], za[...])
        self.z_hi = jnp.where(z_even, za[...], zb[...])

    def beside(self, v, s, row, j):
        a, b = self.ya[s, row : row + 1], self.yb[s, row : row + 1]
        lo = jnp.broadcast_to(jnp.where(self.y_even, b, a), (8, 128))
        hi = jnp.broadcast_to(jnp.where(self.y_even, a, b), (8, 128))
        ym = jnp.where(self.sub == 0, lo, pltpu.roll(v, 1, 0))
        yp = jnp.where(self.sub == 7, hi, pltpu.roll(v, 7, 0))
        zl = pltpu.roll(self.z_lo, (128 - j) % 128, 1) if j else self.z_lo
        zm = jnp.where(self.lane == 0, zl, pltpu.roll(v, 1, 1))
        zp = jnp.where(self.lane == 127, pltpu.roll(self.z_hi, 127 - j, 1), pltpu.roll(v, 127, 1))
        return ym, yp, zm, zp


def advance(s, cm, c, cp, around, spread, drift, upt, up1):
    k = GAIN[s]
    acc = c
    for v, g, d in zip((cm, cp) + tuple(around), spread, drift):
        w = d + (g if k == 1.0 else k * g)
        acc = acc + w * (v - c)
    if s == 2:
        return acc + 2.0 * up1
    return acc - upt * c / (HALF[s] + jnp.abs(c))


def tissue(planes, lo, hi, get_c, get_coef, get_upt, me, store, rims=None, rim_lo=0, rim_hi=0):
    for p in range(lo, hi):
        spread, drift = get_coef(p)
        upt = get_upt(p)
        keep = me > 0 if p < 0 else (me < 15 if p > 7 else None)
        c1 = get_c(1, p)
        up1 = upt * c1 / (HALF[1] + jnp.abs(c1))
        for s in range(4):
            c = get_c(s, p)
            around = planes.beside(c, s, p - lo, s * (hi - lo) + p - lo)
            v = advance(s, get_c(s, p - 1), c, get_c(s, p + 1), around, spread, drift, upt, up1)
            if keep is not None:
                v = jnp.where(keep, v, 0.0)
            store(s, p, v)
            if rim_lo <= p < rim_hi:
                rims.put(v, s * (rim_hi - rim_lo) + p - rim_lo, s, p - rim_lo)


def velocity_kernel(own_ref, slot_ref, recv, drift, blocks, slabs):
    me = lax.axis_index("gx")
    blocks[...] = jnp.zeros(blocks.shape, F32)
    slabs[...] = jnp.zeros(slabs.shape, F32)
    for m in range(16):
        own, low, high = jnp.int32(16), jnp.int32(16), jnp.int32(16)
        for b in range(4):
            o = own_ref[0, 4 * m + b]
            at = slot_ref[0, 4 * m + b]
            own = jnp.where(o == me, at, own)
            low = jnp.where(o == me - 1, at, low)
            high = jnp.where(o == me + 1, at, high)
        blocks[pl.ds(pl.multiple_of(16 * own, 16), 16), :] = recv[m, 0:16]
        for a in range(3):
            slabs[a, pl.ds(low, 1), :] = recv[m, 12 + a : 13 + a]
            slabs[3 + a, pl.ds(high, 1), :] = recv[m, 15 + a : 16 + a]
    group = lax.broadcasted_iota(jnp.int32, (16, 128), 1) >> 3
    masks = [(group & (1 << bit)) != 0 for bit in range(4)]

    def turned(x):
        x = pltpu.roll(x, 8, 1, stride=8, stride_axis=0)
        for bit in range(4):
            x = jnp.where(masks[bit], pltpu.roll(x, 16 - (1 << bit), 0), x)
        return pltpu.roll(x, 0, 1, stride=8, stride_axis=0)

    for a in range(3):
        for r in range(6):
            if r == 0:
                x = slabs[a, 0:16]
            elif r == 5:
                x = slabs[3 + a, 0:16]
            else:
                x = blocks[pl.ds(4 * a + r - 1, 16, stride=16), :]
            t = turned(x)
            for h in range(2):
                u = 3.0 * t[8 * h : 8 * h + 8]
                drift[2 * a, 2 * r + h] = jnp.maximum(u, 0.0)
                drift[2 * a + 1, 2 * r + h] = -jnp.minimum(u, 0.0)


def tissue1_kernel(drift, conc, diff, upt, xl, xr, za, zb, ya, yb,
                   c_out, spread_out, y0, y1, z0, z1):
    me = lax.axis_index("gx")
    planes = Planes(ya, yb, za, zb)

    def field(f, own):
        def get(p):
            if p < 0:
                return xl[slab(f, 3 + p)]
            if p > 7:
                return xr[slab(f, p - 8)]
            return own(p)
        return get

    get_d = field(4, lambda p: diff[p])
    get_u = field(5, lambda p: upt[p])
    gets = [field(s, lambda p, s=s: conc[s, p]) for s in range(4)]

    def get_coef(p):
        d = get_d(p)
        q = p + 2
        around = planes.beside(d, 4, q, 48 + q)
        spread = [0.5 * (d + n) for n in (get_d(p - 1), get_d(p + 1)) + tuple(around)]
        for n in range(6):
            spread_out[n, q] = spread[n]
        return spread, [drift[n, q] for n in range(6)]

    def store(s, p, v):
        c_out[s, p + 2] = v

    rims = Rims(planes.lane, y0, y1)
    tissue(planes, -2, 10, lambda s, p: gets[s](p), get_coef, get_u, me, store, rims, -1, 9)
    rims.finish(z0, z1)


def later_coef(spread, drift):
    return lambda p: ([spread[n, p + 2] for n in range(6)], [drift[n, p + 2] for n in range(6)])


def tissue2_kernel(drift, spread, conc, upt, xl, xr, za, zb, ya, yb, c_out, y0, y1, z0, z1):
    me = lax.axis_index("gx")
    planes = Planes(ya, yb, za, zb)

    def get_u(p):
        return xl[slab(5, 3 + p)] if p < 0 else (xr[slab(5, p - 8)] if p > 7 else upt[p])

    def store(s, p, v):
        c_out[s, p + 1] = v

    rims = Rims(planes.lane, y0, y1)
    tissue(planes, -1, 9, lambda s, p: conc[s, p + 2], later_coef(spread, drift), get_u, me, store,
           rims, 0, 8)
    rims.finish(z0, z1)


def tissue3_kernel(drift, spread, conc, upt, za, zb, ya, yb, out):
    planes = Planes(ya, yb, za, zb)

    def store(s, p, v):
        out[s, p] = v

    tissue(planes, 0, 8, lambda s, p: conc[s, p + 1], later_coef(spread, drift), lambda p: upt[p],
           None, store)


VMEM = pltpu.VMEM


def call(kernel, smem, arrays, outs, scratch=(), space=VMEM, limit=8 << 20):
    return pl.pallas_call(
        kernel,
        in_specs=[pl.BlockSpec(memory_space=pltpu.SMEM)] * len(smem)
        + [pl.BlockSpec(memory_space=space)] * len(arrays),
        out_specs=tuple(pl.BlockSpec(memory_space=VMEM) for _ in outs),
        out_shape=tuple(jax.ShapeDtypeStruct(s, t) for s, t in outs),
        scratch_shapes=[VMEM(*x) if isinstance(x, tuple) else x for x in scratch],
        compiler_params=pltpu.CompilerParams(vmem_limit_bytes=limit),
        name=kernel.__name__,
    )(*smem, *arrays)


def hop(x, axis, step):
    n = lax.axis_size(axis)
    return lax.ppermute(x, axis, [(i, i + step) for i in range(n) if 0 <= i + step < n])


def swap(x, axis, first):
    n = lax.axis_size(axis)
    return lax.ppermute(x, axis, [(i, j) for i in range(n) for j in [i ^ 1 if first else ((i + 1) ^ 1) - 1] if 0 <= j < n])


def swaps(turn, ya, yb, za, zb):
    out = []
    for name, x, axis, first in (("za", za, "gz", True), ("zb", zb, "gz", False), ("ya", ya, "gy", True), ("yb", yb, "gy", False)):
        with jax.named_scope(f"{name}{turn}"):
            out.append(swap(x, axis, first))
    return tuple(out)


def shards(populations, viscosity, links, flags, neighbours, owners, slots, conc, diff, upt):
    i32 = jnp.int32
    tiles = lambda n: ((n, 8, 128), F32)
    tile = ((8, 128), F32)
    faces = lambda fields, rows: [((fields, rows, 128), F32)] * 2 + [tile, tile]
    pool = [((6, 48, 128), F32), ((18, 16, 128), F32)]
    state, lo, hi = call(
        first_kernel, (neighbours,), (populations, viscosity, links, flags, conc, diff, upt),
        [tiles(54), tiles(30), tiles(30)],
        [((20, 16, 128), F32), ((2, 16, 128), i32), ((19, 1, 4, 512), F32), ((1, 4, 512), F32),
         ((1, 4, 512), i32), ((1, 4, 512), i32), pltpu.SemaphoreType.DMA((16,))],
        space=pltpu.HBM, limit=67043328 - (420 << 10),
    )
    xl, xr = hop(hi, "gx", 1), hop(lo, "gx", -1)
    post, unit, *rim = call(
        second_kernel, (neighbours,), (state, xl, xr, conc, diff),
        [tiles(38), tiles(12)] + faces(5, 16), pool,
    )
    rim = swaps(0, *rim)
    for _ in range(FLOW_STEPS - 2):
        left, right = hop(unit, "gx", 1), hop(unit, "gx", -1)
        post, unit = call(
            step_kernel, (neighbours,), (state, post, unit, left, right), [tiles(38), tiles(12)], pool
        )
    left, right = hop(unit, "gx", 1), hop(unit, "gx", -1)
    weighted, send = call(
        last_kernel, (neighbours, owners), (state, post, unit, left, right),
        [((19, 1, 4, 512), F32), ((16, 24, 128), F32)],
        pool + [((19, 16, 128), F32), ((3, 16, 128), F32)],
    )
    with jax.named_scope("spread"):
        recv = lax.all_to_all(send, "gx", 0, 0)
    with jax.named_scope("drift"):
        (drift,) = call(
            velocity_kernel, (owners, slots), (recv,), [((6, 12, 8, 128), F32)],
            [((17 * 16, 128), F32), ((6, 24, 128), F32)],
        )
    c1, spread, *faces1 = call(
        tissue1_kernel, (), (drift, conc, diff, upt, xl, xr) + rim,
        [((4, 12, 8, 128), F32), ((6, 12, 8, 128), F32)] + faces(4, 16),
    )
    c2, *faces2 = call(
        tissue2_kernel, (), (drift, spread, c1, upt, xl, xr) + swaps(1, *faces1),
        [((4, 10, 8, 128), F32)] + faces(4, 8),
    )
    (out,) = call(
        tissue3_kernel, (), (drift, spread, c2, upt) + swaps(2, *faces2), [((4, 8, 8, 128), F32)]
    )
    return weighted, out


def solution(mesh):
    site = P(("gy", "gz"), "gx", None)
    brick = P("gx", "gy", "gz")
    return jax.shard_map(
        shards,
        mesh=mesh,
        in_specs=(
            P(None, ("gy", "gz"), "gx", None), site, site, site, site,
            P(("gy", "gz"), None), P(("gy", "gz"), None),
            P(None, "gx", "gy", "gz"), brick, brick,
        ),
        out_specs=(P(None, ("gy", "gz"), "gx", None), P(None, "gx", "gy", "gz")),
        check_vma=False,
    )
```

time: 572 us -> 111 us (0.19)
  the two profiles are of different devices: /device:TPU:90 before, /device:TPU:21 now
where the time goes in v1:
time: 111 us; the launch traced here: 110 us
  starting transfers between devices  79.4 us (72%)
  waiting for transfers between devices  15.4 us (14%)
  Pallas kernels  13 us (12%)
    ppermute x12, starting transfers between devices, swap(): lax.ppermute(x, axis, [(i, j) for i in range(n) for j in [i ^ 1 if first...  37.5 us
    ppermute x8, starting transfers between devices, hop(): lax.ppermute(x, axis, [(i, i + step) for i in range(n) if 0 <= i + step <...  23.1 us
    all_to_all x1, starting transfers between devices, shards(): recv = lax.all_to_all(send, 'gx', 0, 0)  18.7 us
    pallas_call x9, Pallas kernels, call(): pl.pallas_call(kernel, in_specs=[pl.BlockSpec(memory_space=pltpu.SMEM)] *...  13 us
    ppermute x8, waiting for transfers between devices, hop(): lax.ppermute(x, axis, [(i, i + step) for i in range(n) if 0 <= i + step <...  8.54 us
    ppermute x12, waiting for transfers between devices, swap(): lax.ppermute(x, axis, [(i, j) for i in range(n) for j in [i ^ 1 if first...  6.9 us
  transfers between devices with their start and end apart: 21, of which 9 were waited for; matrix products, arithmetic and copies ran while one was open for 0% of the time, Pallas kernels for 1%

profile of v1, /device:TPU:21, one launch (start us, length us, event | category | flops | bytes accessed | tf_op | source)
XLA Modules:
  0.0 109.7 jit_solution(10572169857182788484)
XLA Ops:
  0.7 2.8 %first_kernel.1 = (f32[54,8,128]{2,1,0:T(8,128)}, f32[30,8,128]{2,1,0:T(8,128)}, f32[30,8,128]{2,1,0:T(8,128)}) custom-call(s32[1,4,18]{2,1,0:T(4,128)} %nbr_ref.9, f32[19,1,4,512]{3,2,1,0:T(4,128)} %pop_hbm.1, f32[1,4,512]{2,1,0:T(4,128)} %visc_hbm.1, s32[1,4,512]{2,1,0:T(4,128)} %link_hbm.1, s32[1,4,512]{2,1,0:T(4,128)} %flag_hbm.1, ...), custom_call_target="tpu_custom_call" | custom-call | tf_op jit(solution)/shard_map/first_kernel/pallas_call | solution.py:505
  3.5 3.5 %collective-permute-start = (f32[30,8,128]{2,1,0:T(8,128)}, f32[30,8,128]{2,1,0:T(8,128)S(1)}, u32[]{:S(2)}, u32[]{:S(2)}) collective-permute-start(f32[30,8,128]{2,1,0:T(8,128)} %get-tuple-element.29), channel_id=1, source_target_pairs={{0,32},{32,64},{64,96},{96,128},{128,160},{160,192},{192,224},{224... | collective-permute-start | bytes 368648 | tf_op jit(solution)/shard_map/ppermute | solution.py:519
  7.1 1.3 %collective-permute-start.1 = (f32[30,8,128]{2,1,0:T(8,128)}, f32[30,8,128]{2,1,0:T(8,128)S(1)}, u32[]{:S(2)}, u32[]{:S(2)}) collective-permute-start(f32[30,8,128]{2,1,0:T(8,128)} %get-tuple-element.30), channel_id=1, source_target_pairs={{32,0},{64,32},{96,64},{128,96},{160,128},{192,160},{224,192},{256... | collective-permute-start | bytes 368648 | tf_op jit(solution)/shard_map/ppermute | solution.py:519
  9.4 4.1 %collective-permute-done.1.right_ref.xr = f32[30,8,128]{2,1,0:T(8,128)S(1)} collective-permute-done((f32[30,8,128]{2,1,0:T(8,128)}, f32[30,8,128]{2,1,0:T(8,128)S(1)}, u32[]{:S(2)}, u32[]{:S(2)}) %collective-permute-start.1) | collective-permute-done | bytes 122912 | tf_op jit(solution)/shard_map/ppermute | solution.py:519
  14.4 1.2 %second_kernel.1 = (f32[38,8,128]{2,1,0:T(8,128)S(1)}, f32[12,8,128]{2,1,0:T(8,128)S(1)}, f32[5,16,128]{2,1,0:T(8,128)S(1)}, f32[5,16,128]{2,1,0:T(8,128)S(1)}, ...) custom-call(s32[1,4,18]{2,1,0:T(4,128)S(1)} %copy-done.5, f32[54,8,128]{2,1,0:T(8,128)S(1)} %copy-done, ...), custom_call_target="tpu_custom_call" | custom-call | tf_op jit(solution)/shard_map/second_kernel/pallas_call | solution.py:505
  15.6 1.3 %collective-permute-start.3 = (f32[12,8,128]{2,1,0:T(8,128)S(1)}, f32[12,8,128]{2,1,0:T(8,128)S(1)}, u32[]{:S(2)}, u32[]{:S(2)}) collective-permute-start(f32[12,8,128]{2,1,0:T(8,128)S(1)} %get-tuple-element.32.unit_in), channel_id=1, source_target_pairs={{32,0},{64,32},{96,64},{128,96},{160,128},{192,160},{224,192},{256... | collective-permute-start | bytes 147464 | tf_op jit(solution)/shard_map/ppermute | solution.py:519
  16.9 4.2 %collective-permute-start.2 = (f32[12,8,128]{2,1,0:T(8,128)S(1)}, f32[12,8,128]{2,1,0:T(8,128)S(1)}, u32[]{:S(2)}, u32[]{:S(2)}) collective-permute-start(f32[12,8,128]{2,1,0:T(8,128)S(1)} %get-tuple-element.32.unit_in), channel_id=1, source_target_pairs={{0,32},{32,64},{64,96},{96,128},{128,160},{160,192},{192,224},{224... | collective-permute-start | bytes 147464 | tf_op jit(solution)/shard_map/ppermute | solution.py:519
  21.0 1.1 %collective-permute-done.2.left_ref = f32[12,8,128]{2,1,0:T(8,128)S(1)} collective-permute-done((f32[12,8,128]{2,1,0:T(8,128)S(1)}, f32[12,8,128]{2,1,0:T(8,128)S(1)}, u32[]{:S(2)}, u32[]{:S(2)}) %collective-permute-start.2) | collective-permute-done | bytes 49184 | tf_op jit(solution)/shard_map/ppermute | solution.py:519
  23.2 1.3 %collective-permute-start.5 = (f32[12,8,128]{2,1,0:T(8,128)S(1)}, f32[12,8,128]{2,1,0:T(8,128)S(1)}, u32[]{:S(2)}, u32[]{:S(2)}) collective-permute-start(f32[12,8,128]{2,1,0:T(8,128)S(1)} %get-tuple-element.34.unit_in), channel_id=1, source_target_pairs={{32,0},{64,32},{96,64},{128,96},{160,128},{192,160},{224,192},{256... | collective-permute-start | bytes 147464 | tf_op jit(solution)/shard_map/ppermute | solution.py:519
  24.5 5.5 %collective-permute-start.4 = (f32[12,8,128]{2,1,0:T(8,128)S(1)}, f32[12,8,128]{2,1,0:T(8,128)S(1)}, u32[]{:S(2)}, u32[]{:S(2)}) collective-permute-start(f32[12,8,128]{2,1,0:T(8,128)S(1)} %get-tuple-element.34.unit_in), channel_id=1, source_target_pairs={{0,32},{32,64},{64,96},{96,128},{128,160},{160,192},{192,224},{224... | collective-permute-start | bytes 147464 | tf_op jit(solution)/shard_map/ppermute | solution.py:519
  30.0 1.1 %collective-permute-done.4.left_ref = f32[12,8,128]{2,1,0:T(8,128)S(1)} collective-permute-done((f32[12,8,128]{2,1,0:T(8,128)S(1)}, f32[12,8,128]{2,1,0:T(8,128)S(1)}, u32[]{:S(2)}, u32[]{:S(2)}) %collective-permute-start.4) | collective-permute-done | bytes 49184 | tf_op jit(solution)/shard_map/ppermute | solution.py:519
  32.2 1.3 %collective-permute-start.7 = (f32[12,8,128]{2,1,0:T(8,128)S(1)}, f32[12,8,128]{2,1,0:T(8,128)S(1)}, u32[]{:S(2)}, u32[]{:S(2)}) collective-permute-start(f32[12,8,128]{2,1,0:T(8,128)S(1)} %get-tuple-element.36.unit_in), channel_id=1, source_target_pairs={{32,0},{64,32},{96,64},{128,96},{160,128},{192,160},{224,192},{256... | collective-permute-start | bytes 147464 | tf_op jit(solution)/shard_map/ppermute | solution.py:519
  33.5 4.7 %collective-permute-start.6 = (f32[12,8,128]{2,1,0:T(8,128)S(1)}, f32[12,8,128]{2,1,0:T(8,128)S(1)}, u32[]{:S(2)}, u32[]{:S(2)}) collective-permute-start(f32[12,8,128]{2,1,0:T(8,128)S(1)} %get-tuple-element.36.unit_in), channel_id=1, source_target_pairs={{0,32},{32,64},{64,96},{96,128},{128,160},{160,192},{192,224},{224... | collective-permute-start | bytes 147464 | tf_op jit(solution)/shard_map/ppermute | solution.py:519
  38.3 1.1 %collective-permute-done.6.left_ref = f32[12,8,128]{2,1,0:T(8,128)S(1)} collective-permute-done((f32[12,8,128]{2,1,0:T(8,128)S(1)}, f32[12,8,128]{2,1,0:T(8,128)S(1)}, u32[]{:S(2)}, u32[]{:S(2)}) %collective-permute-start.6) | collective-permute-done | bytes 49184 | tf_op jit(solution)/shard_map/ppermute | solution.py:519
  39.4 1.9 %last_kernel.1 = (f32[19,1,4,512]{3,2,1,0:T(4,128)}, f32[16,24,128]{2,1,0:T(8,128)}) custom-call(s32[1,4,18]{2,1,0:T(4,128)S(1)} %copy-done.5, s32[1,64]{1,0:T(1,128)S(1)} %copy-done.6, f32[54,8,128]{2,1,0:T(8,128)S(1)} %copy-done.1, f32[38,8,128]{2,1,0:T(8,128)S(1)} %get-tuple-element.35.post_in, f32[12,8,128]{2,1,0:T(8,128)S(1)} %get-tuple-element.36.unit_in, ...), custom_call_target="tpu_custom_call" | custom-call | tf_op jit(solution)/shard_map/last_kernel/pallas_call | solution.py:505
  41.3 18.7 %all-to-all-start = ((f32[16,24,128]{2,1,0:T(8,128)}), f32[16,24,128]{2,1,0:T(8,128)S(1)}, u32[]{:S(2)}, u32[]{:S(2)}) async-start(f32[16,24,128]{2,1,0:T(8,128)} %get-tuple-element.38), calls=%async_computation | async-start | bytes 393216 | tf_op jit(solution)/shard_map/spread/all_to_all | solution.py:566
  60.1 8.0 %collective-permute-start.10 = (f32[5,16,128]{2,1,0:T(8,128)S(1)}, f32[5,16,128]{2,1,0:T(8,128)S(1)}, u32[]{:S(2)}, u32[]{:S(2)}) collective-permute-start(f32[5,16,128]{2,1,0:T(8,128)S(1)} %get-tuple-element.41), channel_id=1, source_target_pairs={{0,4},{4,0},{8,12},{12,8},{16,20},{20,16},{24,28},{28,24},{1,5},{5... | collective-permute-start | bytes 122888 | tf_op jit(solution)/shard_map/ya0/ppermute | solution.py:524
  68.1 2.7 %collective-permute-start.11 = (f32[5,16,128]{2,1,0:T(8,128)S(1)}, f32[5,16,128]{2,1,0:T(8,128)S(1)}, u32[]{:S(2)}, u32[]{:S(2)}) collective-permute-start(f32[5,16,128]{2,1,0:T(8,128)S(1)} %get-tuple-element.42), channel_id=1, source_target_pairs={{4,8},{8,4},{12,16},{16,12},{20,24},{24,20},{5,9},{9,5},{13,17},{1... | collective-permute-start | bytes 122888 | tf_op jit(solution)/shard_map/yb0/ppermute | solution.py:524
  70.9 2.9 %collective-permute-start.8 = (f32[8,128]{1,0:T(8,128)S(1)}, f32[8,128]{1,0:T(8,128)S(1)}, u32[]{:S(2)}, u32[]{:S(2)}) collective-permute-start(f32[8,128]{1,0:T(8,128)S(1)} %get-tuple-element.39), channel_id=1, source_target_pairs={{0,1},{1,0},{2,3},{3,2},{4,5},{5,4},{6,7},{7,6},{8,9},{9,8},{10,11... | collective-permute-start | bytes 12296 | tf_op jit(solution)/shard_map/za0/ppermute | solution.py:524
  73.8 1.9 %collective-permute-start.9 = (f32[8,128]{1,0:T(8,128)S(1)}, f32[8,128]{1,0:T(8,128)S(1)}, u32[]{:S(2)}, u32[]{:S(2)}) collective-permute-start(f32[8,128]{1,0:T(8,128)S(1)} %get-tuple-element.40), channel_id=1, source_target_pairs={{1,2},{2,1},{5,6},{6,5},{9,10},{10,9},{13,14},{14,13},{17,18},{18,... | collective-permute-start | bytes 12296 | tf_op jit(solution)/shard_map/zb0/ppermute | solution.py:524
  76.7 1.7 %collective-permute-done.9.zb = f32[8,128]{1,0:T(8,128)S(1)} collective-permute-done((f32[8,128]{1,0:T(8,128)S(1)}, f32[8,128]{1,0:T(8,128)S(1)}, u32[]{:S(2)}, u32[]{:S(2)}) %collective-permute-start.9) | collective-permute-done | bytes 4128 | tf_op jit(solution)/shard_map/zb0/ppermute | solution.py:524
  78.5 2.1 %tissue1_kernel.1 = (f32[4,12,8,128]{3,2,1,0:T(8,128)S(1)}, f32[6,12,8,128]{3,2,1,0:T(8,128)S(1)}, f32[4,16,128]{2,1,0:T(8,128)S(1)}, f32[4,16,128]{2,1,0:T(8,12...) custom-call(f32[6,12,8,128]{3,2,1,0:T(8,128)S(1)} %velocity_kernel.1.drift, f32[4,8,8,128]{3,2,1,0:T(8,128)S(1)} %copy-done.2, ...), custom_call_target="tpu_custom_call" | custom-call | tf_op jit(solution)/shard_map/tissue1_kernel/pallas_call | solution.py:505
  80.5 4.4 %collective-permute-start.14 = (f32[4,16,128]{2,1,0:T(8,128)S(1)}, f32[4,16,128]{2,1,0:T(8,128)S(1)}, u32[]{:S(2)}, u32[]{:S(2)}) collective-permute-start(f32[4,16,128]{2,1,0:T(8,128)S(1)} %get-tuple-element.47), channel_id=1, source_target_pairs={{0,4},{4,0},{8,12},{12,8},{16,20},{20,16},{24,28},{28,24},{1,5},{5... | collective-permute-start | bytes 98312 | tf_op jit(solution)/shard_map/ya1/ppermute | solution.py:524
  84.9 2.7 %collective-permute-start.15 = (f32[4,16,128]{2,1,0:T(8,128)S(1)}, f32[4,16,128]{2,1,0:T(8,128)S(1)}, u32[]{:S(2)}, u32[]{:S(2)}) collective-permute-start(f32[4,16,128]{2,1,0:T(8,128)S(1)} %get-tuple-element.48), channel_id=1, source_target_pairs={{4,8},{8,4},{12,16},{16,12},{20,24},{24,20},{5,9},{9,5},{13,17},{1... | collective-permute-start | bytes 98312 | tf_op jit(solution)/shard_map/yb1/ppermute | solution.py:524
  87.6 2.9 %collective-permute-start.12 = (f32[8,128]{1,0:T(8,128)S(1)}, f32[8,128]{1,0:T(8,128)S(1)}, u32[]{:S(2)}, u32[]{:S(2)}) collective-permute-start(f32[8,128]{1,0:T(8,128)S(1)} %get-tuple-element.45), channel_id=1, source_target_pairs={{0,1},{1,0},{2,3},{3,2},{4,5},{5,4},{6,7},{7,6},{8,9},{9,8},{10,11... | collective-permute-start | bytes 12296 | tf_op jit(solution)/shard_map/za1/ppermute | solution.py:524
  90.6 1.9 %collective-permute-start.13 = (f32[8,128]{1,0:T(8,128)S(1)}, f32[8,128]{1,0:T(8,128)S(1)}, u32[]{:S(2)}, u32[]{:S(2)}) collective-permute-start(f32[8,128]{1,0:T(8,128)S(1)} %get-tuple-element.46), channel_id=1, source_target_pairs={{1,2},{2,1},{5,6},{6,5},{9,10},{10,9},{13,14},{14,13},{17,18},{18,... | collective-permute-start | bytes 12296 | tf_op jit(solution)/shard_map/zb1/ppermute | solution.py:524
  92.5 2.4 %collective-permute-done.13.zb = f32[8,128]{1,0:T(8,128)S(1)} collective-permute-done((f32[8,128]{1,0:T(8,128)S(1)}, f32[8,128]{1,0:T(8,128)S(1)}, u32[]{:S(2)}, u32[]{:S(2)}) %collective-permute-start.13) | collective-permute-done | bytes 4128 | tf_op jit(solution)/shard_map/zb1/ppermute | solution.py:524
  96.0 3.2 %collective-permute-start.18 = (f32[4,8,128]{2,1,0:T(8,128)S(1)}, f32[4,8,128]{2,1,0:T(8,128)S(1)}, u32[]{:S(2)}, u32[]{:S(2)}) collective-permute-start(f32[4,8,128]{2,1,0:T(8,128)S(1)} %get-tuple-element.52), channel_id=1, source_target_pairs={{0,4},{4,0},{8,12},{12,8},{16,20},{20,16},{24,28},{28,24},{1,5},{5... | collective-permute-start | bytes 49160 | tf_op jit(solution)/shard_map/ya2/ppermute | solution.py:524
  99.2 3.0 %collective-permute-start.19 = (f32[4,8,128]{2,1,0:T(8,128)S(1)}, f32[4,8,128]{2,1,0:T(8,128)S(1)}, u32[]{:S(2)}, u32[]{:S(2)}) collective-permute-start(f32[4,8,128]{2,1,0:T(8,128)S(1)} %get-tuple-element.53), channel_id=1, source_target_pairs={{4,8},{8,4},{12,16},{16,12},{20,24},{24,20},{5,9},{9,5},{13,17},{1... | collective-permute-start | bytes 49160 | tf_op jit(solution)/shard_map/yb2/ppermute | solution.py:524
  102.2 1.9 %collective-permute-start.16 = (f32[8,128]{1,0:T(8,128)S(1)}, f32[8,128]{1,0:T(8,128)S(1)}, u32[]{:S(2)}, u32[]{:S(2)}) collective-permute-start(f32[8,128]{1,0:T(8,128)S(1)} %get-tuple-element.50), channel_id=1, source_target_pairs={{0,1},{1,0},{2,3},{3,2},{4,5},{5,4},{6,7},{7,6},{8,9},{9,8},{10,11... | collective-permute-start | bytes 12296 | tf_op jit(solution)/shard_map/za2/ppermute | solution.py:524
  104.1 1.9 %collective-permute-start.17 = (f32[8,128]{1,0:T(8,128)S(1)}, f32[8,128]{1,0:T(8,128)S(1)}, u32[]{:S(2)}, u32[]{:S(2)}) collective-permute-start(f32[8,128]{1,0:T(8,128)S(1)} %get-tuple-element.51), channel_id=1, source_target_pairs={{1,2},{2,1},{5,6},{6,5},{9,10},{10,9},{13,14},{14,13},{17,18},{18,... | collective-permute-start | bytes 12296 | tf_op jit(solution)/shard_map/zb2/ppermute | solution.py:524
  106.9 1.9 %collective-permute-done.17.zb = f32[8,128]{1,0:T(8,128)S(1)} collective-permute-done((f32[8,128]{1,0:T(8,128)S(1)}, f32[8,128]{1,0:T(8,128)S(1)}, u32[]{:S(2)}, u32[]{:S(2)}) %collective-permute-start.17) | collective-permute-done | bytes 4128 | tf_op jit(solution)/shard_map/zb2/ppermute | solution.py:524
  (35 shorter events, 7.8 us)
Async XLA Ops:
  0.6 12.8 %copy-start.4 = (f32[8,8,128]{2,1,0:T(8,128)S(1)}, f32[8,8,128]{2,1,0:T(8,128)}, u32[]{:S(2)}) copy-start(f32[8,8,128]{2,1,0:T(8,128)} %diff.3) | copy-start | bytes 98308
  0.6 12.8 %copy-start.2 = (f32[4,8,8,128]{3,2,1,0:T(8,128)S(1)}, f32[4,8,8,128]{3,2,1,0:T(8,128)}, u32[]{:S(2)}) copy-start(f32[4,8,8,128]{3,2,1,0:T(8,128)} %conc.3) | copy-start | bytes 393220
  3.5 10.0 %copy-start.5 = (s32[1,4,18]{2,1,0:T(4,128)S(1)}, s32[1,4,18]{2,1,0:T(4,128)}, u32[]{:S(2)}) copy-start(s32[1,4,18]{2,1,0:T(4,128)} %nbr_ref.9) | copy-start | bytes 868
  3.5 5.9 %collective-permute-start = (f32[30,8,128]{2,1,0:T(8,128)}, f32[30,8,128]{2,1,0:T(8,128)S(1)}, u32[]{:S(2)}, u32[]{:S(2)}) collective-permute-start(f32[30,8,128]{2,1,0:T(8,128)} %get-tuple-element.29), channel_id=1, source_target_pairs={{0,32},{32,64},{64,96},{96,128},{128,160},{160,192},{192,224},{224... | collective-permute-start | bytes 368648 | tf_op jit(solution)/shard_map/ppermute | solution.py:519
  7.1 6.4 %collective-permute-start.1 = (f32[30,8,128]{2,1,0:T(8,128)}, f32[30,8,128]{2,1,0:T(8,128)S(1)}, u32[]{:S(2)}, u32[]{:S(2)}) collective-permute-start(f32[30,8,128]{2,1,0:T(8,128)} %get-tuple-element.30), channel_id=1, source_target_pairs={{32,0},{64,32},{96,64},{128,96},{160,128},{192,160},{224,192},{256... | collective-permute-start | bytes 368648 | tf_op jit(solution)/shard_map/ppermute | solution.py:519
  13.5 0.9 copy-start
  14.4 7.8 %copy-start.1 = (f32[54,8,128]{2,1,0:T(8,128)S(1)}, f32[54,8,128]{2,1,0:T(8,128)}, u32[]{:S(2)}) copy-start(f32[54,8,128]{2,1,0:T(8,128)} %get-tuple-element.28.state) | copy-start | bytes 663556
  15.6 5.5 %collective-permute-start.3 = (f32[12,8,128]{2,1,0:T(8,128)S(1)}, f32[12,8,128]{2,1,0:T(8,128)S(1)}, u32[]{:S(2)}, u32[]{:S(2)}) collective-permute-start(f32[12,8,128]{2,1,0:T(8,128)S(1)} %get-tuple-element.32.unit_in), channel_id=1, source_target_pairs={{32,0},{64,32},{96,64},{128,96},{160,128},{192,160},{224,192},{256... | collective-permute-start | bytes 147464 | tf_op jit(solution)/shard_map/ppermute | solution.py:519
  16.9 5.3 %collective-permute-start.2 = (f32[12,8,128]{2,1,0:T(8,128)S(1)}, f32[12,8,128]{2,1,0:T(8,128)S(1)}, u32[]{:S(2)}, u32[]{:S(2)}) collective-permute-start(f32[12,8,128]{2,1,0:T(8,128)S(1)} %get-tuple-element.32.unit_in), channel_id=1, source_target_pairs={{0,32},{32,64},{64,96},{96,128},{128,160},{160,192},{192,224},{224... | collective-permute-start | bytes 147464 | tf_op jit(solution)/shard_map/ppermute | solution.py:519
  23.2 6.8 %collective-permute-start.5 = (f32[12,8,128]{2,1,0:T(8,128)S(1)}, f32[12,8,128]{2,1,0:T(8,128)S(1)}, u32[]{:S(2)}, u32[]{:S(2)}) collective-permute-start(f32[12,8,128]{2,1,0:T(8,128)S(1)} %get-tuple-element.34.unit_in), channel_id=1, source_target_pairs={{32,0},{64,32},{96,64},{128,96},{160,128},{192,160},{224,192},{256... | collective-permute-start | bytes 147464 | tf_op jit(solution)/shard_map/ppermute | solution.py:519
  24.5 6.6 %collective-permute-start.4 = (f32[12,8,128]{2,1,0:T(8,128)S(1)}, f32[12,8,128]{2,1,0:T(8,128)S(1)}, u32[]{:S(2)}, u32[]{:S(2)}) collective-permute-start(f32[12,8,128]{2,1,0:T(8,128)S(1)} %get-tuple-element.34.unit_in), channel_id=1, source_target_pairs={{0,32},{32,64},{64,96},{96,128},{128,160},{160,192},{192,224},{224... | collective-permute-start | bytes 147464 | tf_op jit(solution)/shard_map/ppermute | solution.py:519
  32.2 7.2 %copy-start.6 = (s32[1,64]{1,0:T(1,128)S(1)}, s32[1,64]{1,0:T(1,128)}, u32[]{:S(2)}) copy-start(s32[1,64]{1,0:T(1,128)} %own_ref.3) | copy-start | bytes 772
  32.2 6.0 %collective-permute-start.7 = (f32[12,8,128]{2,1,0:T(8,128)S(1)}, f32[12,8,128]{2,1,0:T(8,128)S(1)}, u32[]{:S(2)}, u32[]{:S(2)}) collective-permute-start(f32[12,8,128]{2,1,0:T(8,128)S(1)} %get-tuple-element.36.unit_in), channel_id=1, source_target_pairs={{32,0},{64,32},{96,64},{128,96},{160,128},{192,160},{224,192},{256... | collective-permute-start | bytes 147464 | tf_op jit(solution)/shard_map/ppermute | solution.py:519
  33.5 5.9 %collective-permute-start.6 = (f32[12,8,128]{2,1,0:T(8,128)S(1)}, f32[12,8,128]{2,1,0:T(8,128)S(1)}, u32[]{:S(2)}, u32[]{:S(2)}) collective-permute-start(f32[12,8,128]{2,1,0:T(8,128)S(1)} %get-tuple-element.36.unit_in), channel_id=1, source_target_pairs={{0,32},{32,64},{64,96},{96,128},{128,160},{160,192},{192,224},{224... | collective-permute-start | bytes 147464 | tf_op jit(solution)/shard_map/ppermute | solution.py:519
  41.3 34.4 %all-to-all-start = ((f32[16,24,128]{2,1,0:T(8,128)}), f32[16,24,128]{2,1,0:T(8,128)S(1)}, u32[]{:S(2)}, u32[]{:S(2)}) async-start(f32[16,24,128]{2,1,0:T(8,128)} %get-tuple-element.38), calls=%async_computation | async-start | bytes 393216 | tf_op jit(solution)/shard_map/spread/all_to_all | solution.py:566
  60.1 18.4 %collective-permute-start.10 = (f32[5,16,128]{2,1,0:T(8,128)S(1)}, f32[5,16,128]{2,1,0:T(8,128)S(1)}, u32[]{:S(2)}, u32[]{:S(2)}) collective-permute-start(f32[5,16,128]{2,1,0:T(8,128)S(1)} %get-tuple-element.41), channel_id=1, source_target_pairs={{0,4},{4,0},{8,12},{12,8},{16,20},{20,16},{24,28},{28,24},{1,5},{5... | collective-permute-start | bytes 122888 | tf_op jit(solution)/shard_map/ya0/ppermute | solution.py:524
  68.1 10.3 %collective-permute-start.11 = (f32[5,16,128]{2,1,0:T(8,128)S(1)}, f32[5,16,128]{2,1,0:T(8,128)S(1)}, u32[]{:S(2)}, u32[]{:S(2)}) collective-permute-start(f32[5,16,128]{2,1,0:T(8,128)S(1)} %get-tuple-element.42), channel_id=1, source_target_pairs={{4,8},{8,4},{12,16},{16,12},{20,24},{24,20},{5,9},{9,5},{13,17},{1... | collective-permute-start | bytes 122888 | tf_op jit(solution)/shard_map/yb0/ppermute | solution.py:524
  70.9 4.9 %copy-start.7 = (s32[1,64]{1,0:T(1,128)S(1)}, s32[1,64]{1,0:T(1,128)}, u32[]{:S(2)}) copy-start(s32[1,64]{1,0:T(1,128)} %slot_ref.1) | copy-start | bytes 772
  70.9 5.9 %collective-permute-start.8 = (f32[8,128]{1,0:T(8,128)S(1)}, f32[8,128]{1,0:T(8,128)S(1)}, u32[]{:S(2)}, u32[]{:S(2)}) collective-permute-start(f32[8,128]{1,0:T(8,128)S(1)} %get-tuple-element.39), channel_id=1, source_target_pairs={{0,1},{1,0},{2,3},{3,2},{4,5},{5,4},{6,7},{7,6},{8,9},{9,8},{10,11... | collective-permute-start | bytes 12296 | tf_op jit(solution)/shard_map/za0/ppermute | solution.py:524
  73.8 4.7 %copy-start.3 = (f32[8,8,128]{2,1,0:T(8,128)S(1)}, f32[8,8,128]{2,1,0:T(8,128)}, u32[]{:S(2)}) copy-start(f32[8,8,128]{2,1,0:T(8,128)} %upt.5) | copy-start | bytes 98308
  73.8 4.6 %collective-permute-start.9 = (f32[8,128]{1,0:T(8,128)S(1)}, f32[8,128]{1,0:T(8,128)S(1)}, u32[]{:S(2)}, u32[]{:S(2)}) collective-permute-start(f32[8,128]{1,0:T(8,128)S(1)} %get-tuple-element.40), channel_id=1, source_target_pairs={{1,2},{2,1},{5,6},{6,5},{9,10},{10,9},{13,14},{14,13},{17,18},{18,... | collective-permute-start | bytes 12296 | tf_op jit(solution)/shard_map/zb0/ppermute | solution.py:524
  80.5 14.4 %collective-permute-start.14 = (f32[4,16,128]{2,1,0:T(8,128)S(1)}, f32[4,16,128]{2,1,0:T(8,128)S(1)}, u32[]{:S(2)}, u32[]{:S(2)}) collective-permute-start(f32[4,16,128]{2,1,0:T(8,128)S(1)} %get-tuple-element.47), channel_id=1, source_target_pairs={{0,4},{4,0},{8,12},{12,8},{16,20},{20,16},{24,28},{28,24},{1,5},{5... | collective-permute-start | bytes 98312 | tf_op jit(solution)/shard_map/ya1/ppermute | solution.py:524
  84.9 10.0 %collective-permute-start.15 = (f32[4,16,128]{2,1,0:T(8,128)S(1)}, f32[4,16,128]{2,1,0:T(8,128)S(1)}, u32[]{:S(2)}, u32[]{:S(2)}) collective-permute-start(f32[4,16,128]{2,1,0:T(8,128)S(1)} %get-tuple-element.48), channel_id=1, source_target_pairs={{4,8},{8,4},{12,16},{16,12},{20,24},{24,20},{5,9},{9,5},{13,17},{1... | collective-permute-start | bytes 98312 | tf_op jit(solution)/shard_map/yb1/ppermute | solution.py:524
  87.6 4.8 %collective-permute-start.12 = (f32[8,128]{1,0:T(8,128)S(1)}, f32[8,128]{1,0:T(8,128)S(1)}, u32[]{:S(2)}, u32[]{:S(2)}) collective-permute-start(f32[8,128]{1,0:T(8,128)S(1)} %get-tuple-element.45), channel_id=1, source_target_pairs={{0,1},{1,0},{2,3},{3,2},{4,5},{5,4},{6,7},{7,6},{8,9},{9,8},{10,11... | collective-permute-start | bytes 12296 | tf_op jit(solution)/shard_map/za1/ppermute | solution.py:524
  90.6 4.4 %collective-permute-start.13 = (f32[8,128]{1,0:T(8,128)S(1)}, f32[8,128]{1,0:T(8,128)S(1)}, u32[]{:S(2)}, u32[]{:S(2)}) collective-permute-start(f32[8,128]{1,0:T(8,128)S(1)} %get-tuple-element.46), channel_id=1, source_target_pairs={{1,2},{2,1},{5,6},{6,5},{9,10},{10,9},{13,14},{14,13},{17,18},{18,... | collective-permute-start | bytes 12296 | tf_op jit(solution)/shard_map/zb1/ppermute | solution.py:524
  96.0 12.8 %collective-permute-start.18 = (f32[4,8,128]{2,1,0:T(8,128)S(1)}, f32[4,8,128]{2,1,0:T(8,128)S(1)}, u32[]{:S(2)}, u32[]{:S(2)}) collective-permute-start(f32[4,8,128]{2,1,0:T(8,128)S(1)} %get-tuple-element.52), channel_id=1, source_target_pairs={{0,4},{4,0},{8,12},{12,8},{16,20},{20,16},{24,28},{28,24},{1,5},{5... | collective-permute-start | bytes 49160 | tf_op jit(solution)/shard_map/ya2/ppermute | solution.py:524
  99.2 9.6 %collective-permute-start.19 = (f32[4,8,128]{2,1,0:T(8,128)S(1)}, f32[4,8,128]{2,1,0:T(8,128)S(1)}, u32[]{:S(2)}, u32[]{:S(2)}) collective-permute-start(f32[4,8,128]{2,1,0:T(8,128)S(1)} %get-tuple-element.53), channel_id=1, source_target_pairs={{4,8},{8,4},{12,16},{16,12},{20,24},{24,20},{5,9},{9,5},{13,17},{1... | collective-permute-start | bytes 49160 | tf_op jit(solution)/shard_map/yb2/ppermute | solution.py:524
  102.2 4.7 %collective-permute-start.16 = (f32[8,128]{1,0:T(8,128)S(1)}, f32[8,128]{1,0:T(8,128)S(1)}, u32[]{:S(2)}, u32[]{:S(2)}) collective-permute-start(f32[8,128]{1,0:T(8,128)S(1)} %get-tuple-element.50), channel_id=1, source_target_pairs={{0,1},{1,0},{2,3},{3,2},{4,5},{5,4},{6,7},{7,6},{8,9},{9,8},{10,11... | collective-permute-start | bytes 12296 | tf_op jit(solution)/shard_map/za2/ppermute | solution.py:524
  104.1 4.7 %collective-permute-start.17 = (f32[8,128]{1,0:T(8,128)S(1)}, f32[8,128]{1,0:T(8,128)S(1)}, u32[]{:S(2)}, u32[]{:S(2)}) collective-permute-start(f32[8,128]{1,0:T(8,128)S(1)} %get-tuple-element.51), channel_id=1, source_target_pairs={{1,2},{2,1},{5,6},{6,5},{9,10},{10,9},{13,14},{14,13},{17,18},{18,... | collective-permute-start | bytes 12296 | tf_op jit(solution)/shard_map/zb2/ppermute | solution.py:524

commit v2 on v1

--- a/solution.py
+++ b/solution.py
@@ -343,25 +343,23 @@
     rims.finish(za, zb)
 
 
-class Planes:
-    def __init__(self, ya, yb, za, zb):
-        self.sub = lax.broadcasted_iota(jnp.int32, (8, 128), 0)
-        self.lane = lax.broadcasted_iota(jnp.int32, (8, 128), 1)
-        self.ya, self.yb, self.y_even = ya, yb, even("gy")
-        z_even = even("gz")
-        self.z_lo = jnp.where(z_even, zb[...], za[...])
-        self.z_hi = jnp.where(z_even, za[...], zb[...])
-
-    def beside(self, v, s, row, j):
-        a, b = self.ya[s, row : row + 1], self.yb[s, row : row + 1]
-        lo = jnp.broadcast_to(jnp.where(self.y_even, b, a), (8, 128))
-        hi = jnp.broadcast_to(jnp.where(self.y_even, a, b), (8, 128))
-        ym = jnp.where(self.sub == 0, lo, pltpu.roll(v, 1, 0))
-        yp = jnp.where(self.sub == 7, hi, pltpu.roll(v, 7, 0))
-        zl = pltpu.roll(self.z_lo, (128 - j) % 128, 1) if j else self.z_lo
-        zm = jnp.where(self.lane == 0, zl, pltpu.roll(v, 1, 1))
-        zp = jnp.where(self.lane == 127, pltpu.roll(self.z_hi, 127 - j, 1), pltpu.roll(v, 127, 1))
-        return ym, yp, zm, zp
+def beside(v, lo, hi, z_lo, z_hi, j):
+    sub = lax.broadcasted_iota(jnp.int32, (8, 128), 0)
+    lane = lax.broadcasted_iota(jnp.int32, (8, 128), 1)
+    ym = jnp.where(sub == 0, jnp.broadcast_to(lo, (8, 128)), pltpu.roll(v, 1, 0))
+    yp = jnp.where(sub == 7, jnp.broadcast_to(hi, (8, 128)), pltpu.roll(v, 7, 0))
+    return (ym, yp) + beside_z(v, z_lo, z_hi, j, j)
+
+
+def beside_z(v, z_lo, z_hi, j_lo, j_hi):
+    lane = lax.broadcasted_iota(jnp.int32, (8, 128), 1)
+    zm = jnp.where(lane == 0, turn(z_lo, -j_lo), pltpu.roll(v, 1, 1))
+    zp = jnp.where(lane == 127, turn(z_hi, 127 - j_hi), pltpu.roll(v, 127, 1))
+    return zm, zp
+
+
+def turn(v, n):
+    return pltpu.roll(v, n % 128, 1) if n % 128 else v
 
 
 def advance(s, cm, c, cp, around, spread, drift, upt, up1):
@@ -375,7 +373,7 @@
     return acc - upt * c / (HALF[s] + jnp.abs(c))
 
 
-def tissue(planes, lo, hi, get_c, get_coef, get_upt, me, store, rims=None, rim_lo=0, rim_hi=0):
+def tissue(lo, hi, get_c, around, get_coef, get_upt, me, store):
     for p in range(lo, hi):
         spread, drift = get_coef(p)
         upt = get_upt(p)
@@ -384,13 +382,10 @@
         up1 = upt * c1 / (HALF[1] + jnp.abs(c1))
         for s in range(4):
             c = get_c(s, p)
-            around = planes.beside(c, s, p - lo, s * (hi - lo) + p - lo)
-            v = advance(s, get_c(s, p - 1), c, get_c(s, p + 1), around, spread, drift, upt, up1)
+            v = advance(s, get_c(s, p - 1), c, get_c(s, p + 1), around(s, p, c), spread, drift, upt, up1)
             if keep is not None:
                 v = jnp.where(keep, v, 0.0)
             store(s, p, v)
-            if rim_lo <= p < rim_hi:
-                rims.put(v, s * (rim_hi - rim_lo) + p - rim_lo, s, p - rim_lo)
 
 
 def velocity_kernel(own_ref, slot_ref, recv, drift, blocks, slabs):
@@ -433,10 +428,21 @@
                 drift[2 * a + 1, 2 * r + h] = -jnp.minimum(u, 0.0)
 
 
+NEXT, COEF, FACE_ROWS = 64, 96, 176
+
+
 def tissue1_kernel(drift, conc, diff, upt, xl, xr, za, zb, ya, yb,
-                   c_out, spread_out, y0, y1, z0, z1):
+                   c_out, spread_out, ma, mb, pack_lo, pack_hi, coef_lo, coef_hi):
     me = lax.axis_index("gx")
-    planes = Planes(ya, yb, za, zb)
+    y_even, z_even = even("gy"), even("gz")
+    lane = lax.broadcasted_iota(jnp.int32, (8, 128), 1)
+    z_lo = jnp.where(z_even, zb[...], za[...])
+    z_hi = jnp.where(z_even, za[...], zb[...])
+    zero = jnp.zeros((8, 128), F32)
+    packs = [zero, zero]
+    coefs = [zero, zero]
+    ma[...] = jnp.zeros(ma.shape, F32)
+    mb[...] = jnp.zeros(mb.shape, F32)
 
     def field(f, own):
         def get(p):
@@ -451,51 +457,151 @@
     get_u = field(5, lambda p: upt[p])
     gets = [field(s, lambda p, s=s: conc[s, p]) for s in range(4)]
 
+    def around(s, p, c):
+        a, b = ya[s, p + 2 : p + 3], yb[s, p + 2 : p + 3]
+        lo, hi = jnp.where(y_even, b, a), jnp.where(y_even, a, b)
+        return beside(c, lo, hi, z_lo, z_hi, 12 * s + p + 2)
+
+    def put_rows(row, low, high):
+        ma[row : row + 1] = jnp.where(y_even, high, low)
+        mb[row : row + 1] = jnp.where(y_even, low, high)
+
+    def put_lanes(pair, j, value, depth):
+        at = lane == j
+        pair[0] = jnp.where(at, turn(value, j - depth), pair[0])
+        pair[1] = jnp.where(at, turn(value, j - 127 + depth), pair[1])
+
     def get_coef(p):
         d = get_d(p)
         q = p + 2
-        around = planes.beside(d, 4, q, 48 + q)
-        spread = [0.5 * (d + n) for n in (get_d(p - 1), get_d(p + 1)) + tuple(around)]
+        spread = [0.5 * (d + n) for n in (get_d(p - 1), get_d(p + 1)) + around(4, p, d)]
+        flow = [drift[n, q] for n in range(6)]
         for n in range(6):
             spread_out[n, q] = spread[n]
-        return spread, [drift[n, q] for n in range(6)]
+        if 0 <= p < 8:
+            fields = spread + [flow[2 * a] - flow[2 * a + 1] for a in range(3)] + [get_u(p)]
+            for n, v in enumerate(fields):
+                put_rows(COEF + 8 * n + p, v[0:1], v[7:8])
+                put_lanes(coefs, 8 * n + p, v, 0)
+        return spread, flow
 
     def store(s, p, v):
         c_out[s, p + 2] = v
-
-    rims = Rims(planes.lane, y0, y1)
-    tissue(planes, -2, 10, lambda s, p: gets[s](p), get_coef, get_u, me, store, rims, -1, 9)
-    rims.finish(z0, z1)
-
-
-def later_coef(spread, drift):
-    return lambda p: ([spread[n, p + 2] for n in range(6)], [drift[n, p + 2] for n in range(6)])
-
-
-def tissue2_kernel(drift, spread, conc, upt, xl, xr, za, zb, ya, yb, c_out, y0, y1, z0, z1):
+        if -1 <= p < 9:
+            put_rows(16 * s + p + 1, v[0:1], v[7:8])
+            put_lanes(packs, 10 * s + p + 1, v, 0)
+        if 0 <= p < 8:
+            put_rows(NEXT + 8 * s + p, v[1:2], v[6:7])
+            put_lanes(packs, 40 + 8 * s + p, v, 1)
+
+    tissue(-2, 10, lambda s, p: gets[s](p), around, get_coef, get_u, me, store)
+    pack_lo[...] = packs[0]
+    pack_hi[...] = packs[1]
+    coef_lo[...] = coefs[0]
+    coef_hi[...] = coefs[1]
+
+
+class Faces:
+    def __init__(self, a, b):
+        self.a, self.b, self.y_even = a, b, even("gy")
+
+    def rows(self, side, start, count):
+        a, b = self.a[start : start + count], self.b[start : start + count]
+        return jnp.where(self.y_even, b, a) if side == 0 else jnp.where(self.y_even, a, b)
+
+
+def corner_kernel(ya, yb, pack_lo, pack_hi, coef_lo, coef_hi, za, zb):
+    lane = lax.broadcasted_iota(jnp.int32, (8, 128), 1)
+    faces = Faces(ya, yb)
+    corners = [jnp.zeros((8, 128), F32)] * 2
+    for side in range(2):
+        for s in range(4):
+            v = faces.rows(side, 16 * s + 1, 8)
+            at = lane == 4 * side + s
+            corners[0] = jnp.where(at, turn(v, 4 * side + s), corners[0])
+            corners[1] = jnp.where(at, turn(v, 4 * side + s - 127), corners[1])
+    z_even = even("gz")
+    low = (pack_lo[...], coef_lo[...], corners[0])
+    high = (pack_hi[...], coef_hi[...], corners[1])
+    for n in range(3):
+        za[n] = jnp.where(z_even, high[n], low[n])
+        zb[n] = jnp.where(z_even, low[n], high[n])
+
+
+def tissue23_kernel(drift, spread, conc, upt, xl, xr, ya, yb, ma, mb, pack_lo, pack_hi, za, zb,
+                    out, mid, y_face):
     me = lax.axis_index("gx")
-    planes = Planes(ya, yb, za, zb)
+    sub = lax.broadcasted_iota(jnp.int32, (8, 128), 0)
+    lane = lax.broadcasted_iota(jnp.int32, (8, 128), 1)
+    got, sent = Faces(ya, yb), Faces(ma, mb)
+    z_even = even("gz")
+    low = [jnp.where(z_even, zb[n], za[n]) for n in range(3)]
+    high = [jnp.where(z_even, za[n], zb[n]) for n in range(3)]
+
+    def flows(u):
+        parts = []
+        for v in u:
+            parts += [jnp.maximum(v, 0.0), -jnp.minimum(v, 0.0)]
+        return parts
+
+    for side in range(2):
+        coef = [got.rows(side, COEF + 8 * n, 8) for n in range(10)]
+        cs = [got.rows(side, 16 * s + 1, 8) for s in range(4)]
+        up1 = coef[9] * cs[1] / (HALF[1] + jnp.abs(cs[1]))
+        for s in range(4):
+            inner = sent.rows(side, 16 * s + 1, 8)
+            outer = got.rows(side, NEXT + 8 * s, 8)
+            j = 4 * side + s
+            around = ((outer, inner) if side == 0 else (inner, outer)) + beside_z(cs[s], low[2], high[2], j, j)
+            y_face[side, s] = advance(
+                s, got.rows(side, 16 * s, 8), cs[s], got.rows(side, 16 * s + 2, 8), around,
+                coef[:6], flows(coef[6:9]), coef[9], up1,
+            )
+    z_face = []
+    for side, (pack, own) in enumerate(((low, pack_lo[...]), (high, pack_hi[...]))):
+        coef = [turn(pack[1], -8 * n) for n in range(10)]
+        flow = flows(coef[6:9])
+        cs = [turn(pack[0], -(10 * s + 1)) for s in range(4)]
+        up1 = coef[9] * cs[1] / (HALF[1] + jnp.abs(cs[1]))
+        for s in range(4):
+            edge = []
+            for y_side in range(2):
+                j = 4 * y_side + s
+                column = jnp.broadcast_to(pack[2][:, j : j + 1], (8, 128))
+                edge.append(jnp.sum(jnp.where(sub == lane, column, 0.0), axis=0, keepdims=True))
+            ym = jnp.where(sub == 0, jnp.broadcast_to(edge[0], (8, 128)), pltpu.roll(cs[s], 1, 0))
+            yp = jnp.where(sub == 7, jnp.broadcast_to(edge[1], (8, 128)), pltpu.roll(cs[s], 7, 0))
+            inner, outer = turn(own, -(10 * s + 1)), turn(pack[0], -(40 + 8 * s))
+            around = (ym, yp) + ((outer, inner) if side == 0 else (inner, outer))
+            z_face.append(advance(
+                s, turn(pack[0], -10 * s), cs[s], turn(pack[0], -(10 * s + 2)), around,
+                coef[:6], flow, coef[9], up1,
+            ))
 
     def get_u(p):
         return xl[slab(5, 3 + p)] if p < 0 else (xr[slab(5, p - 8)] if p > 7 else upt[p])
 
-    def store(s, p, v):
-        c_out[s, p + 1] = v
-
-    rims = Rims(planes.lane, y0, y1)
-    tissue(planes, -1, 9, lambda s, p: conc[s, p + 2], later_coef(spread, drift), get_u, me, store,
-           rims, 0, 8)
-    rims.finish(z0, z1)
-
-
-def tissue3_kernel(drift, spread, conc, upt, za, zb, ya, yb, out):
-    planes = Planes(ya, yb, za, zb)
-
-    def store(s, p, v):
+    def get_coef(p):
+        return [spread[n, p + 2] for n in range(6)], [drift[n, p + 2] for n in range(6)]
+
+    def around2(s, p, c):
+        q = p + 1
+        lo, hi = got.rows(0, 16 * s + q, 1), got.rows(1, 16 * s + q, 1)
+        return beside(c, lo, hi, low[0], high[0], 10 * s + q)
+
+    def store2(s, p, v):
+        mid[s, p + 1] = v
+
+    tissue(-1, 9, lambda s, p: conc[s, p + 2], around2, get_coef, get_u, me, store2)
+
+    def around3(s, p, c):
+        lo, hi = y_face[0, s, p : p + 1], y_face[1, s, p : p + 1]
+        return beside(c, lo, hi, z_face[s], z_face[4 + s], p)
+
+    def store3(s, p, v):
         out[s, p] = v
 
-    tissue(planes, 0, 8, lambda s, p: conc[s, p + 1], later_coef(spread, drift), lambda p: upt[p],
-           None, store)
+    tissue(0, 8, lambda s, p: mid[s, p + 1], around3, get_coef, get_u, me, store3)
 
 
 VMEM = pltpu.VMEM
@@ -569,16 +675,20 @@
             velocity_kernel, (owners, slots), (recv,), [((6, 12, 8, 128), F32)],
             [((17 * 16, 128), F32), ((6, 24, 128), F32)],
         )
-    c1, spread, *faces1 = call(
+    face = ((FACE_ROWS, 128), F32)
+    c1, spread, ma, mb, pack_lo, pack_hi, coef_lo, coef_hi = call(
         tissue1_kernel, (), (drift, conc, diff, upt, xl, xr) + rim,
-        [((4, 12, 8, 128), F32), ((6, 12, 8, 128), F32)] + faces(4, 16),
+        [((4, 12, 8, 128), F32), ((6, 12, 8, 128), F32), face, face] + [tile] * 4,
     )
-    c2, *faces2 = call(
-        tissue2_kernel, (), (drift, spread, c1, upt, xl, xr) + swaps(1, *faces1),
-        [((4, 10, 8, 128), F32)] + faces(4, 8),
+    ya, yb = swap(ma, "gy", True), swap(mb, "gy", False)
+    za, zb = call(
+        corner_kernel, (), (ya, yb, pack_lo, pack_hi, coef_lo, coef_hi), [tiles(3), tiles(3)]
     )
+    za, zb = swap(za, "gz", True), swap(zb, "gz", False)
     (out,) = call(
-        tissue3_kernel, (), (drift, spread, c2, upt) + swaps(2, *faces2), [((4, 8, 8, 128), F32)]
+        tissue23_kernel, (),
+        (drift, spread, c1, upt, xl, xr, ya, yb, ma, mb, pack_lo, pack_hi, za, zb),
+        [((4, 8, 8, 128), F32)], [((4, 10, 8, 128), F32), ((2, 4, 8, 128), F32)],
     )
     return weighted, out
 

time: 111 us -> 102 us (0.919)
  starting transfers between devices: 79.4 us -> 69.3 us
    ppermute x12 -> x8, starting transfers between devices: 37.5 us -> 27.5 us  [swap(): lax.ppermute(x, axis, [(i, j) for i in range(n) for j in [i ^ 1 if first...]
    ppermute x12 -> x8, waiting for transfers between devices: 6.9 us -> 7.33 us  [swap(): lax.ppermute(x, axis, [(i, j) for i in range(n) for j in [i ^ 1 if first...]
  transfers between devices with their start and end apart: 21 -> 17, of which waited for: 9 -> 8; matrix products, arithmetic and copies ran while one was open for 0% -> 0% of each run, Pallas kernels for 1% -> 1%
where the time goes in v2:
time: 102 us; the launch traced here: 100 us
  starting transfers between devices  69.3 us (68%)
  waiting for transfers between devices  15.9 us (16%)
  Pallas kernels  13.3 us (13%)
    ppermute x8, starting transfers between devices, swap(): lax.ppermute(x, axis, [(i, j) for i in range(n) for j in [i ^ 1 if first...  27.5 us
    ppermute x8, starting transfers between devices, hop(): lax.ppermute(x, axis, [(i, i + step) for i in range(n) if 0 <= i + step <...  23.1 us
    all_to_all x1, starting transfers between devices, shards(): recv = lax.all_to_all(send, 'gx', 0, 0)  18.7 us
    pallas_call x9, Pallas kernels, call(): pl.pallas_call(kernel, in_specs=[pl.BlockSpec(memory_space=pltpu.SMEM)] *...  13.3 us
    ppermute x8, waiting for transfers between devices, hop(): lax.ppermute(x, axis, [(i, i + step) for i in range(n) if 0 <= i + step <...  8.54 us
    ppermute x8, waiting for transfers between devices, swap(): lax.ppermute(x, axis, [(i, j) for i in range(n) for j in [i ^ 1 if first...  7.33 us
  transfers between devices with their start and end apart: 17, of which 8 were waited for; matrix products, arithmetic and copies ran while one was open for 0% of the time, Pallas kernels for 1%

profile of v2, /device:TPU:21, one launch (start us, length us, event | category | flops | bytes accessed | tf_op | source)
XLA Modules:
  0.0 100.5 jit_solution(573969118858363035)
XLA Ops:
  0.7 2.8 %first_kernel.1 = (f32[54,8,128]{2,1,0:T(8,128)}, f32[30,8,128]{2,1,0:T(8,128)}, f32[30,8,128]{2,1,0:T(8,128)}) custom-call(s32[1,4,18]{2,1,0:T(4,128)} %nbr_ref.9, f32[19,1,4,512]{3,2,1,0:T(4,128)} %pop_hbm.1, f32[1,4,512]{2,1,0:T(4,128)} %visc_hbm.1, s32[1,4,512]{2,1,0:T(4,128)} %link_hbm.1, s32[1,4,512]{2,1,0:T(4,128)} %flag_hbm.1, ...), custom_call_target="tpu_custom_call" | custom-call | tf_op jit(solution)/shard_map/first_kernel/pallas_call | solution.py:611
  3.5 3.5 %collective-permute-start = (f32[30,8,128]{2,1,0:T(8,128)}, f32[30,8,128]{2,1,0:T(8,128)S(1)}, u32[]{:S(2)}, u32[]{:S(2)}) collective-permute-start(f32[30,8,128]{2,1,0:T(8,128)} %get-tuple-element.28), channel_id=1, source_target_pairs={{0,32},{32,64},{64,96},{96,128},{128,160},{160,192},{192,224},{224... | collective-permute-start | bytes 368648 | tf_op jit(solution)/shard_map/ppermute | solution.py:625
  7.1 1.3 %collective-permute-start.1 = (f32[30,8,128]{2,1,0:T(8,128)}, f32[30,8,128]{2,1,0:T(8,128)S(1)}, u32[]{:S(2)}, u32[]{:S(2)}) collective-permute-start(f32[30,8,128]{2,1,0:T(8,128)} %get-tuple-element.29), channel_id=1, source_target_pairs={{32,0},{64,32},{96,64},{128,96},{160,128},{192,160},{224,192},{256... | collective-permute-start | bytes 368648 | tf_op jit(solution)/shard_map/ppermute | solution.py:625
  8.4 1.0 collective-permute-done.left_ref.xl
  9.4 4.1 %collective-permute-done.1.right_ref.xr = f32[30,8,128]{2,1,0:T(8,128)S(1)} collective-permute-done((f32[30,8,128]{2,1,0:T(8,128)}, f32[30,8,128]{2,1,0:T(8,128)S(1)}, u32[]{:S(2)}, u32[]{:S(2)}) %collective-permute-start.1) | collective-permute-done | bytes 122912 | tf_op jit(solution)/shard_map/ppermute | solution.py:625
  14.4 1.2 %second_kernel.1 = (f32[38,8,128]{2,1,0:T(8,128)S(1)}, f32[12,8,128]{2,1,0:T(8,128)S(1)}, f32[5,16,128]{2,1,0:T(8,128)S(1)}, f32[5,16,128]{2,1,0:T(8,128)S(1)}, ...) custom-call(s32[1,4,18]{2,1,0:T(4,128)S(1)} %copy-done.5, f32[54,8,128]{2,1,0:T(8,128)S(1)} %copy-done, ...), custom_call_target="tpu_custom_call" | custom-call | tf_op jit(solution)/shard_map/second_kernel/pallas_call | solution.py:611
  15.6 1.3 %collective-permute-start.3 = (f32[12,8,128]{2,1,0:T(8,128)S(1)}, f32[12,8,128]{2,1,0:T(8,128)S(1)}, u32[]{:S(2)}, u32[]{:S(2)}) collective-permute-start(f32[12,8,128]{2,1,0:T(8,128)S(1)} %get-tuple-element.31.unit_in), channel_id=1, source_target_pairs={{32,0},{64,32},{96,64},{128,96},{160,128},{192,160},{224,192},{256... | collective-permute-start | bytes 147464 | tf_op jit(solution)/shard_map/ppermute | solution.py:625
  16.9 4.2 %collective-permute-start.2 = (f32[12,8,128]{2,1,0:T(8,128)S(1)}, f32[12,8,128]{2,1,0:T(8,128)S(1)}, u32[]{:S(2)}, u32[]{:S(2)}) collective-permute-start(f32[12,8,128]{2,1,0:T(8,128)S(1)} %get-tuple-element.31.unit_in), channel_id=1, source_target_pairs={{0,32},{32,64},{64,96},{96,128},{128,160},{160,192},{192,224},{224... | collective-permute-start | bytes 147464 | tf_op jit(solution)/shard_map/ppermute | solution.py:625
  21.0 1.1 %collective-permute-done.2.left_ref = f32[12,8,128]{2,1,0:T(8,128)S(1)} collective-permute-done((f32[12,8,128]{2,1,0:T(8,128)S(1)}, f32[12,8,128]{2,1,0:T(8,128)S(1)}, u32[]{:S(2)}, u32[]{:S(2)}) %collective-permute-start.2) | collective-permute-done | bytes 49184 | tf_op jit(solution)/shard_map/ppermute | solution.py:625
  22.2 1.0 %step_kernel.2 = (f32[38,8,128]{2,1,0:T(8,128)S(1)}, f32[12,8,128]{2,1,0:T(8,128)S(1)}) custom-call(s32[1,4,18]{2,1,0:T(4,128)S(1)} %copy-done.5, f32[54,8,128]{2,1,0:T(8,128)S(1)} %copy-done.1, f32[38,8,128]{2,1,0:T(8,128)S(1)} %get-tuple-element.30.post_in, f32[12,8,128]{2,1,0:T(8,128)S(1)} %get-tuple-element.31.unit_in, ...), custom_call_target="tpu_custom_call" | custom-call | tf_op jit(solution)/shard_map/step_kernel/pallas_call | solution.py:611
  23.2 1.3 %collective-permute-start.5 = (f32[12,8,128]{2,1,0:T(8,128)S(1)}, f32[12,8,128]{2,1,0:T(8,128)S(1)}, u32[]{:S(2)}, u32[]{:S(2)}) collective-permute-start(f32[12,8,128]{2,1,0:T(8,128)S(1)} %get-tuple-element.33.unit_in), channel_id=1, source_target_pairs={{32,0},{64,32},{96,64},{128,96},{160,128},{192,160},{224,192},{256... | collective-permute-start | bytes 147464 | tf_op jit(solution)/shard_map/ppermute | solution.py:625
  24.5 5.5 %collective-permute-start.4 = (f32[12,8,128]{2,1,0:T(8,128)S(1)}, f32[12,8,128]{2,1,0:T(8,128)S(1)}, u32[]{:S(2)}, u32[]{:S(2)}) collective-permute-start(f32[12,8,128]{2,1,0:T(8,128)S(1)} %get-tuple-element.33.unit_in), channel_id=1, source_target_pairs={{0,32},{32,64},{64,96},{96,128},{128,160},{160,192},{192,224},{224... | collective-permute-start | bytes 147464 | tf_op jit(solution)/shard_map/ppermute | solution.py:625
  30.0 1.1 %collective-permute-done.4.left_ref = f32[12,8,128]{2,1,0:T(8,128)S(1)} collective-permute-done((f32[12,8,128]{2,1,0:T(8,128)S(1)}, f32[12,8,128]{2,1,0:T(8,128)S(1)}, u32[]{:S(2)}, u32[]{:S(2)}) %collective-permute-start.4) | collective-permute-done | bytes 49184 | tf_op jit(solution)/shard_map/ppermute | solution.py:625
  31.2 1.0 %step_kernel.3 = (f32[38,8,128]{2,1,0:T(8,128)S(1)}, f32[12,8,128]{2,1,0:T(8,128)S(1)}) custom-call(s32[1,4,18]{2,1,0:T(4,128)S(1)} %copy-done.5, f32[54,8,128]{2,1,0:T(8,128)S(1)} %copy-done.1, f32[38,8,128]{2,1,0:T(8,128)S(1)} %get-tuple-element.32.post_in, f32[12,8,128]{2,1,0:T(8,128)S(1)} %get-tuple-element.33.unit_in, ...), custom_call_target="tpu_custom_call" | custom-call | tf_op jit(solution)/shard_map/step_kernel/pallas_call | solution.py:611
  32.2 1.3 %collective-permute-start.7 = (f32[12,8,128]{2,1,0:T(8,128)S(1)}, f32[12,8,128]{2,1,0:T(8,128)S(1)}, u32[]{:S(2)}, u32[]{:S(2)}) collective-permute-start(f32[12,8,128]{2,1,0:T(8,128)S(1)} %get-tuple-element.35.unit_in), channel_id=1, source_target_pairs={{32,0},{64,32},{96,64},{128,96},{160,128},{192,160},{224,192},{256... | collective-permute-start | bytes 147464 | tf_op jit(solution)/shard_map/ppermute | solution.py:625
  33.5 4.7 %collective-permute-start.6 = (f32[12,8,128]{2,1,0:T(8,128)S(1)}, f32[12,8,128]{2,1,0:T(8,128)S(1)}, u32[]{:S(2)}, u32[]{:S(2)}) collective-permute-start(f32[12,8,128]{2,1,0:T(8,128)S(1)} %get-tuple-element.35.unit_in), channel_id=1, source_target_pairs={{0,32},{32,64},{64,96},{96,128},{128,160},{160,192},{192,224},{224... | collective-permute-start | bytes 147464 | tf_op jit(solution)/shard_map/ppermute | solution.py:625
  38.3 1.1 %collective-permute-done.6.left_ref = f32[12,8,128]{2,1,0:T(8,128)S(1)} collective-permute-done((f32[12,8,128]{2,1,0:T(8,128)S(1)}, f32[12,8,128]{2,1,0:T(8,128)S(1)}, u32[]{:S(2)}, u32[]{:S(2)}) %collective-permute-start.6) | collective-permute-done | bytes 49184 | tf_op jit(solution)/shard_map/ppermute | solution.py:625
  39.4 1.9 %last_kernel.1 = (f32[19,1,4,512]{3,2,1,0:T(4,128)}, f32[16,24,128]{2,1,0:T(8,128)}) custom-call(s32[1,4,18]{2,1,0:T(4,128)S(1)} %copy-done.5, s32[1,64]{1,0:T(1,128)S(1)} %copy-done.6, f32[54,8,128]{2,1,0:T(8,128)S(1)} %copy-done.1, f32[38,8,128]{2,1,0:T(8,128)S(1)} %get-tuple-element.34.post_in, f32[12,8,128]{2,1,0:T(8,128)S(1)} %get-tuple-element.35.unit_in, ...), custom_call_target="tpu_custom_call" | custom-call | tf_op jit(solution)/shard_map/last_kernel/pallas_call | solution.py:611
  41.3 18.7 %all-to-all-start = ((f32[16,24,128]{2,1,0:T(8,128)}), f32[16,24,128]{2,1,0:T(8,128)S(1)}, u32[]{:S(2)}, u32[]{:S(2)}) async-start(f32[16,24,128]{2,1,0:T(8,128)} %get-tuple-element.37), calls=%async_computation | async-start | bytes 393216 | tf_op jit(solution)/shard_map/spread/all_to_all | solution.py:672
  60.1 8.0 %collective-permute-start.10 = (f32[5,16,128]{2,1,0:T(8,128)S(1)}, f32[5,16,128]{2,1,0:T(8,128)S(1)}, u32[]{:S(2)}, u32[]{:S(2)}) collective-permute-start(f32[5,16,128]{2,1,0:T(8,128)S(1)} %get-tuple-element.40), channel_id=1, source_target_pairs={{0,4},{4,0},{8,12},{12,8},{16,20},{20,16},{24,28},{28,24},{1,5},{5... | collective-permute-start | bytes 122888 | tf_op jit(solution)/shard_map/ya0/ppermute | solution.py:630
  68.1 2.7 %collective-permute-start.11 = (f32[5,16,128]{2,1,0:T(8,128)S(1)}, f32[5,16,128]{2,1,0:T(8,128)S(1)}, u32[]{:S(2)}, u32[]{:S(2)}) collective-permute-start(f32[5,16,128]{2,1,0:T(8,128)S(1)} %get-tuple-element.41), channel_id=1, source_target_pairs={{4,8},{8,4},{12,16},{16,12},{20,24},{24,20},{5,9},{9,5},{13,17},{1... | collective-permute-start | bytes 122888 | tf_op jit(solution)/shard_map/yb0/ppermute | solution.py:630
  70.9 2.9 %collective-permute-start.8 = (f32[8,128]{1,0:T(8,128)S(1)}, f32[8,128]{1,0:T(8,128)S(1)}, u32[]{:S(2)}, u32[]{:S(2)}) collective-permute-start(f32[8,128]{1,0:T(8,128)S(1)} %get-tuple-element.38), channel_id=1, source_target_pairs={{0,1},{1,0},{2,3},{3,2},{4,5},{5,4},{6,7},{7,6},{8,9},{9,8},{10,11... | collective-permute-start | bytes 12296 | tf_op jit(solution)/shard_map/za0/ppermute | solution.py:630
  73.8 1.9 %collective-permute-start.9 = (f32[8,128]{1,0:T(8,128)S(1)}, f32[8,128]{1,0:T(8,128)S(1)}, u32[]{:S(2)}, u32[]{:S(2)}) collective-permute-start(f32[8,128]{1,0:T(8,128)S(1)} %get-tuple-element.39), channel_id=1, source_target_pairs={{1,2},{2,1},{5,6},{6,5},{9,10},{10,9},{13,14},{14,13},{17,18},{18,... | collective-permute-start | bytes 12296 | tf_op jit(solution)/shard_map/zb0/ppermute | solution.py:630
  76.7 1.7 %collective-permute-done.9.zb = f32[8,128]{1,0:T(8,128)S(1)} collective-permute-done((f32[8,128]{1,0:T(8,128)S(1)}, f32[8,128]{1,0:T(8,128)S(1)}, u32[]{:S(2)}, u32[]{:S(2)}) %collective-permute-start.9) | collective-permute-done | bytes 4128 | tf_op jit(solution)/shard_map/zb0/ppermute | solution.py:630
  78.5 3.0 %tissue1_kernel.1 = (f32[4,12,8,128]{3,2,1,0:T(8,128)S(1)}, f32[6,12,8,128]{3,2,1,0:T(8,128)S(1)}, f32[176,128]{1,0:T(8,128)S(1)}, f32[176,128]{1,0:T(8,128)S(1)...) custom-call(f32[6,12,8,128]{3,2,1,0:T(8,128)S(1)} %velocity_kernel.1.drift, ...), custom_call_target="tpu_custom_call" | custom-call | tf_op jit(solution)/shard_map/tissue1_kernel/pallas_call | solution.py:611
  81.5 4.4 %collective-permute-start.12 = (f32[176,128]{1,0:T(8,128)S(1)}, f32[176,128]{1,0:T(8,128)S(1)}, u32[]{:S(2)}, u32[]{:S(2)}) collective-permute-start(f32[176,128]{1,0:T(8,128)S(1)} %get-tuple-element.44.ma), channel_id=1, source_target_pairs={{0,4},{4,0},{8,12},{12,8},{16,20},{20,16},{24,28},{28,24},{1,5},{5... | collective-permute-start | bytes 270344 | tf_op jit(solution)/shard_map/ppermute | solution.py:630
  85.9 2.7 %collective-permute-start.13 = (f32[176,128]{1,0:T(8,128)S(1)}, f32[176,128]{1,0:T(8,128)S(1)}, u32[]{:S(2)}, u32[]{:S(2)}) collective-permute-start(f32[176,128]{1,0:T(8,128)S(1)} %get-tuple-element.45.mb), channel_id=1, source_target_pairs={{4,8},{8,4},{12,16},{16,12},{20,24},{24,20},{5,9},{9,5},{13,17},{1... | collective-permute-start | bytes 270344 | tf_op jit(solution)/shard_map/ppermute | solution.py:630
  88.6 3.1 %collective-permute-done.13.yb = f32[176,128]{1,0:T(8,128)S(1)} collective-permute-done((f32[176,128]{1,0:T(8,128)S(1)}, f32[176,128]{1,0:T(8,128)S(1)}, u32[]{:S(2)}, u32[]{:S(2)}) %collective-permute-start.13) | collective-permute-done | bytes 90144 | tf_op jit(solution)/shard_map/ppermute | solution.py:630
  91.8 2.9 %collective-permute-start.14 = (f32[3,8,128]{2,1,0:T(8,128)S(1)}, f32[3,8,128]{2,1,0:T(8,128)S(1)}, u32[]{:S(2)}, u32[]{:S(2)}) collective-permute-start(f32[3,8,128]{2,1,0:T(8,128)S(1)} %get-tuple-element.50), channel_id=1, source_target_pairs={{0,1},{1,0},{2,3},{3,2},{4,5},{5,4},{6,7},{7,6},{8,9},{9,8},{10,11... | collective-permute-start | bytes 36872 | tf_op jit(solution)/shard_map/ppermute | solution.py:630
  94.7 1.9 %collective-permute-start.15 = (f32[3,8,128]{2,1,0:T(8,128)S(1)}, f32[3,8,128]{2,1,0:T(8,128)S(1)}, u32[]{:S(2)}, u32[]{:S(2)}) collective-permute-start(f32[3,8,128]{2,1,0:T(8,128)S(1)} %get-tuple-element.51), channel_id=1, source_target_pairs={{1,2},{2,1},{5,6},{6,5},{9,10},{10,9},{13,14},{14,13},{17,18},{18,... | collective-permute-start | bytes 36872 | tf_op jit(solution)/shard_map/ppermute | solution.py:630
  96.7 2.5 %collective-permute-done.15.zb = f32[3,8,128]{2,1,0:T(8,128)S(1)} collective-permute-done((f32[3,8,128]{2,1,0:T(8,128)S(1)}, f32[3,8,128]{2,1,0:T(8,128)S(1)}, u32[]{:S(2)}, u32[]{:S(2)}) %collective-permute-start.15) | collective-permute-done | bytes 12320 | tf_op jit(solution)/shard_map/ppermute | solution.py:630
  99.2 1.3 %tissue23_kernel.1 = f32[4,8,8,128]{3,2,1,0:T(8,128)} custom-call(f32[6,12,8,128]{3,2,1,0:T(8,128)S(1)} %velocity_kernel.1.drift, f32[6,12,8,128]{3,2,1,0:T(8,128)S(1)} %get-tuple-element.42.spread, f32[4,12,8,128]{3,2,1,0:T(8,128)S(1)} %get-tuple-element.43.conc, f32[8,8,128]{2,1,0:T(8,128)S(1)} %copy-done.4, ...), custom_call_target="tpu_custom_call" | custom-call | tf_op jit(solution)/shard_map/tissue23_kernel/pallas_call | solution.py:611
  (27 shorter events, 2.0 us)
Async XLA Ops:
  0.6 12.8 %copy-start.3 = (f32[8,8,128]{2,1,0:T(8,128)S(1)}, f32[8,8,128]{2,1,0:T(8,128)}, u32[]{:S(2)}) copy-start(f32[8,8,128]{2,1,0:T(8,128)} %diff.3) | copy-start | bytes 98308
  0.6 12.8 %copy-start.2 = (f32[4,8,8,128]{3,2,1,0:T(8,128)S(1)}, f32[4,8,8,128]{3,2,1,0:T(8,128)}, u32[]{:S(2)}) copy-start(f32[4,8,8,128]{3,2,1,0:T(8,128)} %conc.3) | copy-start | bytes 393220
  3.5 10.0 %copy-start.5 = (s32[1,4,18]{2,1,0:T(4,128)S(1)}, s32[1,4,18]{2,1,0:T(4,128)}, u32[]{:S(2)}) copy-start(s32[1,4,18]{2,1,0:T(4,128)} %nbr_ref.9) | copy-start | bytes 868
  3.5 5.9 %collective-permute-start = (f32[30,8,128]{2,1,0:T(8,128)}, f32[30,8,128]{2,1,0:T(8,128)S(1)}, u32[]{:S(2)}, u32[]{:S(2)}) collective-permute-start(f32[30,8,128]{2,1,0:T(8,128)} %get-tuple-element.28), channel_id=1, source_target_pairs={{0,32},{32,64},{64,96},{96,128},{128,160},{160,192},{192,224},{224... | collective-permute-start | bytes 368648 | tf_op jit(solution)/shard_map/ppermute | solution.py:625
  7.1 6.4 %collective-permute-start.1 = (f32[30,8,128]{2,1,0:T(8,128)}, f32[30,8,128]{2,1,0:T(8,128)S(1)}, u32[]{:S(2)}, u32[]{:S(2)}) collective-permute-start(f32[30,8,128]{2,1,0:T(8,128)} %get-tuple-element.29), channel_id=1, source_target_pairs={{32,0},{64,32},{96,64},{128,96},{160,128},{192,160},{224,192},{256... | collective-permute-start | bytes 368648 | tf_op jit(solution)/shard_map/ppermute | solution.py:625
  13.5 0.9 copy-start
  14.4 7.8 %copy-start.1 = (f32[54,8,128]{2,1,0:T(8,128)S(1)}, f32[54,8,128]{2,1,0:T(8,128)}, u32[]{:S(2)}) copy-start(f32[54,8,128]{2,1,0:T(8,128)} %get-tuple-element.27.state) | copy-start | bytes 663556
  15.6 5.5 %collective-permute-start.3 = (f32[12,8,128]{2,1,0:T(8,128)S(1)}, f32[12,8,128]{2,1,0:T(8,128)S(1)}, u32[]{:S(2)}, u32[]{:S(2)}) collective-permute-start(f32[12,8,128]{2,1,0:T(8,128)S(1)} %get-tuple-element.31.unit_in), channel_id=1, source_target_pairs={{32,0},{64,32},{96,64},{128,96},{160,128},{192,160},{224,192},{256... | collective-permute-start | bytes 147464 | tf_op jit(solution)/shard_map/ppermute | solution.py:625
  16.9 5.3 %collective-permute-start.2 = (f32[12,8,128]{2,1,0:T(8,128)S(1)}, f32[12,8,128]{2,1,0:T(8,128)S(1)}, u32[]{:S(2)}, u32[]{:S(2)}) collective-permute-start(f32[12,8,128]{2,1,0:T(8,128)S(1)} %get-tuple-element.31.unit_in), channel_id=1, source_target_pairs={{0,32},{32,64},{64,96},{96,128},{128,160},{160,192},{192,224},{224... | collective-permute-start | bytes 147464 | tf_op jit(solution)/shard_map/ppermute | solution.py:625
  23.2 6.8 %collective-permute-start.5 = (f32[12,8,128]{2,1,0:T(8,128)S(1)}, f32[12,8,128]{2,1,0:T(8,128)S(1)}, u32[]{:S(2)}, u32[]{:S(2)}) collective-permute-start(f32[12,8,128]{2,1,0:T(8,128)S(1)} %get-tuple-element.33.unit_in), channel_id=1, source_target_pairs={{32,0},{64,32},{96,64},{128,96},{160,128},{192,160},{224,192},{256... | collective-permute-start | bytes 147464 | tf_op jit(solution)/shard_map/ppermute | solution.py:625
  24.5 6.6 %collective-permute-start.4 = (f32[12,8,128]{2,1,0:T(8,128)S(1)}, f32[12,8,128]{2,1,0:T(8,128)S(1)}, u32[]{:S(2)}, u32[]{:S(2)}) collective-permute-start(f32[12,8,128]{2,1,0:T(8,128)S(1)} %get-tuple-element.33.unit_in), channel_id=1, source_target_pairs={{0,32},{32,64},{64,96},{96,128},{128,160},{160,192},{192,224},{224... | collective-permute-start | bytes 147464 | tf_op jit(solution)/shard_map/ppermute | solution.py:625
  32.2 7.2 %copy-start.6 = (s32[1,64]{1,0:T(1,128)S(1)}, s32[1,64]{1,0:T(1,128)}, u32[]{:S(2)}) copy-start(s32[1,64]{1,0:T(1,128)} %own_ref.3) | copy-start | bytes 772
  32.2 6.0 %collective-permute-start.7 = (f32[12,8,128]{2,1,0:T(8,128)S(1)}, f32[12,8,128]{2,1,0:T(8,128)S(1)}, u32[]{:S(2)}, u32[]{:S(2)}) collective-permute-start(f32[12,8,128]{2,1,0:T(8,128)S(1)} %get-tuple-element.35.unit_in), channel_id=1, source_target_pairs={{32,0},{64,32},{96,64},{128,96},{160,128},{192,160},{224,192},{256... | collective-permute-start | bytes 147464 | tf_op jit(solution)/shard_map/ppermute | solution.py:625
  33.5 5.9 %collective-permute-start.6 = (f32[12,8,128]{2,1,0:T(8,128)S(1)}, f32[12,8,128]{2,1,0:T(8,128)S(1)}, u32[]{:S(2)}, u32[]{:S(2)}) collective-permute-start(f32[12,8,128]{2,1,0:T(8,128)S(1)} %get-tuple-element.35.unit_in), channel_id=1, source_target_pairs={{0,32},{32,64},{64,96},{96,128},{128,160},{160,192},{192,224},{224... | collective-permute-start | bytes 147464 | tf_op jit(solution)/shard_map/ppermute | solution.py:625
  41.3 34.4 %all-to-all-start = ((f32[16,24,128]{2,1,0:T(8,128)}), f32[16,24,128]{2,1,0:T(8,128)S(1)}, u32[]{:S(2)}, u32[]{:S(2)}) async-start(f32[16,24,128]{2,1,0:T(8,128)} %get-tuple-element.37), calls=%async_computation | async-start | bytes 393216 | tf_op jit(solution)/shard_map/spread/all_to_all | solution.py:672
  60.1 18.4 %collective-permute-start.10 = (f32[5,16,128]{2,1,0:T(8,128)S(1)}, f32[5,16,128]{2,1,0:T(8,128)S(1)}, u32[]{:S(2)}, u32[]{:S(2)}) collective-permute-start(f32[5,16,128]{2,1,0:T(8,128)S(1)} %get-tuple-element.40), channel_id=1, source_target_pairs={{0,4},{4,0},{8,12},{12,8},{16,20},{20,16},{24,28},{28,24},{1,5},{5... | collective-permute-start | bytes 122888 | tf_op jit(solution)/shard_map/ya0/ppermute | solution.py:630
  68.1 10.3 %collective-permute-start.11 = (f32[5,16,128]{2,1,0:T(8,128)S(1)}, f32[5,16,128]{2,1,0:T(8,128)S(1)}, u32[]{:S(2)}, u32[]{:S(2)}) collective-permute-start(f32[5,16,128]{2,1,0:T(8,128)S(1)} %get-tuple-element.41), channel_id=1, source_target_pairs={{4,8},{8,4},{12,16},{16,12},{20,24},{24,20},{5,9},{9,5},{13,17},{1... | collective-permute-start | bytes 122888 | tf_op jit(solution)/shard_map/yb0/ppermute | solution.py:630
  70.9 4.9 %copy-start.7 = (s32[1,64]{1,0:T(1,128)S(1)}, s32[1,64]{1,0:T(1,128)}, u32[]{:S(2)}) copy-start(s32[1,64]{1,0:T(1,128)} %slot_ref.1) | copy-start | bytes 772
  70.9 5.9 %collective-permute-start.8 = (f32[8,128]{1,0:T(8,128)S(1)}, f32[8,128]{1,0:T(8,128)S(1)}, u32[]{:S(2)}, u32[]{:S(2)}) collective-permute-start(f32[8,128]{1,0:T(8,128)S(1)} %get-tuple-element.38), channel_id=1, source_target_pairs={{0,1},{1,0},{2,3},{3,2},{4,5},{5,4},{6,7},{7,6},{8,9},{9,8},{10,11... | collective-permute-start | bytes 12296 | tf_op jit(solution)/shard_map/za0/ppermute | solution.py:630
  73.8 4.7 %copy-start.4 = (f32[8,8,128]{2,1,0:T(8,128)S(1)}, f32[8,8,128]{2,1,0:T(8,128)}, u32[]{:S(2)}) copy-start(f32[8,8,128]{2,1,0:T(8,128)} %upt.3) | copy-start | bytes 98308
  73.8 4.6 %collective-permute-start.9 = (f32[8,128]{1,0:T(8,128)S(1)}, f32[8,128]{1,0:T(8,128)S(1)}, u32[]{:S(2)}, u32[]{:S(2)}) collective-permute-start(f32[8,128]{1,0:T(8,128)S(1)} %get-tuple-element.39), channel_id=1, source_target_pairs={{1,2},{2,1},{5,6},{6,5},{9,10},{10,9},{13,14},{14,13},{17,18},{18,... | collective-permute-start | bytes 12296 | tf_op jit(solution)/shard_map/zb0/ppermute | solution.py:630
  81.5 7.1 %collective-permute-start.12 = (f32[176,128]{1,0:T(8,128)S(1)}, f32[176,128]{1,0:T(8,128)S(1)}, u32[]{:S(2)}, u32[]{:S(2)}) collective-permute-start(f32[176,128]{1,0:T(8,128)S(1)} %get-tuple-element.44.ma), channel_id=1, source_target_pairs={{0,4},{4,0},{8,12},{12,8},{16,20},{20,16},{24,28},{28,24},{1,5},{5... | collective-permute-start | bytes 270344 | tf_op jit(solution)/shard_map/ppermute | solution.py:630
  85.9 5.8 %collective-permute-start.13 = (f32[176,128]{1,0:T(8,128)S(1)}, f32[176,128]{1,0:T(8,128)S(1)}, u32[]{:S(2)}, u32[]{:S(2)}) collective-permute-start(f32[176,128]{1,0:T(8,128)S(1)} %get-tuple-element.45.mb), channel_id=1, source_target_pairs={{4,8},{8,4},{12,16},{16,12},{20,24},{24,20},{5,9},{9,5},{13,17},{1... | collective-permute-start | bytes 270344 | tf_op jit(solution)/shard_map/ppermute | solution.py:630
  91.8 4.8 %collective-permute-start.14 = (f32[3,8,128]{2,1,0:T(8,128)S(1)}, f32[3,8,128]{2,1,0:T(8,128)S(1)}, u32[]{:S(2)}, u32[]{:S(2)}) collective-permute-start(f32[3,8,128]{2,1,0:T(8,128)S(1)} %get-tuple-element.50), channel_id=1, source_target_pairs={{0,1},{1,0},{2,3},{3,2},{4,5},{5,4},{6,7},{7,6},{8,9},{9,8},{10,11... | collective-permute-start | bytes 36872 | tf_op jit(solution)/shard_map/ppermute | solution.py:630
  94.7 4.4 %collective-permute-start.15 = (f32[3,8,128]{2,1,0:T(8,128)S(1)}, f32[3,8,128]{2,1,0:T(8,128)S(1)}, u32[]{:S(2)}, u32[]{:S(2)}) collective-permute-start(f32[3,8,128]{2,1,0:T(8,128)S(1)} %get-tuple-element.51), channel_id=1, source_target_pairs={{1,2},{2,1},{5,6},{6,5},{9,10},{10,9},{13,14},{14,13},{17,18},{18,... | collective-permute-start | bytes 36872 | tf_op jit(solution)/shard_map/ppermute | solution.py:630

commit v3 on v2

--- a/solution.py
+++ b/solution.py
@@ -5,6 +5,7 @@
 from jax.experimental import pallas as pl
 from jax.experimental.pallas import tpu as pltpu
 from jax.sharding import PartitionSpec as P
+
 
 FLOW_STEPS = 4
 DIRS = (
@@ -183,7 +184,7 @@
     return [jnp.where(edge, feq[i], f[i]) for i in range(19)]
 
 
-def to_rows(dst, value, b_rows=4):
+def to_rows(dst, value):
     for r in range(4):
         dst[pl.ds(r, 4, stride=4), :] = value[:, 128 * r : 128 * r + 128]
 
@@ -268,12 +269,12 @@
     first_rims(conc, diff, left_ref, right_ref, ya, yb, za, zb)
 
 
-def last_kernel(nbr_ref, own_ref, state, post_in, unit_in, left_ref, right_ref, out_ref, send_ref, pool, got, rows, jrows):
+def last_kernel(nbr_ref, own_ref, slot_ref, state, post_in, unit_in, left_ref, right_ref, f_ref, send_ref, pool, got, jrows):
     sites = Sites()
     me = lax.axis_index("gx")
     f = stream(sites, me, nbr_ref, post_in, unit_in, left_ref, right_ref, state, pool, got)
     for i in range(19):
-        rows[i] = (f[i] * np.float32(1.0 / WEIGHT[i])).reshape(16, 128)
+        f_ref[i] = f[i].reshape(16, 128)
     j = moments(f)
     for a in range(3):
         v = j[a]
@@ -286,21 +287,27 @@
     for b in range(4):
         o = own_ref[0, 4 * me + b]
         for a in range(3):
-            send_ref[o, 4 * a : 4 * a + 4] = jrows[a, 4 * b : 4 * b + 4]
+            for r in range(4):
+                send_ref[o, 2 * a + r // 2, r % 2 : r % 2 + 1] = jrows[a, 4 * b + r : 4 * b + r + 1]
 
         @pl.when(o < 15)
         def _():
             for a in range(3):
-                send_ref[o + 1, 12 + a : 13 + a] = jrows[a, 4 * b + 3 : 4 * b + 4]
+                k = 12 + a
+                send_ref[o + 1, k // 2, k % 2 : k % 2 + 1] = jrows[a, 4 * b + 3 : 4 * b + 4]
 
         @pl.when(o > 0)
         def _():
             for a in range(3):
-                send_ref[o - 1, 15 + a : 16 + a] = jrows[a, 4 * b : 4 * b + 1]
-
+                k = 15 + a
+                send_ref[o - 1, k // 2, k % 2 : k % 2 + 1] = jrows[a, 4 * b : 4 * b + 1]
+
+
+def weighted_kernel(f_ref, out_ref):
     for i in range(19):
         for r in range(4):
-            out_ref[i, 0, :, 128 * r : 128 * r + 128] = rows[i, pl.ds(r, 4, stride=4), :]
+            rows = f_ref[i, pl.ds(r, 4, stride=4), :]
+            out_ref[i, 0, :, 128 * r : 128 * r + 128] = rows * np.float32(1.0 / WEIGHT[i])
 
 
 def even(axis):
@@ -388,7 +395,7 @@
             store(s, p, v)
 
 
-def velocity_kernel(own_ref, slot_ref, recv, drift, blocks, slabs):
+def place_velocity(own_ref, slot_ref, recv, drift, blocks, slabs):
     me = lax.axis_index("gx")
     blocks[...] = jnp.zeros(blocks.shape, F32)
     slabs[...] = jnp.zeros(slabs.shape, F32)
@@ -400,10 +407,12 @@
             own = jnp.where(o == me, at, own)
             low = jnp.where(o == me - 1, at, low)
             high = jnp.where(o == me + 1, at, high)
-        blocks[pl.ds(pl.multiple_of(16 * own, 16), 16), :] = recv[m, 0:16]
-        for a in range(3):
-            slabs[a, pl.ds(low, 1), :] = recv[m, 12 + a : 13 + a]
-            slabs[3 + a, pl.ds(high, 1), :] = recv[m, 15 + a : 16 + a]
+        for k in range(18):
+            row = recv[m, k // 2, k % 2 : k % 2 + 1]
+            if k < 12:
+                blocks[pl.ds(16 * own + k, 1), :] = row
+            else:
+                slabs[k - 12, pl.ds(low if k < 15 else high, 1), :] = row
     group = lax.broadcasted_iota(jnp.int32, (16, 128), 1) >> 3
     masks = [(group & (1 << bit)) != 0 for bit in range(4)]
 
@@ -431,70 +440,106 @@
 NEXT, COEF, FACE_ROWS = 64, 96, 176
 
 
-def tissue1_kernel(drift, conc, diff, upt, xl, xr, za, zb, ya, yb,
-                   c_out, spread_out, ma, mb, pack_lo, pack_hi, coef_lo, coef_hi):
-    me = lax.axis_index("gx")
+def brick_field(xl, xr, f, own):
+    def get(p):
+        if p < 0:
+            return xl[slab(f, 3 + p)]
+        if p > 7:
+            return xr[slab(f, p - 8)]
+        return own(p)
+
+    return get
+
+
+def first_around(za, zb, ya, yb):
     y_even, z_even = even("gy"), even("gz")
-    lane = lax.broadcasted_iota(jnp.int32, (8, 128), 1)
     z_lo = jnp.where(z_even, zb[...], za[...])
     z_hi = jnp.where(z_even, za[...], zb[...])
-    zero = jnp.zeros((8, 128), F32)
-    packs = [zero, zero]
-    coefs = [zero, zero]
-    ma[...] = jnp.zeros(ma.shape, F32)
-    mb[...] = jnp.zeros(mb.shape, F32)
-
-    def field(f, own):
-        def get(p):
-            if p < 0:
-                return xl[slab(f, 3 + p)]
-            if p > 7:
-                return xr[slab(f, p - 8)]
-            return own(p)
-        return get
-
-    get_d = field(4, lambda p: diff[p])
-    get_u = field(5, lambda p: upt[p])
-    gets = [field(s, lambda p, s=s: conc[s, p]) for s in range(4)]
 
     def around(s, p, c):
         a, b = ya[s, p + 2 : p + 3], yb[s, p + 2 : p + 3]
         lo, hi = jnp.where(y_even, b, a), jnp.where(y_even, a, b)
         return beside(c, lo, hi, z_lo, z_hi, 12 * s + p + 2)
 
-    def put_rows(row, low, high):
-        ma[row : row + 1] = jnp.where(y_even, high, low)
-        mb[row : row + 1] = jnp.where(y_even, low, high)
-
-    def put_lanes(pair, j, value, depth):
-        at = lane == j
-        pair[0] = jnp.where(at, turn(value, j - depth), pair[0])
-        pair[1] = jnp.where(at, turn(value, j - 127 + depth), pair[1])
-
-    def get_coef(p):
-        d = get_d(p)
-        q = p + 2
+    return around
+
+
+def put_rows(ma, mb, y_even, row, low, high):
+    ma[row : row + 1] = jnp.where(y_even, high, low)
+    mb[row : row + 1] = jnp.where(y_even, low, high)
+
+
+def put_lanes(pair, j, value, depth):
+    at = lax.broadcasted_iota(jnp.int32, (8, 128), 1) == j
+    pair[0] = jnp.where(at, turn(value, j - depth), pair[0])
+    pair[1] = jnp.where(at, turn(value, j - 127 + depth), pair[1])
+
+
+def spread_kernel(conc, diff, upt, xl, xr, za, zb, ya, yb, part, spread_out, ca, cb, coef_lo, coef_hi):
+    y_even = even("gy")
+    around = first_around(za, zb, ya, yb)
+    coefs = [jnp.zeros((8, 128), F32)] * 2
+    get_d = brick_field(xl, xr, 4, lambda p: diff[p])
+    get_u = brick_field(xl, xr, 5, lambda p: upt[p])
+    gets = [brick_field(xl, xr, s, lambda p, s=s: conc[s, p]) for s in range(4)]
+    for p in range(-2, 10):
+        d, u = get_d(p), get_u(p)
         spread = [0.5 * (d + n) for n in (get_d(p - 1), get_d(p + 1)) + around(4, p, d)]
-        flow = [drift[n, q] for n in range(6)]
         for n in range(6):
-            spread_out[n, q] = spread[n]
+            spread_out[n, p + 2] = spread[n]
         if 0 <= p < 8:
-            fields = spread + [flow[2 * a] - flow[2 * a + 1] for a in range(3)] + [get_u(p)]
-            for n, v in enumerate(fields):
-                put_rows(COEF + 8 * n + p, v[0:1], v[7:8])
+            for n, v in enumerate(spread + [u]):
+                put_rows(ca, cb, y_even, 8 * n + p, v[0:1], v[7:8])
                 put_lanes(coefs, 8 * n + p, v, 0)
-        return spread, flow
-
-    def store(s, p, v):
-        c_out[s, p + 2] = v
-        if -1 <= p < 9:
-            put_rows(16 * s + p + 1, v[0:1], v[7:8])
-            put_lanes(packs, 10 * s + p + 1, v, 0)
+        c1 = gets[1](p)
+        up1 = u * c1 / (HALF[1] + jnp.abs(c1))
+        for s in range(4):
+            c = gets[s](p)
+            total = None
+            for g, v in zip(spread, (gets[s](p - 1), gets[s](p + 1)) + around(s, p, c)):
+                t = g * (v - c)
+                total = t if total is None else total + t
+            v = c + GAIN[s] * total
+            part[s, p + 2] = v + 2.0 * up1 if s == 2 else v - u * c / (HALF[s] + jnp.abs(c))
+    coef_lo[...] = coefs[0]
+    coef_hi[...] = coefs[1]
+
+
+def drift_kernel(own_ref, slot_ref, recv, part, conc, xl, xr, za, zb, ya, yb, ca, cb, coef_lo_in, coef_hi_in,
+                 drift, c_out, ma, mb, pack_lo, pack_hi, coef_lo, coef_hi, blocks, slabs):
+    me = lax.axis_index("gx")
+    y_even = even("gy")
+    place_velocity(own_ref, slot_ref, recv, drift, blocks, slabs)
+    around = first_around(za, zb, ya, yb)
+    gets = [brick_field(xl, xr, s, lambda p, s=s: conc[s, p]) for s in range(4)]
+    packs = [jnp.zeros((8, 128), F32)] * 2
+    coefs = [coef_lo_in[...], coef_hi_in[...]]
+    ma[0:COEF] = jnp.zeros((COEF, 128), F32)
+    mb[0:COEF] = jnp.zeros((COEF, 128), F32)
+    ma[COEF : COEF + 56] = ca[...]
+    mb[COEF : COEF + 56] = cb[...]
+    for p in range(-2, 10):
+        flow = [drift[n, p + 2] for n in range(6)]
         if 0 <= p < 8:
-            put_rows(NEXT + 8 * s + p, v[1:2], v[6:7])
-            put_lanes(packs, 40 + 8 * s + p, v, 1)
-
-    tissue(-2, 10, lambda s, p: gets[s](p), around, get_coef, get_u, me, store)
+            for a in range(3):
+                v = flow[2 * a] - flow[2 * a + 1]
+                put_rows(ma, mb, y_even, COEF + 8 * (7 + a) + p, v[0:1], v[7:8])
+                put_lanes(coefs, 8 * (7 + a) + p, v, 0)
+        keep = me > 0 if p < 0 else (me < 15 if p > 7 else None)
+        for s in range(4):
+            c = gets[s](p)
+            v = part[s, p + 2]
+            for d, n in zip(flow, (gets[s](p - 1), gets[s](p + 1)) + around(s, p, c)):
+                v = v + d * (n - c)
+            if keep is not None:
+                v = jnp.where(keep, v, 0.0)
+            c_out[s, p + 2] = v
+            if -1 <= p < 9:
+                put_rows(ma, mb, y_even, 16 * s + p + 1, v[0:1], v[7:8])
+                put_lanes(packs, 10 * s + p + 1, v, 0)
+            if 0 <= p < 8:
+                put_rows(ma, mb, y_even, NEXT + 8 * s + p, v[1:2], v[6:7])
+                put_lanes(packs, 40 + 8 * s + p, v, 1)
     pack_lo[...] = packs[0]
     pack_hi[...] = packs[1]
     coef_lo[...] = coefs[0]
@@ -547,7 +592,7 @@
     for side in range(2):
         coef = [got.rows(side, COEF + 8 * n, 8) for n in range(10)]
         cs = [got.rows(side, 16 * s + 1, 8) for s in range(4)]
-        up1 = coef[9] * cs[1] / (HALF[1] + jnp.abs(cs[1]))
+        up1 = coef[6] * cs[1] / (HALF[1] + jnp.abs(cs[1]))
         for s in range(4):
             inner = sent.rows(side, 16 * s + 1, 8)
             outer = got.rows(side, NEXT + 8 * s, 8)
@@ -555,14 +600,14 @@
             around = ((outer, inner) if side == 0 else (inner, outer)) + beside_z(cs[s], low[2], high[2], j, j)
             y_face[side, s] = advance(
                 s, got.rows(side, 16 * s, 8), cs[s], got.rows(side, 16 * s + 2, 8), around,
-                coef[:6], flows(coef[6:9]), coef[9], up1,
+                coef[:6], flows(coef[7:10]), coef[6], up1,
             )
     z_face = []
     for side, (pack, own) in enumerate(((low, pack_lo[...]), (high, pack_hi[...]))):
         coef = [turn(pack[1], -8 * n) for n in range(10)]
-        flow = flows(coef[6:9])
+        flow = flows(coef[7:10])
         cs = [turn(pack[0], -(10 * s + 1)) for s in range(4)]
-        up1 = coef[9] * cs[1] / (HALF[1] + jnp.abs(cs[1]))
+        up1 = coef[6] * cs[1] / (HALF[1] + jnp.abs(cs[1]))
         for s in range(4):
             edge = []
             for y_side in range(2):
@@ -575,7 +620,7 @@
             around = (ym, yp) + ((outer, inner) if side == 0 else (inner, outer))
             z_face.append(advance(
                 s, turn(pack[0], -10 * s), cs[s], turn(pack[0], -(10 * s + 2)), around,
-                coef[:6], flow, coef[9], up1,
+                coef[:6], flow, coef[6], up1,
             ))
 
     def get_u(p):
@@ -616,7 +661,6 @@
         out_shape=tuple(jax.ShapeDtypeStruct(s, t) for s, t in outs),
         scratch_shapes=[VMEM(*x) if isinstance(x, tuple) else x for x in scratch],
         compiler_params=pltpu.CompilerParams(vmem_limit_bytes=limit),
-        name=kernel.__name__,
     )(*smem, *arrays)
 
 
@@ -630,15 +674,14 @@
     return lax.ppermute(x, axis, [(i, j) for i in range(n) for j in [i ^ 1 if first else ((i + 1) ^ 1) - 1] if 0 <= j < n])
 
 
-def swaps(turn, ya, yb, za, zb):
+def swaps(ya, yb, za, zb):
     out = []
-    for name, x, axis, first in (("za", za, "gz", True), ("zb", zb, "gz", False), ("ya", ya, "gy", True), ("yb", yb, "gy", False)):
-        with jax.named_scope(f"{name}{turn}"):
-            out.append(swap(x, axis, first))
+    for x, axis, first in ((za, "gz", True), (zb, "gz", False), (ya, "gy", True), (yb, "gy", False)):
+        out.append(swap(x, axis, first))
     return tuple(out)
 
 
-def shards(populations, viscosity, links, flags, neighbours, owners, slots, conc, diff, upt):
+def program(populations, viscosity, links, flags, neighbours, owners, slots, conc, diff, upt):
     i32 = jnp.int32
     tiles = lambda n: ((n, 8, 128), F32)
     tile = ((8, 128), F32)
@@ -656,31 +699,32 @@
         second_kernel, (neighbours,), (state, xl, xr, conc, diff),
         [tiles(38), tiles(12)] + faces(5, 16), pool,
     )
-    rim = swaps(0, *rim)
+    rim = swaps(*rim)
     for _ in range(FLOW_STEPS - 2):
         left, right = hop(unit, "gx", 1), hop(unit, "gx", -1)
         post, unit = call(
             step_kernel, (neighbours,), (state, post, unit, left, right), [tiles(38), tiles(12)], pool
         )
     left, right = hop(unit, "gx", 1), hop(unit, "gx", -1)
-    weighted, send = call(
-        last_kernel, (neighbours, owners), (state, post, unit, left, right),
-        [((19, 1, 4, 512), F32), ((16, 24, 128), F32)],
-        pool + [((19, 16, 128), F32), ((3, 16, 128), F32)],
+    last, send = call(
+        last_kernel, (neighbours, owners, slots), (state, post, unit, left, right),
+        [((19, 16, 128), F32), ((16, 9, 2, 128), F32)], pool + [((3, 16, 128), F32)],
     )
-    with jax.named_scope("spread"):
-        recv = lax.all_to_all(send, "gx", 0, 0)
-    with jax.named_scope("drift"):
-        (drift,) = call(
-            velocity_kernel, (owners, slots), (recv,), [((6, 12, 8, 128), F32)],
-            [((17 * 16, 128), F32), ((6, 24, 128), F32)],
-        )
+    recv = lax.all_to_all(send, "gx", 0, 0)
+    (weighted,) = call(weighted_kernel, (), (last,), [((19, 1, 4, 512), F32)])
     face = ((FACE_ROWS, 128), F32)
-    c1, spread, ma, mb, pack_lo, pack_hi, coef_lo, coef_hi = call(
-        tissue1_kernel, (), (drift, conc, diff, upt, xl, xr) + rim,
-        [((4, 12, 8, 128), F32), ((6, 12, 8, 128), F32), face, face] + [tile] * 4,
+    twelve = lambda n: ((n, 12, 8, 128), F32)
+    part, spread, ca, cb, coef_lo, coef_hi = call(
+        spread_kernel, (), (conc, diff, upt, xl, xr) + rim,
+        [twelve(4), twelve(6), ((56, 128), F32), ((56, 128), F32), tile, tile],
     )
-    ya, yb = swap(ma, "gy", True), swap(mb, "gy", False)
+    drift, c1, ma, mb, pack_lo, pack_hi, coef_lo, coef_hi = call(
+        drift_kernel, (owners, slots), (recv, part, conc, xl, xr) + rim + (ca, cb, coef_lo, coef_hi),
+        [twelve(6), twelve(4), face, face] + [tile] * 4,
+        [((17 * 16, 128), F32), ((6, 24, 128), F32)],
+    )
+    ya = swap(ma, "gy", True)
+    yb = swap(mb, "gy", False)
     za, zb = call(
         corner_kernel, (), (ya, yb, pack_lo, pack_hi, coef_lo, coef_hi), [tiles(3), tiles(3)]
     )
@@ -697,7 +741,7 @@
     site = P(("gy", "gz"), "gx", None)
     brick = P("gx", "gy", "gz")
     return jax.shard_map(
-        shards,
+        program,
         mesh=mesh,
         in_specs=(
             P(None, ("gy", "gz"), "gx", None), site, site, site, site,

time: 102 us -> 100 us (0.980)
  starting transfers between devices: 69.3 us -> 67.4 us
    ppermute x8, starting transfers between devices: 27.5 us -> 25.4 us  [swap(): lax.ppermute(x, axis, [(i, j) for i in range(n) for j in [i ^ 1 if first...]
    pallas_call x9 -> x10, Pallas kernels: 13.3 us -> 13.6 us  [call(): pl.pallas_call(kernel, in_specs=[pl.BlockSpec(memory_space=pltpu.SMEM)] *...]
  transfers between devices with their start and end apart: 17 -> 17, of which waited for: 8 -> 8; matrix products, arithmetic and copies ran while one was open for 0% -> 0% of each run, Pallas kernels for 1% -> 2%
where the time goes in v3:
time: 100 us; the launch traced here: 98.8 us
  starting transfers between devices  67.4 us (67%)
  waiting for transfers between devices  15.9 us (16%)
  Pallas kernels  13.6 us (14%)
    ppermute x8, starting transfers between devices, swap(): lax.ppermute(x, axis, [(i, j) for i in range(n) for j in [i ^ 1 if first...  25.4 us
    ppermute x8, starting transfers between devices, hop(): lax.ppermute(x, axis, [(i, i + step) for i in range(n) if 0 <= i + step <...  23.1 us
    all_to_all x1, starting transfers between devices, program(): recv = lax.all_to_all(send, 'gx', 0, 0)  18.9 us
    pallas_call x10, Pallas kernels, call(): pl.pallas_call(kernel, in_specs=[pl.BlockSpec(memory_space=pltpu.SMEM)] *...  13.6 us
    ppermute x8, waiting for transfers between devices, hop(): lax.ppermute(x, axis, [(i, i + step) for i in range(n) if 0 <= i + step <...  8.54 us
    ppermute x8, waiting for transfers between devices, swap(): lax.ppermute(x, axis, [(i, j) for i in range(n) for j in [i ^ 1 if first...  7.33 us
  transfers between devices with their start and end apart: 17, of which 8 were waited for; matrix products, arithmetic and copies ran while one was open for 0% of the time, Pallas kernels for 2%

profile of v3, /device:TPU:21, one launch (start us, length us, event | category | flops | bytes accessed | tf_op | source)
XLA Modules:
  0.0 98.8 jit_solution(13010263095498017796)
XLA Ops:
  0.7 2.8 %shard_map.113 = (f32[54,8,128]{2,1,0:T(8,128)}, f32[30,8,128]{2,1,0:T(8,128)}, f32[30,8,128]{2,1,0:T(8,128)}) custom-call(s32[1,4,18]{2,1,0:T(4,128)} %nbr_ref.9, f32[19,1,4,512]{3,2,1,0:T(4,128)} %pop_hbm.1, f32[1,4,512]{2,1,0:T(4,128)} %visc_hbm.1, s32[1,4,512]{2,1,0:T(4,128)} %link_hbm.1, s32[1,4,512]{2,1,0:T(4,128)} %flag_hbm.1, f32[4,8,8,128]{3,2,1,0:T(8,128)} %conc.5, ...), custom_call_target="tpu_custom_call" | custom-call | tf_op jit(solution)/shard_map/pallas_call | solution.py:656
  3.5 3.5 %collective-permute-start = (f32[30,8,128]{2,1,0:T(8,128)}, f32[30,8,128]{2,1,0:T(8,128)S(1)}, u32[]{:S(2)}, u32[]{:S(2)}) collective-permute-start(f32[30,8,128]{2,1,0:T(8,128)} %get-tuple-element.34), channel_id=1, source_target_pairs={{0,32},{32,64},{64,96},{96,128},{128,160},{160,192},{192,224},{224... | collective-permute-start | bytes 368648 | tf_op jit(solution)/shard_map/ppermute | solution.py:669
  7.1 1.3 %collective-permute-start.1 = (f32[30,8,128]{2,1,0:T(8,128)}, f32[30,8,128]{2,1,0:T(8,128)S(1)}, u32[]{:S(2)}, u32[]{:S(2)}) collective-permute-start(f32[30,8,128]{2,1,0:T(8,128)} %get-tuple-element.35), channel_id=1, source_target_pairs={{32,0},{64,32},{96,64},{128,96},{160,128},{192,160},{224,192},{256... | collective-permute-start | bytes 368648 | tf_op jit(solution)/shard_map/ppermute | solution.py:669
  8.4 1.0 %collective-permute-done.left_ref.xl = f32[30,8,128]{2,1,0:T(8,128)S(1)} collective-permute-done((f32[30,8,128]{2,1,0:T(8,128)}, f32[30,8,128]{2,1,0:T(8,128)S(1)}, u32[]{:S(2)}, u32[]{:S(2)}) %collective-permute-start) | collective-permute-done | bytes 122912 | tf_op jit(solution)/shard_map/ppermute | solution.py:669
  9.4 4.1 %collective-permute-done.1.right_ref.xr = f32[30,8,128]{2,1,0:T(8,128)S(1)} collective-permute-done((f32[30,8,128]{2,1,0:T(8,128)}, f32[30,8,128]{2,1,0:T(8,128)S(1)}, u32[]{:S(2)}, u32[]{:S(2)}) %collective-permute-start.1) | collective-permute-done | bytes 122912 | tf_op jit(solution)/shard_map/ppermute | solution.py:669
  14.4 1.2 %shard_map.114 = (f32[38,8,128]{2,1,0:T(8,128)S(1)}, f32[12,8,128]{2,1,0:T(8,128)S(1)}, f32[5,16,128]{2,1,0:T(8,128)S(1)}, f32[5,16,128]{2,1,0:T(8,128)S(1)}, f3...) custom-call(s32[1,4,18]{2,1,0:T(4,128)S(1)} %copy-done.5, f32[54,8,128]{2,1,0:T(8,128)S(1)} %copy-done, ...), custom_call_target="tpu_custom_call" | custom-call | tf_op jit(solution)/shard_map/pallas_call | solution.py:656
  15.6 1.3 %collective-permute-start.3 = (f32[12,8,128]{2,1,0:T(8,128)S(1)}, f32[12,8,128]{2,1,0:T(8,128)S(1)}, u32[]{:S(2)}, u32[]{:S(2)}) collective-permute-start(f32[12,8,128]{2,1,0:T(8,128)S(1)} %get-tuple-element.37.unit_in), channel_id=1, source_target_pairs={{32,0},{64,32},{96,64},{128,96},{160,128},{192,160},{224,192},{256... | collective-permute-start | bytes 147464 | tf_op jit(solution)/shard_map/ppermute | solution.py:669
  16.9 4.2 %collective-permute-start.2 = (f32[12,8,128]{2,1,0:T(8,128)S(1)}, f32[12,8,128]{2,1,0:T(8,128)S(1)}, u32[]{:S(2)}, u32[]{:S(2)}) collective-permute-start(f32[12,8,128]{2,1,0:T(8,128)S(1)} %get-tuple-element.37.unit_in), channel_id=1, source_target_pairs={{0,32},{32,64},{64,96},{96,128},{128,160},{160,192},{192,224},{224... | collective-permute-start | bytes 147464 | tf_op jit(solution)/shard_map/ppermute | solution.py:669
  21.0 1.1 %collective-permute-done.2.left_ref = f32[12,8,128]{2,1,0:T(8,128)S(1)} collective-permute-done((f32[12,8,128]{2,1,0:T(8,128)S(1)}, f32[12,8,128]{2,1,0:T(8,128)S(1)}, u32[]{:S(2)}, u32[]{:S(2)}) %collective-permute-start.2) | collective-permute-done | bytes 49184 | tf_op jit(solution)/shard_map/ppermute | solution.py:669
  22.2 1.0 %shard_map.115 = (f32[38,8,128]{2,1,0:T(8,128)S(1)}, f32[12,8,128]{2,1,0:T(8,128)S(1)}) custom-call(s32[1,4,18]{2,1,0:T(4,128)S(1)} %copy-done.5, f32[54,8,128]{2,1,0:T(8,128)S(1)} %copy-done.1, f32[38,8,128]{2,1,0:T(8,128)S(1)} %get-tuple-element.36.post_in, f32[12,8,128]{2,1,0:T(8,128)S(1)} %get-tuple-element.37.unit_in, ...), custom_call_target="tpu_custom_call" | custom-call | tf_op jit(solution)/shard_map/pallas_call | solution.py:656
  23.2 1.3 %collective-permute-start.5 = (f32[12,8,128]{2,1,0:T(8,128)S(1)}, f32[12,8,128]{2,1,0:T(8,128)S(1)}, u32[]{:S(2)}, u32[]{:S(2)}) collective-permute-start(f32[12,8,128]{2,1,0:T(8,128)S(1)} %get-tuple-element.39.unit_in), channel_id=1, source_target_pairs={{32,0},{64,32},{96,64},{128,96},{160,128},{192,160},{224,192},{256... | collective-permute-start | bytes 147464 | tf_op jit(solution)/shard_map/ppermute | solution.py:669
  24.5 5.5 %collective-permute-start.4 = (f32[12,8,128]{2,1,0:T(8,128)S(1)}, f32[12,8,128]{2,1,0:T(8,128)S(1)}, u32[]{:S(2)}, u32[]{:S(2)}) collective-permute-start(f32[12,8,128]{2,1,0:T(8,128)S(1)} %get-tuple-element.39.unit_in), channel_id=1, source_target_pairs={{0,32},{32,64},{64,96},{96,128},{128,160},{160,192},{192,224},{224... | collective-permute-start | bytes 147464 | tf_op jit(solution)/shard_map/ppermute | solution.py:669
  30.0 1.1 %collective-permute-done.4.left_ref = f32[12,8,128]{2,1,0:T(8,128)S(1)} collective-permute-done((f32[12,8,128]{2,1,0:T(8,128)S(1)}, f32[12,8,128]{2,1,0:T(8,128)S(1)}, u32[]{:S(2)}, u32[]{:S(2)}) %collective-permute-start.4) | collective-permute-done | bytes 49184 | tf_op jit(solution)/shard_map/ppermute | solution.py:669
  31.2 1.0 %shard_map.116 = (f32[38,8,128]{2,1,0:T(8,128)S(1)}, f32[12,8,128]{2,1,0:T(8,128)S(1)}) custom-call(s32[1,4,18]{2,1,0:T(4,128)S(1)} %copy-done.5, f32[54,8,128]{2,1,0:T(8,128)S(1)} %copy-done.1, f32[38,8,128]{2,1,0:T(8,128)S(1)} %get-tuple-element.38.post_in, f32[12,8,128]{2,1,0:T(8,128)S(1)} %get-tuple-element.39.unit_in, ...), custom_call_target="tpu_custom_call" | custom-call | tf_op jit(solution)/shard_map/pallas_call | solution.py:656
  32.2 1.3 %collective-permute-start.7 = (f32[12,8,128]{2,1,0:T(8,128)S(1)}, f32[12,8,128]{2,1,0:T(8,128)S(1)}, u32[]{:S(2)}, u32[]{:S(2)}) collective-permute-start(f32[12,8,128]{2,1,0:T(8,128)S(1)} %get-tuple-element.41.unit_in), channel_id=1, source_target_pairs={{32,0},{64,32},{96,64},{128,96},{160,128},{192,160},{224,192},{256... | collective-permute-start | bytes 147464 | tf_op jit(solution)/shard_map/ppermute | solution.py:669
  33.5 4.7 %collective-permute-start.6 = (f32[12,8,128]{2,1,0:T(8,128)S(1)}, f32[12,8,128]{2,1,0:T(8,128)S(1)}, u32[]{:S(2)}, u32[]{:S(2)}) collective-permute-start(f32[12,8,128]{2,1,0:T(8,128)S(1)} %get-tuple-element.41.unit_in), channel_id=1, source_target_pairs={{0,32},{32,64},{64,96},{96,128},{128,160},{160,192},{192,224},{224... | collective-permute-start | bytes 147464 | tf_op jit(solution)/shard_map/ppermute | solution.py:669
  38.3 1.1 %collective-permute-done.6.left_ref = f32[12,8,128]{2,1,0:T(8,128)S(1)} collective-permute-done((f32[12,8,128]{2,1,0:T(8,128)S(1)}, f32[12,8,128]{2,1,0:T(8,128)S(1)}, u32[]{:S(2)}, u32[]{:S(2)}) %collective-permute-start.6) | collective-permute-done | bytes 49184 | tf_op jit(solution)/shard_map/ppermute | solution.py:669
  39.4 1.9 %shard_map.117 = (f32[19,16,128]{2,1,0:T(8,128)S(1)}, f32[16,9,2,128]{3,2,1,0:T(2,128)}) custom-call(s32[1,4,18]{2,1,0:T(4,128)S(1)} %copy-done.5, s32[1,64]{1,0:T(1,128)S(1)} %copy-done.6, s32[1,64]{1,0:T(1,128)S(1)} %copy-done.7, f32[54,8,128]{2,1,0:T(8,128)S(1)} %copy-done.1, f32[38,8,128]{2,1,0:T(8,128)S(1)} %get-tuple-element.40.post_in, ...), custom_call_target="tpu_custom_call" | custom-call | tf_op jit(solution)/shard_map/pallas_call | solution.py:656
  41.3 18.9 %all-to-all-start = ((f32[16,9,2,128]{3,2,1,0:T(2,128)}), f32[16,9,2,128]{3,2,1,0:T(2,128)S(1)}, u32[]{:S(2)}, u32[]{:S(2)}) async-start(f32[16,9,2,128]{3,2,1,0:T(2,128)} %get-tuple-element.43), calls=%async_computation | async-start | bytes 294912 | tf_op jit(solution)/shard_map/all_to_all | solution.py:713
  60.2 8.0 %collective-permute-start.10 = (f32[5,16,128]{2,1,0:T(8,128)S(1)}, f32[5,16,128]{2,1,0:T(8,128)S(1)}, u32[]{:S(2)}, u32[]{:S(2)}) collective-permute-start(f32[5,16,128]{2,1,0:T(8,128)S(1)} %get-tuple-element.46), channel_id=1, source_target_pairs={{0,4},{4,0},{8,12},{12,8},{16,20},{20,16},{24,28},{28,24},{1,5},{5... | collective-permute-start | bytes 122888 | tf_op jit(solution)/shard_map/ppermute | solution.py:674
  68.2 2.7 %collective-permute-start.11 = (f32[5,16,128]{2,1,0:T(8,128)S(1)}, f32[5,16,128]{2,1,0:T(8,128)S(1)}, u32[]{:S(2)}, u32[]{:S(2)}) collective-permute-start(f32[5,16,128]{2,1,0:T(8,128)S(1)} %get-tuple-element.47), channel_id=1, source_target_pairs={{4,8},{8,4},{12,16},{16,12},{20,24},{24,20},{5,9},{9,5},{13,17},{1... | collective-permute-start | bytes 122888 | tf_op jit(solution)/shard_map/ppermute | solution.py:674
  70.9 2.9 %collective-permute-start.8 = (f32[8,128]{1,0:T(8,128)S(1)}, f32[8,128]{1,0:T(8,128)S(1)}, u32[]{:S(2)}, u32[]{:S(2)}) collective-permute-start(f32[8,128]{1,0:T(8,128)S(1)} %get-tuple-element.44), channel_id=1, source_target_pairs={{0,1},{1,0},{2,3},{3,2},{4,5},{5,4},{6,7},{7,6},{8,9},{9,8},{10,11... | collective-permute-start | bytes 12296 | tf_op jit(solution)/shard_map/ppermute | solution.py:674
  73.9 1.9 %collective-permute-start.9 = (f32[8,128]{1,0:T(8,128)S(1)}, f32[8,128]{1,0:T(8,128)S(1)}, u32[]{:S(2)}, u32[]{:S(2)}) collective-permute-start(f32[8,128]{1,0:T(8,128)S(1)} %get-tuple-element.45), channel_id=1, source_target_pairs={{1,2},{2,1},{5,6},{6,5},{9,10},{10,9},{13,14},{14,13},{17,18},{18,... | collective-permute-start | bytes 12296 | tf_op jit(solution)/shard_map/ppermute | solution.py:674
  75.8 2.7 %collective-permute-done.9.zb = f32[8,128]{1,0:T(8,128)S(1)} collective-permute-done((f32[8,128]{1,0:T(8,128)S(1)}, f32[8,128]{1,0:T(8,128)S(1)}, u32[]{:S(2)}, u32[]{:S(2)}) %collective-permute-start.9) | collective-permute-done | bytes 4128 | tf_op jit(solution)/shard_map/ppermute | solution.py:674
  79.4 2.8 %shard_map.120 = (f32[6,12,8,128]{3,2,1,0:T(8,128)S(1)}, f32[4,12,8,128]{3,2,1,0:T(8,128)S(1)}, f32[176,128]{1,0:T(8,128)S(1)}, f32[176,128]{1,0:T(8,128)S(1)}, ...) custom-call(s32[1,64]{1,0:T(1,128)S(1)} %copy-done.6, ...), custom_call_target="tpu_custom_call" | custom-call | tf_op jit(solution)/shard_map/pallas_call | solution.py:656
  82.2 2.9 %collective-permute-start.12 = (f32[176,128]{1,0:T(8,128)S(1)}, f32[176,128]{1,0:T(8,128)S(1)}, u32[]{:S(2)}, u32[]{:S(2)}) collective-permute-start(f32[176,128]{1,0:T(8,128)S(1)} %get-tuple-element.56.ma), channel_id=1, source_target_pairs={{0,4},{4,0},{8,12},{12,8},{16,20},{20,16},{24,28},{28,24},{1,5},{5... | collective-permute-start | bytes 270344 | tf_op jit(solution)/shard_map/ppermute | solution.py:674
  85.1 3.0 %collective-permute-start.13 = (f32[176,128]{1,0:T(8,128)S(1)}, f32[176,128]{1,0:T(8,128)S(1)}, u32[]{:S(2)}, u32[]{:S(2)}) collective-permute-start(f32[176,128]{1,0:T(8,128)S(1)} %get-tuple-element.57.mb), channel_id=1, source_target_pairs={{4,8},{8,4},{12,16},{16,12},{20,24},{24,20},{5,9},{9,5},{13,17},{1... | collective-permute-start | bytes 270344 | tf_op jit(solution)/shard_map/ppermute | solution.py:674
  88.1 2.8 %collective-permute-done.13.yb = f32[176,128]{1,0:T(8,128)S(1)} collective-permute-done((f32[176,128]{1,0:T(8,128)S(1)}, f32[176,128]{1,0:T(8,128)S(1)}, u32[]{:S(2)}, u32[]{:S(2)}) %collective-permute-start.13) | collective-permute-done | bytes 90144 | tf_op jit(solution)/shard_map/ppermute | solution.py:674
  91.0 2.0 %collective-permute-start.14 = (f32[3,8,128]{2,1,0:T(8,128)S(1)}, f32[3,8,128]{2,1,0:T(8,128)S(1)}, u32[]{:S(2)}, u32[]{:S(2)}) collective-permute-start(f32[3,8,128]{2,1,0:T(8,128)S(1)} %get-tuple-element.62), channel_id=1, source_target_pairs={{0,1},{1,0},{2,3},{3,2},{4,5},{5,4},{6,7},{7,6},{8,9},{9,8},{10,11... | collective-permute-start | bytes 36872 | tf_op jit(solution)/shard_map/ppermute | solution.py:674
  93.1 1.9 %collective-permute-start.15 = (f32[3,8,128]{2,1,0:T(8,128)S(1)}, f32[3,8,128]{2,1,0:T(8,128)S(1)}, u32[]{:S(2)}, u32[]{:S(2)}) collective-permute-start(f32[3,8,128]{2,1,0:T(8,128)S(1)} %get-tuple-element.63), channel_id=1, source_target_pairs={{1,2},{2,1},{5,6},{6,5},{9,10},{10,9},{13,14},{14,13},{17,18},{18,... | collective-permute-start | bytes 36872 | tf_op jit(solution)/shard_map/ppermute | solution.py:674
  95.7 1.8 %collective-permute-done.15.zb = f32[3,8,128]{2,1,0:T(8,128)S(1)} collective-permute-done((f32[3,8,128]{2,1,0:T(8,128)S(1)}, f32[3,8,128]{2,1,0:T(8,128)S(1)}, u32[]{:S(2)}, u32[]{:S(2)}) %collective-permute-start.15) | collective-permute-done | bytes 12320 | tf_op jit(solution)/shard_map/ppermute | solution.py:674
  97.5 1.3 %shard_map.122 = f32[4,8,8,128]{3,2,1,0:T(8,128)} custom-call(f32[6,12,8,128]{3,2,1,0:T(8,128)S(1)} %get-tuple-element.53.drift, f32[6,12,8,128]{3,2,1,0:T(8,128)S(1)} %get-tuple-element.54.spread, f32[4,12,8,128]{3,2,1,0:T(8,128)S(1)} %get-tuple-element.55.conc, f32[8,8,128]{2,1,0:T(8,128)S(1)} %copy-done.4, ...), custom_call_target="tpu_custom_call" | custom-call | tf_op jit(solution)/shard_map/pallas_call | solution.py:656
  (28 shorter events, 2.6 us)
Async XLA Ops:
  0.6 12.8 %copy-start.2 = (f32[4,8,8,128]{3,2,1,0:T(8,128)S(1)}, f32[4,8,8,128]{3,2,1,0:T(8,128)}, u32[]{:S(2)}) copy-start(f32[4,8,8,128]{3,2,1,0:T(8,128)} %conc.5) | copy-start | bytes 393220
  0.6 12.8 %copy-start.3 = (f32[8,8,128]{2,1,0:T(8,128)S(1)}, f32[8,8,128]{2,1,0:T(8,128)}, u32[]{:S(2)}) copy-start(f32[8,8,128]{2,1,0:T(8,128)} %diff.3) | copy-start | bytes 98308
  3.5 10.0 %copy-start.5 = (s32[1,4,18]{2,1,0:T(4,128)S(1)}, s32[1,4,18]{2,1,0:T(4,128)}, u32[]{:S(2)}) copy-start(s32[1,4,18]{2,1,0:T(4,128)} %nbr_ref.9) | copy-start | bytes 868
  3.5 5.9 %collective-permute-start = (f32[30,8,128]{2,1,0:T(8,128)}, f32[30,8,128]{2,1,0:T(8,128)S(1)}, u32[]{:S(2)}, u32[]{:S(2)}) collective-permute-start(f32[30,8,128]{2,1,0:T(8,128)} %get-tuple-element.34), channel_id=1, source_target_pairs={{0,32},{32,64},{64,96},{96,128},{128,160},{160,192},{192,224},{224... | collective-permute-start | bytes 368648 | tf_op jit(solution)/shard_map/ppermute | solution.py:669
  7.1 6.4 %collective-permute-start.1 = (f32[30,8,128]{2,1,0:T(8,128)}, f32[30,8,128]{2,1,0:T(8,128)S(1)}, u32[]{:S(2)}, u32[]{:S(2)}) collective-permute-start(f32[30,8,128]{2,1,0:T(8,128)} %get-tuple-element.35), channel_id=1, source_target_pairs={{32,0},{64,32},{96,64},{128,96},{160,128},{192,160},{224,192},{256... | collective-permute-start | bytes 368648 | tf_op jit(solution)/shard_map/ppermute | solution.py:669
  13.5 0.9 copy-start
  14.4 7.8 %copy-start.1 = (f32[54,8,128]{2,1,0:T(8,128)S(1)}, f32[54,8,128]{2,1,0:T(8,128)}, u32[]{:S(2)}) copy-start(f32[54,8,128]{2,1,0:T(8,128)} %get-tuple-element.33.state) | copy-start | bytes 663556
  15.6 5.5 %collective-permute-start.3 = (f32[12,8,128]{2,1,0:T(8,128)S(1)}, f32[12,8,128]{2,1,0:T(8,128)S(1)}, u32[]{:S(2)}, u32[]{:S(2)}) collective-permute-start(f32[12,8,128]{2,1,0:T(8,128)S(1)} %get-tuple-element.37.unit_in), channel_id=1, source_target_pairs={{32,0},{64,32},{96,64},{128,96},{160,128},{192,160},{224,192},{256... | collective-permute-start | bytes 147464 | tf_op jit(solution)/shard_map/ppermute | solution.py:669
  16.9 5.3 %collective-permute-start.2 = (f32[12,8,128]{2,1,0:T(8,128)S(1)}, f32[12,8,128]{2,1,0:T(8,128)S(1)}, u32[]{:S(2)}, u32[]{:S(2)}) collective-permute-start(f32[12,8,128]{2,1,0:T(8,128)S(1)} %get-tuple-element.37.unit_in), channel_id=1, source_target_pairs={{0,32},{32,64},{64,96},{96,128},{128,160},{160,192},{192,224},{224... | collective-permute-start | bytes 147464 | tf_op jit(solution)/shard_map/ppermute | solution.py:669
  23.2 6.8 %collective-permute-start.5 = (f32[12,8,128]{2,1,0:T(8,128)S(1)}, f32[12,8,128]{2,1,0:T(8,128)S(1)}, u32[]{:S(2)}, u32[]{:S(2)}) collective-permute-start(f32[12,8,128]{2,1,0:T(8,128)S(1)} %get-tuple-element.39.unit_in), channel_id=1, source_target_pairs={{32,0},{64,32},{96,64},{128,96},{160,128},{192,160},{224,192},{256... | collective-permute-start | bytes 147464 | tf_op jit(solution)/shard_map/ppermute | solution.py:669
  24.5 6.6 %collective-permute-start.4 = (f32[12,8,128]{2,1,0:T(8,128)S(1)}, f32[12,8,128]{2,1,0:T(8,128)S(1)}, u32[]{:S(2)}, u32[]{:S(2)}) collective-permute-start(f32[12,8,128]{2,1,0:T(8,128)S(1)} %get-tuple-element.39.unit_in), channel_id=1, source_target_pairs={{0,32},{32,64},{64,96},{96,128},{128,160},{160,192},{192,224},{224... | collective-permute-start | bytes 147464 | tf_op jit(solution)/shard_map/ppermute | solution.py:669
  32.2 7.2 %copy-start.6 = (s32[1,64]{1,0:T(1,128)S(1)}, s32[1,64]{1,0:T(1,128)}, u32[]{:S(2)}) copy-start(s32[1,64]{1,0:T(1,128)} %own_ref.3) | copy-start | bytes 772
  32.2 7.2 %copy-start.7 = (s32[1,64]{1,0:T(1,128)S(1)}, s32[1,64]{1,0:T(1,128)}, u32[]{:S(2)}) copy-start(s32[1,64]{1,0:T(1,128)} %slot_ref.3) | copy-start | bytes 772
  32.2 6.0 %collective-permute-start.7 = (f32[12,8,128]{2,1,0:T(8,128)S(1)}, f32[12,8,128]{2,1,0:T(8,128)S(1)}, u32[]{:S(2)}, u32[]{:S(2)}) collective-permute-start(f32[12,8,128]{2,1,0:T(8,128)S(1)} %get-tuple-element.41.unit_in), channel_id=1, source_target_pairs={{32,0},{64,32},{96,64},{128,96},{160,128},{192,160},{224,192},{256... | collective-permute-start | bytes 147464 | tf_op jit(solution)/shard_map/ppermute | solution.py:669
  33.5 5.9 %collective-permute-start.6 = (f32[12,8,128]{2,1,0:T(8,128)S(1)}, f32[12,8,128]{2,1,0:T(8,128)S(1)}, u32[]{:S(2)}, u32[]{:S(2)}) collective-permute-start(f32[12,8,128]{2,1,0:T(8,128)S(1)} %get-tuple-element.41.unit_in), channel_id=1, source_target_pairs={{0,32},{32,64},{64,96},{96,128},{128,160},{160,192},{192,224},{224... | collective-permute-start | bytes 147464 | tf_op jit(solution)/shard_map/ppermute | solution.py:669
  41.3 37.2 %copy-start.4 = (f32[8,8,128]{2,1,0:T(8,128)S(1)}, f32[8,8,128]{2,1,0:T(8,128)}, u32[]{:S(2)}) copy-start(f32[8,8,128]{2,1,0:T(8,128)} %upt.3) | copy-start | bytes 98308
  41.3 38.1 %all-to-all-start = ((f32[16,9,2,128]{3,2,1,0:T(2,128)}), f32[16,9,2,128]{3,2,1,0:T(2,128)S(1)}, u32[]{:S(2)}, u32[]{:S(2)}) async-start(f32[16,9,2,128]{3,2,1,0:T(2,128)} %get-tuple-element.43), calls=%async_computation | async-start | bytes 294912 | tf_op jit(solution)/shard_map/all_to_all | solution.py:713
  60.2 18.3 %collective-permute-start.10 = (f32[5,16,128]{2,1,0:T(8,128)S(1)}, f32[5,16,128]{2,1,0:T(8,128)S(1)}, u32[]{:S(2)}, u32[]{:S(2)}) collective-permute-start(f32[5,16,128]{2,1,0:T(8,128)S(1)} %get-tuple-element.46), channel_id=1, source_target_pairs={{0,4},{4,0},{8,12},{12,8},{16,20},{20,16},{24,28},{28,24},{1,5},{5... | collective-permute-start | bytes 122888 | tf_op jit(solution)/shard_map/ppermute | solution.py:674
  68.2 10.3 %collective-permute-start.11 = (f32[5,16,128]{2,1,0:T(8,128)S(1)}, f32[5,16,128]{2,1,0:T(8,128)S(1)}, u32[]{:S(2)}, u32[]{:S(2)}) collective-permute-start(f32[5,16,128]{2,1,0:T(8,128)S(1)} %get-tuple-element.47), channel_id=1, source_target_pairs={{4,8},{8,4},{12,16},{16,12},{20,24},{24,20},{5,9},{9,5},{13,17},{1... | collective-permute-start | bytes 122888 | tf_op jit(solution)/shard_map/ppermute | solution.py:674
  70.9 4.8 %collective-permute-start.8 = (f32[8,128]{1,0:T(8,128)S(1)}, f32[8,128]{1,0:T(8,128)S(1)}, u32[]{:S(2)}, u32[]{:S(2)}) collective-permute-start(f32[8,128]{1,0:T(8,128)S(1)} %get-tuple-element.44), channel_id=1, source_target_pairs={{0,1},{1,0},{2,3},{3,2},{4,5},{5,4},{6,7},{7,6},{8,9},{9,8},{10,11... | collective-permute-start | bytes 12296 | tf_op jit(solution)/shard_map/ppermute | solution.py:674
  73.9 4.6 %collective-permute-start.9 = (f32[8,128]{1,0:T(8,128)S(1)}, f32[8,128]{1,0:T(8,128)S(1)}, u32[]{:S(2)}, u32[]{:S(2)}) collective-permute-start(f32[8,128]{1,0:T(8,128)S(1)} %get-tuple-element.45), channel_id=1, source_target_pairs={{1,2},{2,1},{5,6},{6,5},{9,10},{10,9},{13,14},{14,13},{17,18},{18,... | collective-permute-start | bytes 12296 | tf_op jit(solution)/shard_map/ppermute | solution.py:674
  82.2 5.9 %collective-permute-start.12 = (f32[176,128]{1,0:T(8,128)S(1)}, f32[176,128]{1,0:T(8,128)S(1)}, u32[]{:S(2)}, u32[]{:S(2)}) collective-permute-start(f32[176,128]{1,0:T(8,128)S(1)} %get-tuple-element.56.ma), channel_id=1, source_target_pairs={{0,4},{4,0},{8,12},{12,8},{16,20},{20,16},{24,28},{28,24},{1,5},{5... | collective-permute-start | bytes 270344 | tf_op jit(solution)/shard_map/ppermute | solution.py:674
  85.1 5.8 %collective-permute-start.13 = (f32[176,128]{1,0:T(8,128)S(1)}, f32[176,128]{1,0:T(8,128)S(1)}, u32[]{:S(2)}, u32[]{:S(2)}) collective-permute-start(f32[176,128]{1,0:T(8,128)S(1)} %get-tuple-element.57.mb), channel_id=1, source_target_pairs={{4,8},{8,4},{12,16},{16,12},{20,24},{24,20},{5,9},{9,5},{13,17},{1... | collective-permute-start | bytes 270344 | tf_op jit(solution)/shard_map/ppermute | solution.py:674
  91.0 4.7 %collective-permute-start.14 = (f32[3,8,128]{2,1,0:T(8,128)S(1)}, f32[3,8,128]{2,1,0:T(8,128)S(1)}, u32[]{:S(2)}, u32[]{:S(2)}) collective-permute-start(f32[3,8,128]{2,1,0:T(8,128)S(1)} %get-tuple-element.62), channel_id=1, source_target_pairs={{0,1},{1,0},{2,3},{3,2},{4,5},{5,4},{6,7},{7,6},{8,9},{9,8},{10,11... | collective-permute-start | bytes 36872 | tf_op jit(solution)/shard_map/ppermute | solution.py:674
  93.1 4.4 %collective-permute-start.15 = (f32[3,8,128]{2,1,0:T(8,128)S(1)}, f32[3,8,128]{2,1,0:T(8,128)S(1)}, u32[]{:S(2)}, u32[]{:S(2)}) collective-permute-start(f32[3,8,128]{2,1,0:T(8,128)S(1)} %get-tuple-element.63), channel_id=1, source_target_pairs={{1,2},{2,1},{5,6},{6,5},{9,10},{10,9},{13,14},{14,13},{17,18},{18,... | collective-permute-start | bytes 36872 | tf_op jit(solution)/shard_map/ppermute | solution.py:674

commit v4 on v3

--- a/solution.py
+++ b/solution.py
@@ -132,11 +132,15 @@
         unit_ref[base + 2 * u : base + 2 * u + 2] = acc
 
 
-def stream(sites, me, nbr_ref, post_ref, unit_ref, left_ref, right_ref, code_ref, pool, got, base=0):
+def stream(sites, me, nbr_ref, post_ref, unit_ref, left_ref, right_ref, code_ref, pool, got, base=0, swapped=True):
+    x_even = even("gx")
     for u in range(6):
-        pool[u, 0:16] = left_ref[2 * u : 2 * u + 2].reshape(16, 128)
+        left, right = left_ref[2 * u : 2 * u + 2], right_ref[2 * u : 2 * u + 2]
+        if swapped:
+            left, right = jnp.where(x_even, right, left), jnp.where(x_even, left, right)
+        pool[u, 0:16] = left.reshape(16, 128)
         pool[u, 16:32] = unit_ref[base + 2 * u : base + 2 * u + 2].reshape(16, 128)
-        pool[u, 32:48] = right_ref[2 * u : 2 * u + 2].reshape(16, 128)
+        pool[u, 32:48] = right.reshape(16, 128)
     first = (me - 1) * 4
     for k in range(18):
         d = DIRS[k + 1]
@@ -204,7 +208,7 @@
     copies = [pltpu.make_async_copy(src, dst, sem.at[n]) for n, (src, dst) in enumerate(pairs)]
     for copy in copies:
         copy.start()
-    for copy in copies:
+    for copy in copies[:4]:
         copy.wait()
     sites = Sites()
     f = []
@@ -251,6 +255,8 @@
     collide_pack(sites, f, relax, state, state, CODE + 4)
     lo[0:12] = state[42:54]
     hi[0:12] = state[42:54]
+    for copy in copies[4:]:
+        copy.wait()
 
 
 def step_kernel(nbr_ref, state, post_in, unit_in, left_ref, right_ref, post_ref, unit_ref, pool, got):
@@ -264,7 +270,7 @@
                   post_ref, unit_ref, ya, yb, za, zb, pool, got):
     sites = Sites()
     me = lax.axis_index("gx")
-    f = stream(sites, me, nbr_ref, state, state, left_ref, right_ref, state, pool, got, CODE + 4)
+    f = stream(sites, me, nbr_ref, state, state, left_ref, right_ref, state, pool, got, CODE + 4, False)
     collide_pack(sites, f, state[CODE : CODE + 2], post_ref, unit_ref)
     first_rims(conc, diff, left_ref, right_ref, ya, yb, za, zb)
 
@@ -701,11 +707,11 @@
     )
     rim = swaps(*rim)
     for _ in range(FLOW_STEPS - 2):
-        left, right = hop(unit, "gx", 1), hop(unit, "gx", -1)
+        left, right = swap(unit, "gx", True), swap(unit, "gx", False)
         post, unit = call(
             step_kernel, (neighbours,), (state, post, unit, left, right), [tiles(38), tiles(12)], pool
         )
-    left, right = hop(unit, "gx", 1), hop(unit, "gx", -1)
+    left, right = swap(unit, "gx", True), swap(unit, "gx", False)
     last, send = call(
         last_kernel, (neighbours, owners, slots), (state, post, unit, left, right),
         [((19, 16, 128), F32), ((16, 9, 2, 128), F32)], pool + [((3, 16, 128), F32)],

time: 100 us -> 100 us (level)
  the two profiles are of different devices: /device:TPU:21 before, /device:TPU:22 now
where the time goes in v4:
time: 100 us; the launch traced here: 99.2 us
  starting transfers between devices  62 us (62%)
  waiting for transfers between devices  21.7 us (22%)
  Pallas kernels  13.7 us (14%)
    ppermute x14, starting transfers between devices, swap(): lax.ppermute(x, axis, [(i, j) for i in range(n) for j in [i ^ 1 if first...  43.8 us
    ppermute x14, waiting for transfers between devices, swap(): lax.ppermute(x, axis, [(i, j) for i in range(n) for j in [i ^ 1 if first...  16 us
    pallas_call x10, Pallas kernels, call(): pl.pallas_call(kernel, in_specs=[pl.BlockSpec(memory_space=pltpu.SMEM)] *...  13.7 us
    all_to_all x1, starting transfers between devices, program(): recv = lax.all_to_all(send, 'gx', 0, 0)  13.1 us
    ppermute x2, waiting for transfers between devices, hop(): lax.ppermute(x, axis, [(i, i + step) for i in range(n) if 0 <= i + step <...  5.77 us
    ppermute x2, starting transfers between devices, hop(): lax.ppermute(x, axis, [(i, i + step) for i in range(n) if 0 <= i + step <...  5.12 us
  transfers between devices with their start and end apart: 17, of which 10 were waited for; matrix products, arithmetic and copies ran while one was open for 0% of the time, Pallas kernels for 2%

profile of v4, /device:TPU:22, one launch (start us, length us, event | category | flops | bytes accessed | tf_op | source)
XLA Modules:
  0.0 99.2 jit_solution(7993881051670555500)
XLA Ops:
  0.7 2.8 %shard_map.113 = (f32[54,8,128]{2,1,0:T(8,128)}, f32[30,8,128]{2,1,0:T(8,128)}, f32[30,8,128]{2,1,0:T(8,128)}) custom-call(s32[1,4,18]{2,1,0:T(4,128)} %nbr_ref.9, f32[19,1,4,512]{3,2,1,0:T(4,128)} %pop_hbm.1, f32[1,4,512]{2,1,0:T(4,128)} %visc_hbm.1, s32[1,4,512]{2,1,0:T(4,128)} %link_hbm.1, s32[1,4,512]{2,1,0:T(4,128)} %flag_hbm.1, f32[4,8,8,128]{3,2,1,0:T(8,128)} %conc.5, ...), custom_call_target="tpu_custom_call" | custom-call | tf_op jit(solution)/shard_map/pallas_call | solution.py:662
  3.5 3.8 %collective-permute-start = (f32[30,8,128]{2,1,0:T(8,128)}, f32[30,8,128]{2,1,0:T(8,128)S(1)}, u32[]{:S(2)}, u32[]{:S(2)}) collective-permute-start(f32[30,8,128]{2,1,0:T(8,128)} %get-tuple-element.34), channel_id=1, source_target_pairs={{0,32},{32,64},{64,96},{96,128},{128,160},{160,192},{192,224},{224... | collective-permute-start | bytes 368648 | tf_op jit(solution)/shard_map/ppermute | solution.py:675
  7.3 1.3 %collective-permute-start.1 = (f32[30,8,128]{2,1,0:T(8,128)}, f32[30,8,128]{2,1,0:T(8,128)S(1)}, u32[]{:S(2)}, u32[]{:S(2)}) collective-permute-start(f32[30,8,128]{2,1,0:T(8,128)} %get-tuple-element.35), channel_id=1, source_target_pairs={{32,0},{64,32},{96,64},{128,96},{160,128},{192,160},{224,192},{256... | collective-permute-start | bytes 368648 | tf_op jit(solution)/shard_map/ppermute | solution.py:675
  8.6 1.6 %collective-permute-done.left_ref.xl = f32[30,8,128]{2,1,0:T(8,128)S(1)} collective-permute-done((f32[30,8,128]{2,1,0:T(8,128)}, f32[30,8,128]{2,1,0:T(8,128)S(1)}, u32[]{:S(2)}, u32[]{:S(2)}) %collective-permute-start) | collective-permute-done | bytes 122912 | tf_op jit(solution)/shard_map/ppermute | solution.py:675
  10.2 4.2 %collective-permute-done.1.right_ref.xr = f32[30,8,128]{2,1,0:T(8,128)S(1)} collective-permute-done((f32[30,8,128]{2,1,0:T(8,128)}, f32[30,8,128]{2,1,0:T(8,128)S(1)}, u32[]{:S(2)}, u32[]{:S(2)}) %collective-permute-start.1) | collective-permute-done | bytes 122912 | tf_op jit(solution)/shard_map/ppermute | solution.py:675
  14.4 0.9 copy-done
  15.4 1.2 %shard_map.114 = (f32[38,8,128]{2,1,0:T(8,128)S(1)}, f32[12,8,128]{2,1,0:T(8,128)S(1)}, f32[5,16,128]{2,1,0:T(8,128)S(1)}, f32[5,16,128]{2,1,0:T(8,128)S(1)}, f3...) custom-call(s32[1,4,18]{2,1,0:T(4,128)S(1)} %copy-done.5, f32[54,8,128]{2,1,0:T(8,128)S(1)} %copy-done, ...), custom_call_target="tpu_custom_call" | custom-call | tf_op jit(solution)/shard_map/pallas_call | solution.py:662
  17.2 8.2 %collective-permute-start.2 = (f32[12,8,128]{2,1,0:T(8,128)S(1)}, f32[12,8,128]{2,1,0:T(8,128)S(1)}, u32[]{:S(2)}, u32[]{:S(2)}) collective-permute-start(f32[12,8,128]{2,1,0:T(8,128)S(1)} %get-tuple-element.37.unit_in), channel_id=1, source_target_pairs={{0,32},{32,0},{64,96},{96,64},{128,160},{160,128},{192,224},{224,1... | collective-permute-start | bytes 147464 | tf_op jit(solution)/shard_map/ppermute | solution.py:680
  25.4 2.0 %collective-permute-done.2.left_ref = f32[12,8,128]{2,1,0:T(8,128)S(1)} collective-permute-done((f32[12,8,128]{2,1,0:T(8,128)S(1)}, f32[12,8,128]{2,1,0:T(8,128)S(1)}, u32[]{:S(2)}, u32[]{:S(2)}) %collective-permute-start.2) | collective-permute-done | bytes 49184 | tf_op jit(solution)/shard_map/ppermute | solution.py:680
  27.4 1.0 %shard_map.115 = (f32[38,8,128]{2,1,0:T(8,128)S(1)}, f32[12,8,128]{2,1,0:T(8,128)S(1)}) custom-call(s32[1,4,18]{2,1,0:T(4,128)S(1)} %copy-done.5, f32[54,8,128]{2,1,0:T(8,128)S(1)} %copy-done.1, f32[38,8,128]{2,1,0:T(8,128)S(1)} %get-tuple-element.36.post_in, f32[12,8,128]{2,1,0:T(8,128)S(1)} %get-tuple-element.37.unit_in, ...), custom_call_target="tpu_custom_call" | custom-call | tf_op jit(solution)/shard_map/pallas_call | solution.py:662
  29.1 7.0 %collective-permute-start.4 = (f32[12,8,128]{2,1,0:T(8,128)S(1)}, f32[12,8,128]{2,1,0:T(8,128)S(1)}, u32[]{:S(2)}, u32[]{:S(2)}) collective-permute-start(f32[12,8,128]{2,1,0:T(8,128)S(1)} %get-tuple-element.39.unit_in), channel_id=1, source_target_pairs={{0,32},{32,0},{64,96},{96,64},{128,160},{160,128},{192,224},{224,1... | collective-permute-start | bytes 147464 | tf_op jit(solution)/shard_map/ppermute | solution.py:680
  36.2 2.0 %collective-permute-done.4.left_ref = f32[12,8,128]{2,1,0:T(8,128)S(1)} collective-permute-done((f32[12,8,128]{2,1,0:T(8,128)S(1)}, f32[12,8,128]{2,1,0:T(8,128)S(1)}, u32[]{:S(2)}, u32[]{:S(2)}) %collective-permute-start.4) | collective-permute-done | bytes 49184 | tf_op jit(solution)/shard_map/ppermute | solution.py:680
  38.2 1.0 %shard_map.116 = (f32[38,8,128]{2,1,0:T(8,128)S(1)}, f32[12,8,128]{2,1,0:T(8,128)S(1)}) custom-call(s32[1,4,18]{2,1,0:T(4,128)S(1)} %copy-done.5, f32[54,8,128]{2,1,0:T(8,128)S(1)} %copy-done.1, f32[38,8,128]{2,1,0:T(8,128)S(1)} %get-tuple-element.38.post_in, f32[12,8,128]{2,1,0:T(8,128)S(1)} %get-tuple-element.39.unit_in, ...), custom_call_target="tpu_custom_call" | custom-call | tf_op jit(solution)/shard_map/pallas_call | solution.py:662
  39.9 8.2 %collective-permute-start.6 = (f32[12,8,128]{2,1,0:T(8,128)S(1)}, f32[12,8,128]{2,1,0:T(8,128)S(1)}, u32[]{:S(2)}, u32[]{:S(2)}) collective-permute-start(f32[12,8,128]{2,1,0:T(8,128)S(1)} %get-tuple-element.41.unit_in), channel_id=1, source_target_pairs={{0,32},{32,0},{64,96},{96,64},{128,160},{160,128},{192,224},{224,1... | collective-permute-start | bytes 147464 | tf_op jit(solution)/shard_map/ppermute | solution.py:680
  48.1 2.0 %collective-permute-done.6.left_ref = f32[12,8,128]{2,1,0:T(8,128)S(1)} collective-permute-done((f32[12,8,128]{2,1,0:T(8,128)S(1)}, f32[12,8,128]{2,1,0:T(8,128)S(1)}, u32[]{:S(2)}, u32[]{:S(2)}) %collective-permute-start.6) | collective-permute-done | bytes 49184 | tf_op jit(solution)/shard_map/ppermute | solution.py:680
  50.2 1.9 %shard_map.117 = (f32[19,16,128]{2,1,0:T(8,128)S(1)}, f32[16,9,2,128]{3,2,1,0:T(2,128)}) custom-call(s32[1,4,18]{2,1,0:T(4,128)S(1)} %copy-done.5, s32[1,64]{1,0:T(1,128)S(1)} %copy-done.6, s32[1,64]{1,0:T(1,128)S(1)} %copy-done.7, f32[54,8,128]{2,1,0:T(8,128)S(1)} %copy-done.1, f32[38,8,128]{2,1,0:T(8,128)S(1)} %get-tuple-element.40.post_in, ...), custom_call_target="tpu_custom_call" | custom-call | tf_op jit(solution)/shard_map/pallas_call | solution.py:662
  52.1 13.1 %all-to-all-start = ((f32[16,9,2,128]{3,2,1,0:T(2,128)}), f32[16,9,2,128]{3,2,1,0:T(2,128)S(1)}, u32[]{:S(2)}, u32[]{:S(2)}) async-start(f32[16,9,2,128]{3,2,1,0:T(2,128)} %get-tuple-element.43), calls=%async_computation | async-start | bytes 294912 | tf_op jit(solution)/shard_map/all_to_all | solution.py:719
  65.2 1.9 %collective-permute-start.10 = (f32[5,16,128]{2,1,0:T(8,128)S(1)}, f32[5,16,128]{2,1,0:T(8,128)S(1)}, u32[]{:S(2)}, u32[]{:S(2)}) collective-permute-start(f32[5,16,128]{2,1,0:T(8,128)S(1)} %get-tuple-element.46), channel_id=1, source_target_pairs={{0,4},{4,0},{8,12},{12,8},{16,20},{20,16},{24,28},{28,24},{1,5},{5... | collective-permute-start | bytes 122888 | tf_op jit(solution)/shard_map/ppermute | solution.py:680
  67.1 2.8 %collective-permute-start.11 = (f32[5,16,128]{2,1,0:T(8,128)S(1)}, f32[5,16,128]{2,1,0:T(8,128)S(1)}, u32[]{:S(2)}, u32[]{:S(2)}) collective-permute-start(f32[5,16,128]{2,1,0:T(8,128)S(1)} %get-tuple-element.47), channel_id=1, source_target_pairs={{4,8},{8,4},{12,16},{16,12},{20,24},{24,20},{5,9},{9,5},{13,17},{1... | collective-permute-start | bytes 122888 | tf_op jit(solution)/shard_map/ppermute | solution.py:680
  70.0 3.2 %collective-permute-start.8 = (f32[8,128]{1,0:T(8,128)S(1)}, f32[8,128]{1,0:T(8,128)S(1)}, u32[]{:S(2)}, u32[]{:S(2)}) collective-permute-start(f32[8,128]{1,0:T(8,128)S(1)} %get-tuple-element.44), channel_id=1, source_target_pairs={{0,1},{1,0},{2,3},{3,2},{4,5},{5,4},{6,7},{7,6},{8,9},{9,8},{10,11... | collective-permute-start | bytes 12296 | tf_op jit(solution)/shard_map/ppermute | solution.py:680
  73.2 1.9 %collective-permute-start.9 = (f32[8,128]{1,0:T(8,128)S(1)}, f32[8,128]{1,0:T(8,128)S(1)}, u32[]{:S(2)}, u32[]{:S(2)}) collective-permute-start(f32[8,128]{1,0:T(8,128)S(1)} %get-tuple-element.45), channel_id=1, source_target_pairs={{1,2},{2,1},{5,6},{6,5},{9,10},{10,9},{13,14},{14,13},{17,18},{18,... | collective-permute-start | bytes 12296 | tf_op jit(solution)/shard_map/ppermute | solution.py:680
  75.5 3.2 %collective-permute-done.9.zb = f32[8,128]{1,0:T(8,128)S(1)} collective-permute-done((f32[8,128]{1,0:T(8,128)S(1)}, f32[8,128]{1,0:T(8,128)S(1)}, u32[]{:S(2)}, u32[]{:S(2)}) %collective-permute-start.9) | collective-permute-done | bytes 4128 | tf_op jit(solution)/shard_map/ppermute | solution.py:680
  78.7 0.9 shard_map.119
  79.6 2.8 %shard_map.120 = (f32[6,12,8,128]{3,2,1,0:T(8,128)S(1)}, f32[4,12,8,128]{3,2,1,0:T(8,128)S(1)}, f32[176,128]{1,0:T(8,128)S(1)}, f32[176,128]{1,0:T(8,128)S(1)}, ...) custom-call(s32[1,64]{1,0:T(1,128)S(1)} %copy-done.6, ...), custom_call_target="tpu_custom_call" | custom-call | tf_op jit(solution)/shard_map/pallas_call | solution.py:662
  82.4 1.9 %collective-permute-start.12 = (f32[176,128]{1,0:T(8,128)S(1)}, f32[176,128]{1,0:T(8,128)S(1)}, u32[]{:S(2)}, u32[]{:S(2)}) collective-permute-start(f32[176,128]{1,0:T(8,128)S(1)} %get-tuple-element.56.ma), channel_id=1, source_target_pairs={{0,4},{4,0},{8,12},{12,8},{16,20},{20,16},{24,28},{28,24},{1,5},{5... | collective-permute-start | bytes 270344 | tf_op jit(solution)/shard_map/ppermute | solution.py:680
  84.3 2.5 %collective-permute-start.13 = (f32[176,128]{1,0:T(8,128)S(1)}, f32[176,128]{1,0:T(8,128)S(1)}, u32[]{:S(2)}, u32[]{:S(2)}) collective-permute-start(f32[176,128]{1,0:T(8,128)S(1)} %get-tuple-element.57.mb), channel_id=1, source_target_pairs={{4,8},{8,4},{12,16},{16,12},{20,24},{24,20},{5,9},{9,5},{13,17},{1... | collective-permute-start | bytes 270344 | tf_op jit(solution)/shard_map/ppermute | solution.py:680
  86.9 3.3 %collective-permute-done.13.yb = f32[176,128]{1,0:T(8,128)S(1)} collective-permute-done((f32[176,128]{1,0:T(8,128)S(1)}, f32[176,128]{1,0:T(8,128)S(1)}, u32[]{:S(2)}, u32[]{:S(2)}) %collective-permute-start.13) | collective-permute-done | bytes 90144 | tf_op jit(solution)/shard_map/ppermute | solution.py:680
  90.3 2.1 %collective-permute-start.14 = (f32[3,8,128]{2,1,0:T(8,128)S(1)}, f32[3,8,128]{2,1,0:T(8,128)S(1)}, u32[]{:S(2)}, u32[]{:S(2)}) collective-permute-start(f32[3,8,128]{2,1,0:T(8,128)S(1)} %get-tuple-element.62), channel_id=1, source_target_pairs={{0,1},{1,0},{2,3},{3,2},{4,5},{5,4},{6,7},{7,6},{8,9},{9,8},{10,11... | collective-permute-start | bytes 36872 | tf_op jit(solution)/shard_map/ppermute | solution.py:680
  92.4 1.9 %collective-permute-start.15 = (f32[3,8,128]{2,1,0:T(8,128)S(1)}, f32[3,8,128]{2,1,0:T(8,128)S(1)}, u32[]{:S(2)}, u32[]{:S(2)}) collective-permute-start(f32[3,8,128]{2,1,0:T(8,128)S(1)} %get-tuple-element.63), channel_id=1, source_target_pairs={{1,2},{2,1},{5,6},{6,5},{9,10},{10,9},{13,14},{14,13},{17,18},{18,... | collective-permute-start | bytes 36872 | tf_op jit(solution)/shard_map/ppermute | solution.py:680
  95.0 0.8 collective-permute-done.14.za
  95.8 2.1 %collective-permute-done.15.zb = f32[3,8,128]{2,1,0:T(8,128)S(1)} collective-permute-done((f32[3,8,128]{2,1,0:T(8,128)S(1)}, f32[3,8,128]{2,1,0:T(8,128)S(1)}, u32[]{:S(2)}, u32[]{:S(2)}) %collective-permute-start.15) | collective-permute-done | bytes 12320 | tf_op jit(solution)/shard_map/ppermute | solution.py:680
  98.0 1.3 %shard_map.122 = f32[4,8,8,128]{3,2,1,0:T(8,128)} custom-call(f32[6,12,8,128]{3,2,1,0:T(8,128)S(1)} %get-tuple-element.53.drift, f32[6,12,8,128]{3,2,1,0:T(8,128)S(1)} %get-tuple-element.54.spread, f32[4,12,8,128]{3,2,1,0:T(8,128)S(1)} %get-tuple-element.55.conc, f32[8,8,128]{2,1,0:T(8,128)S(1)} %copy-done.4, ...), custom_call_target="tpu_custom_call" | custom-call | tf_op jit(solution)/shard_map/pallas_call | solution.py:662
  (28 shorter events, 3.2 us)
Async XLA Ops:
  0.6 13.8 %copy-start.2 = (f32[4,8,8,128]{3,2,1,0:T(8,128)S(1)}, f32[4,8,8,128]{3,2,1,0:T(8,128)}, u32[]{:S(2)}) copy-start(f32[4,8,8,128]{3,2,1,0:T(8,128)} %conc.5) | copy-start | bytes 393220
  0.6 13.8 %copy-start.3 = (f32[8,8,128]{2,1,0:T(8,128)S(1)}, f32[8,8,128]{2,1,0:T(8,128)}, u32[]{:S(2)}) copy-start(f32[8,8,128]{2,1,0:T(8,128)} %diff.3) | copy-start | bytes 98308
  3.5 10.9 %copy-start.5 = (s32[1,4,18]{2,1,0:T(4,128)S(1)}, s32[1,4,18]{2,1,0:T(4,128)}, u32[]{:S(2)}) copy-start(s32[1,4,18]{2,1,0:T(4,128)} %nbr_ref.9) | copy-start | bytes 868
  3.5 6.7 %collective-permute-start = (f32[30,8,128]{2,1,0:T(8,128)}, f32[30,8,128]{2,1,0:T(8,128)S(1)}, u32[]{:S(2)}, u32[]{:S(2)}) collective-permute-start(f32[30,8,128]{2,1,0:T(8,128)} %get-tuple-element.34), channel_id=1, source_target_pairs={{0,32},{32,64},{64,96},{96,128},{128,160},{160,192},{192,224},{224... | collective-permute-start | bytes 368648 | tf_op jit(solution)/shard_map/ppermute | solution.py:675
  7.3 7.1 %collective-permute-start.1 = (f32[30,8,128]{2,1,0:T(8,128)}, f32[30,8,128]{2,1,0:T(8,128)S(1)}, u32[]{:S(2)}, u32[]{:S(2)}) collective-permute-start(f32[30,8,128]{2,1,0:T(8,128)} %get-tuple-element.35), channel_id=1, source_target_pairs={{32,0},{64,32},{96,64},{128,96},{160,128},{192,160},{224,192},{256... | collective-permute-start | bytes 368648 | tf_op jit(solution)/shard_map/ppermute | solution.py:675
  14.4 0.9 copy-start
  15.4 12.1 %copy-start.1 = (f32[54,8,128]{2,1,0:T(8,128)S(1)}, f32[54,8,128]{2,1,0:T(8,128)}, u32[]{:S(2)}) copy-start(f32[54,8,128]{2,1,0:T(8,128)} %get-tuple-element.33.state) | copy-start | bytes 663556
  16.5 8.9 %collective-permute-start.3 = (f32[12,8,128]{2,1,0:T(8,128)S(1)}, f32[12,8,128]{2,1,0:T(8,128)S(1)}, u32[]{:S(2)}, u32[]{:S(2)}) collective-permute-start(f32[12,8,128]{2,1,0:T(8,128)S(1)} %get-tuple-element.37.unit_in), channel_id=1, source_target_pairs={{32,64},{64,32},{96,128},{128,96},{160,192},{192,160},{224,256},{2... | collective-permute-start | bytes 147464 | tf_op jit(solution)/shard_map/ppermute | solution.py:680
  17.2 10.3 %collective-permute-start.2 = (f32[12,8,128]{2,1,0:T(8,128)S(1)}, f32[12,8,128]{2,1,0:T(8,128)S(1)}, u32[]{:S(2)}, u32[]{:S(2)}) collective-permute-start(f32[12,8,128]{2,1,0:T(8,128)S(1)} %get-tuple-element.37.unit_in), channel_id=1, source_target_pairs={{0,32},{32,0},{64,96},{96,64},{128,160},{160,128},{192,224},{224,1... | collective-permute-start | bytes 147464 | tf_op jit(solution)/shard_map/ppermute | solution.py:680
  28.5 7.7 %collective-permute-start.5 = (f32[12,8,128]{2,1,0:T(8,128)S(1)}, f32[12,8,128]{2,1,0:T(8,128)S(1)}, u32[]{:S(2)}, u32[]{:S(2)}) collective-permute-start(f32[12,8,128]{2,1,0:T(8,128)S(1)} %get-tuple-element.39.unit_in), channel_id=1, source_target_pairs={{32,64},{64,32},{96,128},{128,96},{160,192},{192,160},{224,256},{2... | collective-permute-start | bytes 147464 | tf_op jit(solution)/shard_map/ppermute | solution.py:680
  29.1 9.0 %collective-permute-start.4 = (f32[12,8,128]{2,1,0:T(8,128)S(1)}, f32[12,8,128]{2,1,0:T(8,128)S(1)}, u32[]{:S(2)}, u32[]{:S(2)}) collective-permute-start(f32[12,8,128]{2,1,0:T(8,128)S(1)} %get-tuple-element.39.unit_in), channel_id=1, source_target_pairs={{0,32},{32,0},{64,96},{96,64},{128,160},{160,128},{192,224},{224,1... | collective-permute-start | bytes 147464 | tf_op jit(solution)/shard_map/ppermute | solution.py:680
  39.2 11.0 %copy-start.6 = (s32[1,64]{1,0:T(1,128)S(1)}, s32[1,64]{1,0:T(1,128)}, u32[]{:S(2)}) copy-start(s32[1,64]{1,0:T(1,128)} %own_ref.3) | copy-start | bytes 772
  39.2 10.9 %copy-start.7 = (s32[1,64]{1,0:T(1,128)S(1)}, s32[1,64]{1,0:T(1,128)}, u32[]{:S(2)}) copy-start(s32[1,64]{1,0:T(1,128)} %slot_ref.3) | copy-start | bytes 772
  39.3 8.9 %collective-permute-start.7 = (f32[12,8,128]{2,1,0:T(8,128)S(1)}, f32[12,8,128]{2,1,0:T(8,128)S(1)}, u32[]{:S(2)}, u32[]{:S(2)}) collective-permute-start(f32[12,8,128]{2,1,0:T(8,128)S(1)} %get-tuple-element.41.unit_in), channel_id=1, source_target_pairs={{32,64},{64,32},{96,128},{128,96},{160,192},{192,160},{224,256},{2... | collective-permute-start | bytes 147464 | tf_op jit(solution)/shard_map/ppermute | solution.py:680
  39.9 10.3 %collective-permute-start.6 = (f32[12,8,128]{2,1,0:T(8,128)S(1)}, f32[12,8,128]{2,1,0:T(8,128)S(1)}, u32[]{:S(2)}, u32[]{:S(2)}) collective-permute-start(f32[12,8,128]{2,1,0:T(8,128)S(1)} %get-tuple-element.41.unit_in), channel_id=1, source_target_pairs={{0,32},{32,0},{64,96},{96,64},{128,160},{160,128},{192,224},{224,1... | collective-permute-start | bytes 147464 | tf_op jit(solution)/shard_map/ppermute | solution.py:680
  52.1 26.6 %copy-start.4 = (f32[8,8,128]{2,1,0:T(8,128)S(1)}, f32[8,8,128]{2,1,0:T(8,128)}, u32[]{:S(2)}) copy-start(f32[8,8,128]{2,1,0:T(8,128)} %upt.3) | copy-start | bytes 98308
  52.1 27.5 %all-to-all-start = ((f32[16,9,2,128]{3,2,1,0:T(2,128)}), f32[16,9,2,128]{3,2,1,0:T(2,128)S(1)}, u32[]{:S(2)}, u32[]{:S(2)}) async-start(f32[16,9,2,128]{3,2,1,0:T(2,128)} %get-tuple-element.43), calls=%async_computation | async-start | bytes 294912 | tf_op jit(solution)/shard_map/all_to_all | solution.py:719
  65.2 13.5 %collective-permute-start.10 = (f32[5,16,128]{2,1,0:T(8,128)S(1)}, f32[5,16,128]{2,1,0:T(8,128)S(1)}, u32[]{:S(2)}, u32[]{:S(2)}) collective-permute-start(f32[5,16,128]{2,1,0:T(8,128)S(1)} %get-tuple-element.46), channel_id=1, source_target_pairs={{0,4},{4,0},{8,12},{12,8},{16,20},{20,16},{24,28},{28,24},{1,5},{5... | collective-permute-start | bytes 122888 | tf_op jit(solution)/shard_map/ppermute | solution.py:680
  67.1 11.6 %collective-permute-start.11 = (f32[5,16,128]{2,1,0:T(8,128)S(1)}, f32[5,16,128]{2,1,0:T(8,128)S(1)}, u32[]{:S(2)}, u32[]{:S(2)}) collective-permute-start(f32[5,16,128]{2,1,0:T(8,128)S(1)} %get-tuple-element.47), channel_id=1, source_target_pairs={{4,8},{8,4},{12,16},{16,12},{20,24},{24,20},{5,9},{9,5},{13,17},{1... | collective-permute-start | bytes 122888 | tf_op jit(solution)/shard_map/ppermute | solution.py:680
  70.0 5.5 %collective-permute-start.8 = (f32[8,128]{1,0:T(8,128)S(1)}, f32[8,128]{1,0:T(8,128)S(1)}, u32[]{:S(2)}, u32[]{:S(2)}) collective-permute-start(f32[8,128]{1,0:T(8,128)S(1)} %get-tuple-element.44), channel_id=1, source_target_pairs={{0,1},{1,0},{2,3},{3,2},{4,5},{5,4},{6,7},{7,6},{8,9},{9,8},{10,11... | collective-permute-start | bytes 12296 | tf_op jit(solution)/shard_map/ppermute | solution.py:680
  73.2 5.5 %collective-permute-start.9 = (f32[8,128]{1,0:T(8,128)S(1)}, f32[8,128]{1,0:T(8,128)S(1)}, u32[]{:S(2)}, u32[]{:S(2)}) collective-permute-start(f32[8,128]{1,0:T(8,128)S(1)} %get-tuple-element.45), channel_id=1, source_target_pairs={{1,2},{2,1},{5,6},{6,5},{9,10},{10,9},{13,14},{14,13},{17,18},{18,... | collective-permute-start | bytes 12296 | tf_op jit(solution)/shard_map/ppermute | solution.py:680
  82.4 4.5 %collective-permute-start.12 = (f32[176,128]{1,0:T(8,128)S(1)}, f32[176,128]{1,0:T(8,128)S(1)}, u32[]{:S(2)}, u32[]{:S(2)}) collective-permute-start(f32[176,128]{1,0:T(8,128)S(1)} %get-tuple-element.56.ma), channel_id=1, source_target_pairs={{0,4},{4,0},{8,12},{12,8},{16,20},{20,16},{24,28},{28,24},{1,5},{5... | collective-permute-start | bytes 270344 | tf_op jit(solution)/shard_map/ppermute | solution.py:680
  84.3 5.8 %collective-permute-start.13 = (f32[176,128]{1,0:T(8,128)S(1)}, f32[176,128]{1,0:T(8,128)S(1)}, u32[]{:S(2)}, u32[]{:S(2)}) collective-permute-start(f32[176,128]{1,0:T(8,128)S(1)} %get-tuple-element.57.mb), channel_id=1, source_target_pairs={{4,8},{8,4},{12,16},{16,12},{20,24},{24,20},{5,9},{9,5},{13,17},{1... | collective-permute-start | bytes 270344 | tf_op jit(solution)/shard_map/ppermute | solution.py:680
  90.3 5.6 %collective-permute-start.14 = (f32[3,8,128]{2,1,0:T(8,128)S(1)}, f32[3,8,128]{2,1,0:T(8,128)S(1)}, u32[]{:S(2)}, u32[]{:S(2)}) collective-permute-start(f32[3,8,128]{2,1,0:T(8,128)S(1)} %get-tuple-element.62), channel_id=1, source_target_pairs={{0,1},{1,0},{2,3},{3,2},{4,5},{5,4},{6,7},{7,6},{8,9},{9,8},{10,11... | collective-permute-start | bytes 36872 | tf_op jit(solution)/shard_map/ppermute | solution.py:680
  92.4 5.6 %collective-permute-start.15 = (f32[3,8,128]{2,1,0:T(8,128)S(1)}, f32[3,8,128]{2,1,0:T(8,128)S(1)}, u32[]{:S(2)}, u32[]{:S(2)}) collective-permute-start(f32[3,8,128]{2,1,0:T(8,128)S(1)} %get-tuple-element.63), channel_id=1, source_target_pairs={{1,2},{2,1},{5,6},{6,5},{9,10},{10,9},{13,14},{14,13},{17,18},{18,... | collective-permute-start | bytes 36872 | tf_op jit(solution)/shard_map/ppermute | solution.py:680
